TPU v7x, 32 devices: a whole 2x2x4 slice. The times are simulated.
32 devices in a mesh: ctx: 2 (over core), exp: 16 (over z, y, x).
Axes of the slice: x: 2, y: 2, z: 4, core: 2. Of those that a mesh axis runs over, the one named last changes fastest.
Arguments:
- queries: bfloat16 [512, 36864], P('ctx', 'exp'), may hold values from -400 to 400
- latent: bfloat16 [512, 576], P('ctx'), may hold values from -6.5 to 6.5
- value_up: bfloat16 [64, 512, 128], P('exp'), may hold values from -1 to 1
- out_proj: bfloat16 [8192, 7168], P('exp'), may hold values from -0.0625 to 0.0625
- residual: bfloat16 [512, 7168], P(('ctx', 'exp')), may hold values from -3 to 3
- norm_gain: bfloat16 [7168], replicated, may hold values from 0.5 to 1.5
- routes: int32 [512, 8], P(('ctx', 'exp')), may hold values from 0 to 15, all different within a row; in each aligned block of 16 rows (0 to 15, 16 to 31, ...) at most 12 rows name the same one
- gates: float32 [512, 8], P(('ctx', 'exp')), may hold values from 0.1 to 1
- w_gate: bfloat16 [16, 7168, 1024], P('exp', None, 'ctx'), may hold values from -0.0625 to 0.0625
- w_up: bfloat16 [16, 7168, 1024], P('exp', None, 'ctx'), may hold values from -0.0625 to 0.0625
- w_down: bfloat16 [16, 1024, 7168], P('exp', 'ctx'), may hold values from -0.1875 to 0.1875
Outputs:
- hidden_state: bfloat16 [512, 7168], P(('ctx', 'exp'))
- expert_out: bfloat16 [2, 16, 16, 12, 7168], P('ctx', 'exp')
Inputs may be any that keep to these rules, and one draw needn't show every extreme that they name: `routes`: each token names 8 different experts. In every aligned block of 16 tokens no expert is named by more than 12 tokens, and in every draw some block names some expert exactly 12 times.
All inputs are finite; a program needn't handle non-finite values.
Results may differ from a plain program's by a relative error of at most 0.03.
Values may be sent and summed in bfloat16 or wider, within the bound.
No kernel may reach another device: no remote copies, remote signals or barrier semaphores. Data moves between devices by JAX's collectives and lax.ppermute only.
A program may use at most 128 MiB of HBM per device.

v0:
```python
import jax
import jax.numpy as jnp
from jax import lax
from jax.sharding import PartitionSpec as P

score_scale = 192.0 ** (-0.5)
norm_epsilon = 1e-06
masked_value = -1e30


def attend_block(running, block_keys, query_rows, positions, window_span, latent_width):
    top_prev, total_prev, accumulated_previous = running
    scores = (
        jnp.einsum("thc,kc->htk", query_rows, block_keys, preferred_element_type=jnp.float32)
        * score_scale
    )
    key_pos = jnp.arange(block_keys.shape[0], dtype=jnp.int32)
    visible = (
        (key_pos[None, :] <= positions[:, None])
        & (key_pos[None, :] > positions[:, None] - window_span)
        & (key_pos[None, :] >= 0)
    )
    masked = jnp.where(visible[None], scores, masked_value)
    top_new = jnp.maximum(top_prev, jnp.max(masked, axis=2))
    weights = jnp.where(visible[None], jnp.exp(masked - top_new[:, :, None]), 0.0)
    total_new = jnp.sum(weights, axis=2)
    values = block_keys[:, :latent_width]
    accum_new = jnp.einsum(
        "htk,kl->htl", weights.astype(jnp.bfloat16), values, preferred_element_type=jnp.float32
    )
    return (top_new, total_new, accum_new)


def body(
    queries, latent, value_up, out_proj, residual, norm_gain, routes, gates, w_gate, w_up, w_down
):
    slab_len, qk_width = latent.shape
    heads_here, latent_width, value_width = value_up.shape
    slab_count = lax.axis_size("ctx")
    window_span = slab_len * slab_count // 2
    query_rows = queries.reshape(slab_len, heads_here, qk_width)
    first_pos = lax.axis_index("ctx") * slab_len
    positions = first_pos + jnp.arange(slab_len, dtype=jnp.int32)
    initial = (
        jnp.full((heads_here, slab_len), masked_value, jnp.float32),
        jnp.zeros((heads_here, slab_len), jnp.float32),
        jnp.zeros((heads_here, slab_len, latent_width), jnp.float32),
    )
    running = attend_block(
        initial,
        lax.all_gather(latent, "ctx", axis=0, tiled=True),
        query_rows,
        positions,
        window_span,
        latent_width,
    )
    total_final = running[1]
    accum_final = running[2]
    attended = (accum_final / total_final[:, :, None]).astype(jnp.bfloat16)
    head_values = (
        jnp.einsum("htl,hlv->thv", attended, value_up, preferred_element_type=jnp.float32)
        .astype(jnp.bfloat16)
        .reshape(slab_len, heads_here * value_width)
    )
    token_rows = residual.shape[0]
    projected = lax.psum_scatter(
        jnp.dot(head_values, out_proj, preferred_element_type=jnp.float32).astype(jnp.bfloat16),
        "exp",
        scatter_dimension=0,
        tiled=True,
    ).astype(jnp.float32)
    hidden_state = (residual.astype(jnp.float32) + projected).astype(jnp.bfloat16)
    widened = hidden_state.astype(jnp.float32)
    normed = (
        widened
        * lax.rsqrt(jnp.mean(widened * widened, axis=1, keepdims=True) + norm_epsilon)
        * norm_gain.astype(jnp.float32)
    ).astype(jnp.bfloat16)
    top_count = routes.shape[1]
    sources = lax.axis_size("exp")
    expert_count = sources * w_gate.shape[0]
    capacity = max(2, 3 * token_rows * top_count // (2 * expert_count))
    expert_ids = jnp.arange(expert_count, dtype=jnp.int32)
    onehot = (
        (routes[:, :, None] == expert_ids[None, None, :])
        .astype(jnp.int32)
        .reshape(token_rows * top_count, expert_count)
    )
    earlier_count = jnp.cumsum(onehot, axis=0) - onehot
    slot_index = jnp.sum(earlier_count * onehot, axis=1).reshape(token_rows, top_count)
    slot_ids = jnp.arange(capacity, dtype=jnp.int32)
    matches = (routes[None, None, :, :] == expert_ids[:, None, None, None]) & (
        slot_index[None, None, :, :] == slot_ids[None, :, None, None]
    )
    selected_experts = jnp.any(matches, axis=3).astype(jnp.bfloat16)
    send_gates = jnp.sum(jnp.where(matches, gates[None, None, :, :], 0.0), axis=(2, 3)).astype(
        jnp.bfloat16
    )
    send_rows = jnp.einsum(
        "ekr,rd->ekd", selected_experts, normed, preferred_element_type=jnp.float32
    ).astype(jnp.bfloat16)
    width = normed.shape[1]
    gate_local = w_gate[0]
    up_local = w_up[0]
    down_local = w_down[0]
    arrived, arrived_gates = (
        lax.all_to_all(send_rows, "exp", split_axis=0, concat_axis=0, tiled=True),
        lax.all_to_all(send_gates, "exp", split_axis=0, concat_axis=0, tiled=True),
    )
    flat_rows = arrived.reshape(sources * capacity, width)
    incoming_rows = lax.all_gather(flat_rows, "ctx", axis=0, tiled=True)
    gate_values = jnp.dot(incoming_rows, gate_local, preferred_element_type=jnp.float32)
    up_values = jnp.dot(incoming_rows, up_local, preferred_element_type=jnp.float32)
    hidden_units = (jax.nn.silu(gate_values) * up_values).astype(jnp.bfloat16)
    row_count = sources * capacity
    down_sums = lax.psum_scatter(
        jnp.dot(hidden_units, down_local, preferred_element_type=jnp.float32).astype(jnp.bfloat16),
        "ctx",
        scatter_dimension=0,
        tiled=True,
    ).astype(jnp.float32)
    weighted = (down_sums * arrived_gates.reshape(row_count, 1).astype(jnp.float32)).astype(
        jnp.bfloat16
    )
    return (hidden_state, weighted.reshape(1, 1, sources, capacity, width))


def solution(mesh):
    placed = (
        P("ctx", "exp"),
        P("ctx", None),
        P("exp", None, None),
        P("exp", None),
        P(("ctx", "exp"), None),
        P(),
        P(("ctx", "exp"), None),
        P(("ctx", "exp"), None),
        P("exp", None, "ctx"),
        P("exp", None, "ctx"),
        P("exp", "ctx", None),
    )
    return jax.shard_map(
        body,
        mesh=mesh,
        in_specs=placed,
        out_specs=(P(("ctx", "exp"), None), P("ctx", "exp", None, None, None)),
        check_vma=False,
    )
```

profile of v0, /device:TPU:0, one launch (start us, length us, event | category | flops | bytes accessed | tf_op | source)
XLA Modules:
  0.0 275.4 jit_solution(13595805854051954528)
XLA Ops:
  7.2 2.7 all_gather.6
  9.9 2.4 copy.45
  12.4 2.3 fusion.5
  14.7 0.5 fusion.6
  15.3 2.0 fusion.15
  17.2 7.1 %convolution_convert_fusion.1 = bf16[256,7168]{1,0:T(8,128)(2,1)} fusion(bf16[256,512]{0,1:T(8,128)(2,1)} %bitcast.53, bf16[512,7168]{1,0:T(8,128)(2,1)} %param.14), kind=kOutput, calls=%fused_computation.1 | convolution fusion | flops 1880883200 | bytes 11272192 | tf_op jit(solution)/shard_map/dot_general | solution.py:67
  24.4 0.6 copy-done.4
  25.8 0.2 and_reduce_fusion
  26.1 86.9 %reduce-scatter.3.cloned.1.call-done = bf16[16,7168]{1,0:T(8,128)(2,1)} async-done(((bf16[256,7168]{1,0:T(8,128)(2,1)}), bf16[16,7168]{1,0:T(8,128)(2,1)}) %reduce-scatter.3.cloned.1.call-update) | async-done | bytes 229392 | tf_op jit(solution)/shard_map/reduce_scatter | solution.py:66
  113.0 1.1 fusion.33
  114.1 0.9 convolution_convert_fusion.2
  115.1 1.6 copy.52
  116.7 86.2 %all_to_all.11 = bf16[16,12,7168]{2,1,0:T(8,128)(2,1)} all-to-all(bf16[16,12,7168]{2,1,0:T(8,128)(2,1)S(1)} %copy.52), channel_id=1, replica_groups=mesh['ctx'=2,'exp'=16] {'exp'}, dimensions={0} | all-to-all | bytes 5505024 | tf_op jit(solution)/shard_map/all_to_all | solution.py:107
  202.8 4.5 %reshape.123 = bf16[192,7168]{1,0:T(8,128)(2,1)} reshape(bf16[16,12,7168]{2,1,0:T(8,128)(2,1)} %all_to_all.11) | data formatting | bytes 5505024 | tf_op jit(solution)/shard_map/reshape | solution.py:110
  207.3 0.2 reduce-scatter.5.cloned.1.call-start
  207.5 14.0 %all-gather.2.cloned.1.call-done = bf16[384,7168]{1,0:T(8,128)(2,1)} async-done(((bf16[192,7168]{1,0:T(8,128)(2,1)}), bf16[384,7168]{1,0:T(8,128)(2,1)}) %all-gather.2.cloned.1.call-update) | async-done | bytes 5505040 | tf_op jit(solution)/shard_map/all_gather | solution.py:111
  221.6 6.9 %fusion.3 = f32[384,512]{1,0:T(8,128)S(1)} fusion(bf16[384,7168]{1,0:T(8,128)(2,1)} %all-gather.2.cloned.1.call-done, bf16[1,7168,512]{2,1,0:T(8,128)(2,1)} %param.19), kind=kOutput, calls=%fused_computation.6 | convolution fusion | flops 2818572288 | bytes 13631488 | tf_op jit(solution)/shard_map/dot_general | solution.py:112
  228.5 15.1 %convolution_convert_fusion = bf16[384,7168]{1,0:T(8,128)(2,1)} fusion(bf16[1,512,7168]{2,1,0:T(8,128)(2,1)} %param.21, bf16[384,7168]{1,0:T(8,128)(2,1)} %all-gather.2.cloned.1.call-done, bf16[1,7168,512]{2,1,0:T(8,128)(2,1)} %param.20, f32[384,512]{1,0:T(8,128)S(1)} %fusion.3), kind=kOutput, calls=%fused_computation | convolution fusion | flops 5641076736 | bytes 26476544 | tf_op jit(solution)/shard_map/dot_general | solution.py:117
  243.6 0.7 copy-done.6
  244.3 0.5 fusion.29
  244.8 13.9 %all_to_all.12 = bf16[16,1,12]{2,1,0:T(2,128)(2,1)S(1)} all-to-all(bf16[16,1,12]{2,1,0:T(2,128)(2,1)S(1)} %copy.53), channel_id=1, replica_groups=mesh['ctx'=2,'exp'=16] {'exp'}, dimensions={0} | all-to-all | bytes 768 | tf_op jit(solution)/shard_map/all_to_all | solution.py:108
  258.8 2.4 multiply_convert_fusion
  261.2 2.6 reshape.124
  263.7 5.1 %copy.54 = bf16[1,1,16,12,7168]{4,2,3,1,0:T(8,128)(2,1)} copy(bf16[1,1,16,12,7168]{4,3,2,1,0:T(8,128)(2,1)} %reshape.124) | data formatting | bytes 5505024
  (35 shorter events, 1.2 us)
Async XLA Ops:
  7.2 8.1 %copy-start = (bf16[4,512,128]{2,1,0:T(8,128)(2,1)S(1)}, bf16[4,512,128]{2,1,0:T(8,128)(2,1)}, u32[]{:S(2)}) copy-start(bf16[4,512,128]{2,1,0:T(8,128)(2,1)} %param.13) | copy-start | bytes 1572868
  7.2 105.8 %reduce-scatter.3.cloned.1.call-start = ((), (), s32[]{:S(2)}) async-start(), calls=%async_computation.4 | async-start | bytes 3899392 | tf_op jit(solution)/shard_map/reduce_scatter | solution.py:66
  24.3 0.7 copy-start.4
  24.3 0.8 copy-start.5
  24.3 88.7 %copy-start.3 = (bf16[16,7168]{1,0:T(8,128)(2,1)S(1)}, bf16[16,7168]{1,0:T(8,128)(2,1)}, u32[]{:S(2)}) copy-start(bf16[16,7168]{1,0:T(8,128)(2,1)} %param.15) | copy-start | bytes 688132
  24.3 197.2 %all-gather.2.cloned.1.call-start = ((), (), s32[]{:S(2)}) async-start(), calls=%async_computation.5 | async-start | bytes 8257536 | tf_op jit(solution)/shard_map/all_gather | solution.py:111
  114.1 2.5 copy-start.2
  207.3 51.5 %reduce-scatter.5.cloned.1.call-start = ((), (), s32[]{:S(2)}) async-start(), calls=%async_computation.6 | async-start | bytes 8257536 | tf_op jit(solution)/shard_map/reduce_scatter | solution.py:116
  243.6 0.7 copy-start.6
  261.2 7.7 %copy-start.1 = (bf16[4,512,128]{2,1,0:T(8,128)(2,1)S(1)}, bf16[4,512,128]{2,1,0:T(8,128)(2,1)}, u32[]{:S(2)}) copy-start(bf16[4,512,128]{2,1,0:T(8,128)(2,1)} %param.13) | copy-start | bytes 1572868
Sparse Core Ops, SparseCore 0:
  24.5 88.4 reduce-scatter.2
  207.4 14.0 all-gather.1
  243.8 14.6 reduce-scatter.4
where the time goes:
time: 276 us; the launch traced here: 275 us
  blocking collectives  103 us (37%)
  waiting for transfers between devices  101 us (37%)
  matrix products  34.3 us (12%)
  local copies, waits for them, and re-layouts  17.7 us (6%)
  between operations  13.9 us (5%)
  other arithmetic  5.4 us (2%)
    reduce_scatter x1, waiting for transfers between devices, body(): lax.psum_scatter(jnp.dot(head_values, out_proj, preferred_element_type=jn...  86.9 us
    all_to_all x1, blocking collectives, body(): lax.all_to_all(send_rows, 'exp', split_axis=0, concat_axis=0, tiled=True)  86.2 us
    dot_general x1, matrix products, body(): jnp.dot(hidden_units, down_local, preferred_element_type=jnp.float32)  15.1 us
    all_gather x1, waiting for transfers between devices, body(): incoming_rows = lax.all_gather(flat_rows, 'ctx', axis=0, tiled=True)  14 us
    all_to_all x1, blocking collectives, body(): lax.all_to_all(send_gates, 'exp', split_axis=0, concat_axis=0, tiled=True)  13.9 us
    unnamed x17, local copies, waits for them, and re-layouts  8.83 us
    dot_general x1, matrix products, body(): jnp.dot(head_values, out_proj, preferred_element_type=jnp.float32)  7.08 us
    dot_general x1, matrix products, body(): jnp.dot(incoming_rows, gate_local, preferred_element_type=jnp.float32)  6.94 us
  transfers between devices with their start and end apart: 3, of which 2 were waited for; matrix products, arithmetic and copies ran while one was open for 1% of the time, Pallas kernels for 0%

commit v1 on v0

v1 whole, which is shorter than its diff:
```python
import functools

import jax
import jax.numpy as jnp
from jax import lax
from jax.experimental import pallas as pl
from jax.experimental.pallas import tpu as pltpu
from jax.sharding import PartitionSpec as P

score_scale = 192.0 ** (-0.5)
norm_epsilon = 1e-06
masked_value = -1e30
LANES = 128
f32 = jnp.float32
bf16 = jnp.bfloat16


def bits_of(count):
    return count.bit_length() - 1


def relative_of(pos, order):
    rel = jnp.zeros_like(pos)
    for i, bit in enumerate(order):
        rel = rel | (((pos >> (len(order) - 1 - i)) & 1) << bit)
    return rel


def order_matrix(rows, block, order, me):
    shift = bits_of(block)
    row = lax.broadcasted_iota(jnp.int32, (rows, rows), 0)
    col = lax.broadcasted_iota(jnp.int32, (rows, rows), 1)
    source = ((relative_of(row >> shift, order) ^ me) << shift) | (row & (block - 1))
    return jnp.where(col == source, 1.0, 0.0).astype(bf16)


def attend_kernel(
    slabs, block, orders, place_ref, q_ref, *refs
):
    keys = refs[:slabs]
    up_ref, wa_ref, wb_ref = refs[slabs : slabs + 3]
    hva_ref, hvb_ref, ka_ref, sa_ref, kb_ref, sb_ref = refs[slabs + 3 : slabs + 9]
    padded_ref, hv_ref = refs[slabs + 9 :]
    heads, latent_width, value_width = up_ref.shape
    qk, slab = keys[0].shape
    rows = q_ref.shape[0]
    span = slab * slabs

    @pl.when(pl.program_id(0) == 0)
    def _():
        here = place_ref[0]
        me = place_ref[1]
        offsets = sorted({(h * qk) % LANES for h in range(heads)})
        padded_ref[...] = jnp.zeros_like(padded_ref)
        for n, offset in enumerate(offsets):
            for k in range(slabs):
                padded_ref[n, offset : offset + qk, k * slab : (k + 1) * slab] = keys[k][...]
        col = lax.broadcasted_iota(jnp.int32, (rows, span), 1)
        key_pos = col
        for k in range(slabs):
            base = lax.rem(here - k + slabs, slabs) * slab
            key_pos = jnp.where(col >= k * slab, col - k * slab + base, key_pos)
        query_pos = lax.broadcasted_iota(jnp.int32, (rows, span), 0) + here * slab
        visible = (key_pos <= query_pos) & (key_pos > query_pos - span // 2)
        for h in range(heads):
            offset = (h * qk) % LANES
            start = h * qk - offset
            width = -(-(offset + qk) // LANES) * LANES
            n = offsets.index(offset)
            scores = (
                jnp.dot(
                    q_ref[:, start : start + width],
                    padded_ref[n, :width, :],
                    preferred_element_type=f32,
                )
                * score_scale
            )
            masked = jnp.where(visible, scores, masked_value)
            top = jnp.max(masked, axis=1, keepdims=True)
            weights = jnp.where(visible, jnp.exp(masked - top), 0.0)
            total = jnp.sum(weights, axis=1, keepdims=True)
            mixed = lax.dot_general(
                weights.astype(bf16),
                padded_ref[0, :latent_width, :],
                (((1,), (1,)), ((), ())),
                preferred_element_type=f32,
            )
            attended = (mixed / total).astype(bf16)
            hv_ref[:, h * value_width : (h + 1) * value_width] = jnp.dot(
                attended, up_ref[h], preferred_element_type=f32
            ).astype(bf16)
        hv = hv_ref[...]
        for out_ref, order in zip((hva_ref, hvb_ref), orders):
            out_ref[...] = jnp.dot(
                order_matrix(rows, block, order, me), hv, preferred_element_type=f32
            ).astype(bf16)

    project(hva_ref, wa_ref, ka_ref, sa_ref)
    project(hvb_ref, wb_ref, kb_ref, sb_ref)


def project(hv_ref, w_ref, keep_ref, send_ref):
    half = keep_ref.shape[0]
    out = jnp.dot(hv_ref[...], w_ref[...], preferred_element_type=f32).astype(bf16)
    keep_ref[...] = out[:half]
    send_ref[...] = out[half:]


def project_kernel(hva_ref, hvb_ref, wa_ref, wb_ref, ka_ref, sa_ref, kb_ref, sb_ref):
    project(hva_ref, wa_ref, ka_ref, sa_ref)
    project(hvb_ref, wb_ref, kb_ref, sb_ref)


def column_tile(columns, most):
    tiles = columns // LANES
    return LANES * max(t for t in range(1, tiles + 1) if tiles % t == 0 and t * LANES <= most)


def project_specs(rows, inner, quarter, tile, chunk):
    steps = quarter // tile
    first = 2 * chunk * steps
    weights = [
        pl.BlockSpec((inner, tile), lambda i, first=first: (0, first + i)),
        pl.BlockSpec((inner, tile), lambda i, first=first + steps: (0, first + i)),
    ]
    outs = [pl.BlockSpec((rows // 2, tile), lambda i: (0, i))] * 4
    shapes = [jax.ShapeDtypeStruct((rows // 2, quarter), bf16)] * 4
    return steps, weights, outs, shapes


def whole(shape):
    return pl.BlockSpec(shape, lambda i: (0,) * len(shape))


def attend_project(place, queries, keys, value_up, out_proj, block, orders):
    rows, _ = queries.shape
    heads, _, value_width = value_up.shape
    qk, slab = keys[0].shape
    slabs = len(keys)
    span = slab * slabs
    inner, width = out_proj.shape
    quarter = width // 4
    steps, weights, outs, shapes = project_specs(
        rows, inner, quarter, column_tile(quarter, 896), 0
    )
    offsets = {(h * qk) % LANES for h in range(heads)}
    deep = max(-(-(o + qk) // LANES) * LANES for o in offsets)
    flops = 2 * rows * (heads * span * 2 * qk + inner * (width // 2))
    return pl.pallas_call(
        functools.partial(attend_kernel, slabs, block, orders),
        grid=(steps,),
        in_specs=[
            pl.BlockSpec(memory_space=pltpu.SMEM),
            whole(queries.shape),
            *[whole(k.shape) for k in keys],
            whole(value_up.shape),
            *weights,
        ],
        out_specs=[whole((rows, inner))] * 2 + outs,
        out_shape=[jax.ShapeDtypeStruct((rows, inner), bf16)] * 2 + shapes,
        scratch_shapes=[
            pltpu.VMEM((len(offsets), deep, span), bf16),
            pltpu.VMEM((rows, inner), bf16),
        ],
        compiler_params=pltpu.CompilerParams(vmem_limit_bytes=40 << 20),
        cost_estimate=pl.CostEstimate(
            flops=flops,
            bytes_accessed=inner * width + rows * width + queries.size * 2,
            transcendentals=rows * span * heads,
        ),
        name="attend_project",
    )(place, queries, *keys, value_up, out_proj, out_proj)


def project_more(hva, hvb, out_proj, chunk):
    rows, inner = hva.shape
    width = out_proj.shape[1]
    quarter = width // 4
    steps, weights, outs, shapes = project_specs(
        rows, inner, quarter, column_tile(quarter, 896), chunk
    )
    return pl.pallas_call(
        project_kernel,
        grid=(steps,),
        in_specs=[whole(hva.shape), whole(hvb.shape), *weights],
        out_specs=outs,
        out_shape=shapes,
        compiler_params=pltpu.CompilerParams(vmem_limit_bytes=32 << 20),
        cost_estimate=pl.CostEstimate(
            flops=rows * inner * width,
            bytes_accessed=inner * width + rows * width,
            transcendentals=0,
        ),
        name="project_more",
    )(hva, hvb, out_proj, out_proj)


def place_rows(quarter_rows, columns, deep, a_refs, b_refs, x_ref):
    a_low, a_high = a_refs
    b_low, b_high = b_refs
    q = quarter_rows
    pieces = [
        (a_low, 0, 2 * q, 0, 0),
        (a_high, 0, 2 * q, 2 * q, 0),
        (b_low, 0, q, 0, columns),
        (b_low, q, q, 2 * q, columns),
        (b_high, 0, q, q, columns),
        (b_high, q, q, 3 * q, columns),
    ]
    for ref, source, count, target, first in pieces:
        done = 0
        while done < columns:
            tile, inside = divmod(first + done, deep)
            size = min(deep - inside, columns - done)
            x_ref[tile, target : target + count, inside : inside + size] = ref[
                source : source + count, done : done + size
            ]
            done += size


def gate_up_step(x, gates, ups, acc_ref, base_ref):
    for n, group in enumerate((gates, ups)):
        for p, w_ref in enumerate(group):
            wide = w_ref.shape[2]
            cols = slice(p * wide, (p + 1) * wide)
            acc_ref[n, :, cols] = base_ref[n, :, cols] + jnp.dot(
                x, w_ref[0], preferred_element_type=f32
            )


def gate_up_kernel(slabs, quarter_rows, columns, deep, *refs):
    a_refs, b_refs = refs[:2], refs[2:4]
    gates, ups = refs[4 : 4 + slabs], refs[4 + slabs : 4 + 2 * slabs]
    acc_ref, x_ref = refs[4 + 2 * slabs :]

    @pl.when(pl.program_id(0) == 0)
    def _():
        place_rows(quarter_rows, columns, deep, a_refs, b_refs, x_ref)
        acc_ref[...] = jnp.zeros_like(acc_ref)

    gate_up_step(x_ref[pl.program_id(0)], gates, ups, acc_ref, acc_ref)


def finish_kernel(
    slabs, quarter_rows, columns, deep, steps, block, order, top, senders, slots, place_ref, *refs
):
    a_refs, b_refs = refs[:2], refs[2:4]
    base_ref = refs[4]
    gates, ups = refs[5 : 5 + slabs], refs[5 + slabs : 5 + 2 * slabs]
    downs = refs[5 + 2 * slabs : 5 + 3 * slabs]
    out_ref, x_ref, acc_ref, act_ref, gate_ref = refs[5 + 3 * slabs :]
    step = pl.program_id(0)
    rows = 4 * quarter_rows
    q = quarter_rows

    @pl.when(step == 0)
    def _():
        place_rows(quarter_rows, columns, deep, a_refs, b_refs, x_ref)
        gate_up_step(x_ref[0], gates, ups, acc_ref, base_ref)

    @pl.when((step > 0) & (step < steps))
    def _():
        gate_up_step(x_ref[step], gates, ups, acc_ref, acc_ref)

    @pl.when(step == steps - 1)
    def _():
        me = place_ref[1]
        b_low, b_high = b_refs
        meta = jnp.concatenate(
            [b_low[:q, columns:], b_high[:q, columns:], b_low[q:, columns:], b_high[q:, columns:]],
            axis=0,
        ).astype(f32)
        lane = lax.broadcasted_iota(jnp.int32, (rows, LANES), 1)
        named = (lane < top) & (meta == me.astype(f32))
        hit = jnp.max(jnp.where(named, 1.0, 0.0), axis=1, keepdims=True)
        aligned = pltpu.roll(meta, LANES - top, 1)
        gate = jnp.sum(jnp.where(named, aligned, 0.0), axis=1, keepdims=True)
        inverse = jnp.sum(
            jnp.where((lane == 2 * top) | (lane == 2 * top + 1), meta, 0.0), axis=1, keepdims=True
        )
        r = lax.broadcasted_iota(jnp.int32, (rows, rows), 0)
        c = lax.broadcasted_iota(jnp.int32, (rows, rows), 1)
        shift = bits_of(block)
        before = jnp.where(((r >> shift) == (c >> shift)) & (c < r), 1.0, 0.0).astype(bf16)
        hits = jnp.broadcast_to(hit, (rows, LANES))
        slot = jnp.dot(before, hits.astype(bf16), preferred_element_type=f32)
        pos = lax.broadcasted_iota(jnp.int32, (rows, LANES), 0) >> shift
        sender = (relative_of(pos, order) ^ me).astype(f32)
        target = jnp.where(hits > 0.5, slot * senders + sender, -1.0)
        target_row = jnp.transpose(target)[:1, :]
        wanted = lax.broadcasted_iota(jnp.int32, (slots, rows), 0).astype(f32)
        select = jnp.where(wanted == target_row, 1.0, 0.0).astype(bf16)
        gate_ref[...] = jnp.dot(
            select,
            jnp.broadcast_to(gate, (rows, LANES)).astype(bf16),
            preferred_element_type=f32,
        )
        gated = acc_ref[0] * inverse
        upped = acc_ref[1] * inverse
        act = (gated / (1.0 + jnp.exp(-gated)) * upped).astype(bf16)
        act_ref[...] = jnp.dot(select, act, preferred_element_type=f32).astype(bf16)

    @pl.when(step >= steps)
    def _():
        total = None
        for p, w_ref in enumerate(downs):
            part = w_ref.shape[1]
            term = jnp.dot(
                act_ref[:, p * part : (p + 1) * part], w_ref[0], preferred_element_type=f32
            )
            total = term if total is None else total + term
        out_ref[...] = (total * gate_ref[:, :1]).astype(bf16)


def gate_up(a, b, gates, ups, deep):
    half, columns = a[0].shape
    rows = 2 * half
    hidden = sum(w.shape[2] for w in gates)
    steps = 2 * columns // deep
    spec = [pl.BlockSpec((1, deep, w.shape[2]), lambda i: (0, i, 0)) for w in gates + ups]
    return pl.pallas_call(
        functools.partial(gate_up_kernel, len(gates), rows // 4, columns, deep),
        grid=(steps,),
        in_specs=[whole(v.shape) for v in a + b] + spec,
        out_specs=whole((2, rows, hidden)),
        out_shape=jax.ShapeDtypeStruct((2, rows, hidden), f32),
        scratch_shapes=[pltpu.VMEM((steps, rows, deep), bf16)],
        compiler_params=pltpu.CompilerParams(vmem_limit_bytes=40 << 20),
        cost_estimate=pl.CostEstimate(
            flops=8 * rows * columns * hidden,
            bytes_accessed=8 * columns * hidden + 8 * rows * hidden,
            transcendentals=0,
        ),
        name="gate_up",
    )(*a, *b, *gates, *ups)


def finish(place, a, b, base, gates, ups, downs, deep, block, order, top, senders, capacity):
    half, columns = a[0].shape
    rows = 2 * half
    hidden = sum(w.shape[2] for w in gates)
    width = downs[0].shape[2]
    steps = 2 * columns // deep
    tile = column_tile(width, 1024)
    more = width // tile
    slots = senders * capacity
    last = steps - 1
    spec = [
        pl.BlockSpec((1, deep, w.shape[2]), lambda i: (0, steps + jnp.minimum(i, last), 0))
        for w in gates + ups
    ]
    spec += [
        pl.BlockSpec((1, w.shape[1], tile), lambda i: (0, 0, jnp.maximum(i - steps, 0)))
        for w in downs
    ]
    return pl.pallas_call(
        functools.partial(
            finish_kernel, len(gates), rows // 4, columns, deep, steps, block, order, top, senders, slots
        ),
        grid=(steps + more,),
        in_specs=[pl.BlockSpec(memory_space=pltpu.SMEM)]
        + [whole(v.shape) for v in a + b]
        + [whole(base.shape)]
        + spec,
        out_specs=pl.BlockSpec((slots, tile), lambda i: (0, jnp.maximum(i - steps, 0))),
        out_shape=jax.ShapeDtypeStruct((slots, width), bf16),
        scratch_shapes=[
            pltpu.VMEM((steps, rows, deep), bf16),
            pltpu.VMEM((2, rows, hidden), f32),
            pltpu.VMEM((slots, hidden), bf16),
            pltpu.VMEM((slots, LANES), f32),
        ],
        compiler_params=pltpu.CompilerParams(vmem_limit_bytes=48 << 20),
        cost_estimate=pl.CostEstimate(
            flops=8 * rows * columns * hidden + 2 * slots * hidden * width,
            bytes_accessed=8 * columns * hidden + 2 * hidden * width + 2 * slots * width,
            transcendentals=rows * hidden,
        ),
        name="finish",
    )(place, *a, *b, base, *gates, *ups, *downs)


def add(a, b):
    return (a.astype(f32) + b.astype(f32)).astype(bf16)


def swap(value, bit, count):
    return lax.ppermute(value, "exp", [(i, i ^ (1 << bit)) for i in range(count)])


def shifted(value, count):
    return [value] + [
        lax.ppermute(value, "ctx", [(i, (i + k) % count) for i in range(count)])
        for k in range(1, count)
    ]


def scatter_sum(parts, count, bits):
    keep_a, send_a, keep_b, send_b = parts
    got_a, got_b = swap(send_a, 0, count), swap(send_b, 1, count)
    half = keep_a.shape[0] // 2
    next_a = add(keep_a[half:], got_a[half:])
    next_b = add(keep_b[half:], got_b[half:])
    got_a2, got_b2 = swap(next_a, 1, count), swap(next_b, 0, count)
    keep_a = add(keep_a[:half], got_a[:half])
    keep_b = add(keep_b[:half], got_b[:half])
    keep, got = (
        jnp.concatenate([keep_a, keep_b], axis=1),
        jnp.concatenate([got_a2, got_b2], axis=1),
    )
    for bit in range(2, bits):
        half = keep.shape[0] // 2
        arrived = swap(add(keep[half:], got[half:]), bit, count)
        keep, got = add(keep[:half], got[:half]), arrived
    return keep, got


def gather_rows(rows, split, count, bits):
    for bit in range(bits - 1, 1, -1):
        rows = jnp.concatenate([rows, swap(rows, bit, count)], axis=0)
    out = []
    for part, (first, second) in ((rows[:, :split], (1, 0)), (rows[:, split:], (0, 1))):
        low = jnp.concatenate([part, swap(part, first, count)], axis=0)
        out.append([low, swap(low, second, count)])
    return out


def body(
    queries, latent, value_up, out_proj, residual, norm_gain, routes, gates, w_gate, w_up, w_down
):
    slabs = lax.axis_size("ctx")
    senders = lax.axis_size("exp")
    bits = bits_of(senders)
    block, width = residual.shape
    top = routes.shape[1]
    expert_count = senders * w_gate.shape[0]
    capacity = max(2, 3 * block * top // (2 * expert_count))
    orders = (list(range(bits)), [1, 0, *range(2, bits)])
    place = jnp.stack([lax.axis_index("ctx"), lax.axis_index("exp")]).astype(jnp.int32)

    keys = shifted(latent.T, slabs)
    gate_parts = shifted(w_gate, slabs)
    up_parts = shifted(w_up, slabs)
    down_parts = shifted(w_down, slabs)

    hva, hvb, *parts = attend_project(
        place, queries, keys, value_up, out_proj, block, orders
    )
    chunks = [parts, project_more(hva, hvb, out_proj, 1)]
    half_width = width // 2
    gain = norm_gain.astype(f32)
    hidden, payload, squares = [], [], 0.0
    for c, terms in enumerate(chunks):
        keep, got = scatter_sum(terms, senders, bits)
        cols = slice(c * half_width, (c + 1) * half_width)
        rows = (residual[:, cols].astype(f32) + (keep.astype(f32) + got.astype(f32))).astype(bf16)
        wide = rows.astype(f32)
        squares = squares + jnp.sum(wide * wide, axis=1, keepdims=True)
        hidden.append(rows)
        payload.append((wide * gain[None, cols]).astype(bf16))
    inverse = lax.rsqrt(squares / width + norm_epsilon)
    coarse = lax.reduce_precision(inverse, 8, 7)
    meta = jnp.concatenate(
        [
            routes.astype(bf16),
            gates.astype(bf16),
            coarse.astype(bf16),
            (inverse - coarse).astype(bf16),
            jnp.zeros((block, LANES - 2 * top - 2), bf16),
        ],
        axis=1,
    )
    payload[1] = jnp.concatenate([payload[1], meta], axis=1)

    deep = column_tile(half_width, 512)
    a, b = gather_rows(payload[0], half_width // 2, senders, bits)
    base = gate_up(a, b, gate_parts, up_parts, deep)
    a, b = gather_rows(payload[1], half_width // 2, senders, bits)
    slots = finish(
        place, a, b, base, gate_parts, up_parts, down_parts, deep, block, orders[0], top, senders, capacity
    )
    expert_out = slots.reshape(capacity, senders, width).transpose(1, 0, 2)[None, None]
    return jnp.concatenate(hidden, axis=1), expert_out


def solution(mesh):
    placed = (
        P("ctx", "exp"),
        P("ctx", None),
        P("exp", None, None),
        P("exp", None),
        P(("ctx", "exp"), None),
        P(),
        P(("ctx", "exp"), None),
        P(("ctx", "exp"), None),
        P("exp", None, "ctx"),
        P("exp", None, "ctx"),
        P("exp", "ctx", None),
    )
    return jax.shard_map(
        body,
        mesh=mesh,
        in_specs=placed,
        out_specs=(P(("ctx", "exp"), None), P("ctx", "exp", None, None, None)),
        check_vma=False,
    )
```

time: 276 us -> 152 us (0.55)
  blocking collectives: 103 us -> 0 us
  waiting for transfers between devices: 101 us -> 61 us
  starting transfers between devices: 0.3 us -> 40.2 us
  Pallas kernels: 0 us -> 36.7 us
  matrix products: 34.3 us -> 0 us
  between operations: 13.9 us -> 0.82 us
  local copies, waits for them, and re-layouts: 17.7 us -> 10 us
  other arithmetic: 5.4 us -> 2.19 us
    all_to_all x2 -> x0, blocking collectives: 100 us -> none  [the longest x1 86.2 us: body(): lax.all_to_all(send_rows, 'exp', split_axis=0, concat_axis=0, tiled=True)]
    reduce_scatter x2 -> x0, waiting for transfers between devices: 86.9 us -> none  [the longest x1 86.9 us: body(): lax.psum_scatter(jnp.dot(head_values, out_proj, preferred_element_type=jn...]
    ppermute x0 -> x28, waiting for transfers between devices: none -> 61 us  [the longest x24 59.7 us: swap(): return lax.ppermute(value, 'exp', [(i, i ^ 1 << bit) for i in range(count)])]
    ppermute x0 -> x28, starting transfers between devices: none -> 40.2 us  [the longest x24 39.1 us: swap(): return lax.ppermute(value, 'exp', [(i, i ^ 1 << bit) for i in range(count)])]
    pallas_call x0 -> x4, Pallas kernels: none -> 36.7 us  [the longest x1 19.7 us: finish(): pl.pallas_call(functools.partial(finish_kernel, len(gates), rows // 4, co...]
    dot_general x6 -> x0, matrix products: 34.3 us -> none  [the longest x1 15.1 us: body(): jnp.dot(hidden_units, down_local, preferred_element_type=jnp.float32)]
    all_gather x1 -> x0, waiting for transfers between devices: 14 us -> none  [body(): incoming_rows = lax.all_gather(flat_rows, 'ctx', axis=0, tiled=True)]
    reshape x2 -> x0, local copies, waits for them, and re-layouts: 7 us -> none  [the longest x1 4.45 us: body(): flat_rows = arrived.reshape(sources * capacity, width)]
  transfers between devices with their start and end apart: 3 -> 28, of which waited for: 2 -> 21; matrix products, arithmetic and copies ran while one was open for 1% -> 2% of each run, Pallas kernels for 0% -> 8%
where the time goes in v1:
time: 152 us; the launch traced here: 151 us
  waiting for transfers between devices  61 us (40%)
  starting transfers between devices  40.2 us (26%)
  Pallas kernels  36.7 us (24%)
  local copies, waits for them, and re-layouts  10 us (7%)
  other arithmetic  2.19 us (1%)
    ppermute x24, waiting for transfers between devices, swap(): return lax.ppermute(value, 'exp', [(i, i ^ 1 << bit) for i in range(count)])  59.7 us
    ppermute x24, starting transfers between devices, swap(): return lax.ppermute(value, 'exp', [(i, i ^ 1 << bit) for i in range(count)])  39.1 us
    pallas_call x1, Pallas kernels, finish(): pl.pallas_call(functools.partial(finish_kernel, len(gates), rows // 4, co...  19.7 us
    unnamed x20, local copies, waits for them, and re-layouts  9.49 us
    pallas_call x1, Pallas kernels, gate_up(): pl.pallas_call(functools.partial(gate_up_kernel, len(gates), rows // 4, c...  9.48 us
    pallas_call x1, Pallas kernels, attend_project(): pl.pallas_call(functools.partial(attend_kernel, slabs, block, orders), gr...  5.58 us
  transfers between devices with their start and end apart: 28, of which 21 were waited for; matrix products, arithmetic and copies ran while one was open for 2% of the time, Pallas kernels for 8%

profile of v1, /device:TPU:0, one launch (start us, length us, event | category | flops | bytes accessed | tf_op | source)
XLA Modules:
  0.0 150.9 jit_solution(8227498339313717761)
XLA Ops:
  2.6 3.1 %copy-done = bf16[512,7168]{1,0:T(8,128)(2,1)S(1)} copy-done((bf16[512,7168]{1,0:T(8,128)(2,1)S(1)}, bf16[512,7168]{1,0:T(8,128)(2,1)}, u32[]{:S(2)}) %copy-start) | copy-done | bytes 7340056
  8.9 5.6 %attend_project.1 = (bf16[256,512]{1,0:T(8,128)(2,1)S(1)}, bf16[256,512]{1,0:T(8,128)(2,1)S(1)}, bf16[128,1792]{1,0:T(8,128)(2,1)S(1)}, bf16[128,1792]{1,0:T(8,1...) custom-call(s32[2]{0:T(128)S(1)} %pad_add_fusion.place_ref, bf16[256,2304]{1,0:T(8,128)(2,1)S(1)} %copy-done.2, ...), custom_call_target="tpu_custom_call" | custom-call | flops 2147483648 | bytes 6684672 | tf_op jit(solution)/shard_map/attend_project/pallas_call | solution.py:149
  14.5 2.9 %collective-permute-start.1 = (bf16[128,1792]{1,0:T(8,128)(2,1)S(1)}, bf16[128,1792]{1,0:T(8,128)(2,1)S(1)}, u32[]{:S(2)}, u32[]{:S(2)}) collective-permute-start(bf16[128,1792]{1,0:T(8,128)(2,1)S(1)} %get-tuple-element.13), channel_id=1, source_target_pairs={{0,1},{1,0},{2,3},{3,2},{4,5},{5,4},{6,7},{7,6},{8,9},{9,8},{10,11... | collective-permute-start | bytes 1376264 | tf_op jit(solution)/shard_map/ppermute | solution.py:388
  19.7 3.1 %copy-done.1 = bf16[512,7168]{1,0:T(8,128)(2,1)S(1)} copy-done((bf16[512,7168]{1,0:T(8,128)(2,1)S(1)}, bf16[512,7168]{1,0:T(8,128)(2,1)}, u32[]{:S(2)}) %copy-start.1) | copy-done | bytes 7340056
  22.8 2.0 %project_more.1 = (bf16[128,1792]{1,0:T(8,128)(2,1)S(1)}, bf16[128,1792]{1,0:T(8,128)(2,1)S(1)}, bf16[128,1792]{1,0:T(8,128)(2,1)S(1)}, bf16[128,1792]{1,0:T(8,128)(2,1)S(1)}) custom-call(bf16[256,512]{1,0:T(8,128)(2,1)S(1)} %get-tuple-element.16.hva_ref, bf16[256,512]{1,0:T(8,128)(2,1)S(1)} %get-tuple-element.17.hvb_ref, bf16[512,7168]{1,0:T(8,128)(2,1)S(1)} %copy-done.1, ...), custom_call_target="tpu_custom_call" | custom-call | flops 939524096 | bytes 5505024 | tf_op jit(solution)/shard_map/project_more/pallas_call | solution.py:182
  24.7 3.5 %collective-permute-done.1 = bf16[128,1792]{1,0:T(8,128)(2,1)S(1)} collective-permute-done((bf16[128,1792]{1,0:T(8,128)(2,1)S(1)}, bf16[128,1792]{1,0:T(8,128)(2,1)S(1)}, u32[]{:S(2)}, u32[]{:S(2)}) %collective-permute-start.1) | collective-permute-done | bytes 458784 | tf_op jit(solution)/shard_map/ppermute | solution.py:388
  32.7 7.6 %collective-permute-done.7 = bf16[128,1792]{1,0:T(8,128)(2,1)S(1)} collective-permute-done((bf16[128,1792]{1,0:T(8,128)(2,1)S(1)}, bf16[128,1792]{1,0:T(8,128)(2,1)S(1)}, u32[]{:S(2)}, u32[]{:S(2)}) %collective-permute-start.7) | collective-permute-done | bytes 458784 | tf_op jit(solution)/shard_map/ppermute | solution.py:388
  41.9 2.6 %collective-permute-done.8 = bf16[128,1792]{1,0:T(8,128)(2,1)S(1)} collective-permute-done((bf16[128,1792]{1,0:T(8,128)(2,1)S(1)}, bf16[128,1792]{1,0:T(8,128)(2,1)S(1)}, u32[]{:S(2)}, u32[]{:S(2)}) %collective-permute-start.8) | collective-permute-done | bytes 458784 | tf_op jit(solution)/shard_map/ppermute | solution.py:388
  44.6 3.5 %collective-permute-done.3 = bf16[64,1792]{1,0:T(8,128)(2,1)S(1)} collective-permute-done((bf16[64,1792]{1,0:T(8,128)(2,1)S(1)}, bf16[64,1792]{1,0:T(8,128)(2,1)S(1)}, u32[]{:S(2)}, u32[]{:S(2)}) %collective-permute-start.3) | collective-permute-done | bytes 229408 | tf_op jit(solution)/shard_map/ppermute | solution.py:388
  50.7 3.8 %collective-permute-done.9 = bf16[64,1792]{1,0:T(8,128)(2,1)S(1)} collective-permute-done((bf16[64,1792]{1,0:T(8,128)(2,1)S(1)}, bf16[64,1792]{1,0:T(8,128)(2,1)S(1)}, u32[]{:S(2)}, u32[]{:S(2)}) %collective-permute-start.9) | collective-permute-done | bytes 229408 | tf_op jit(solution)/shard_map/ppermute | solution.py:388
  58.3 5.3 %collective-permute-done.5 = bf16[32,3584]{1,0:T(8,128)(2,1)S(1)} collective-permute-done((bf16[32,3584]{1,0:T(8,128)(2,1)S(1)}, bf16[32,3584]{1,0:T(8,128)(2,1)S(1)}, u32[]{:S(2)}, u32[]{:S(2)}) %collective-permute-start.5) | collective-permute-done | bytes 229408 | tf_op jit(solution)/shard_map/ppermute | solution.py:388
  63.6 2.1 %collective-permute-start.6 = (bf16[16,3584]{1,0:T(8,128)(2,1)S(1)}, bf16[16,3584]{1,0:T(8,128)(2,1)S(1)}, u32[]{:S(2)}, u32[]{:S(2)}) collective-permute-start(bf16[16,3584]{1,0:T(8,128)(2,1)S(1)} %add_convert_fusion.16), channel_id=1, source_target_pairs={{0,8},{1,9},{2,10},{3,11},{4,12},{5,13},{6,14},{7,15},{8,0},{9,1},... | collective-permute-start | bytes 344072 | tf_op jit(solution)/shard_map/ppermute | solution.py:388
  66.1 3.0 %collective-permute-start.12 = (bf16[16,3584]{1,0:T(8,128)(2,1)S(1)}, bf16[16,3584]{1,0:T(8,128)(2,1)S(1)}, u32[]{:S(2)}, u32[]{:S(2)}) collective-permute-start(bf16[16,3584]{1,0:T(8,128)(2,1)S(1)} %add_convert_fusion.13), channel_id=1, source_target_pairs={{0,8},{1,9},{2,10},{3,11},{4,12},{5,13},{6,14},{7,15},{8,0},{9,1},... | collective-permute-start | bytes 344072 | tf_op jit(solution)/shard_map/ppermute | solution.py:388
  69.2 2.5 %collective-permute-done.6 = bf16[16,3584]{1,0:T(8,128)(2,1)S(1)} collective-permute-done((bf16[16,3584]{1,0:T(8,128)(2,1)S(1)}, bf16[16,3584]{1,0:T(8,128)(2,1)S(1)}, u32[]{:S(2)}, u32[]{:S(2)}) %collective-permute-start.6) | collective-permute-done | bytes 114720 | tf_op jit(solution)/shard_map/ppermute | solution.py:388
  71.6 3.2 %collective-permute-done.12 = bf16[16,3584]{1,0:T(8,128)(2,1)S(1)} collective-permute-done((bf16[16,3584]{1,0:T(8,128)(2,1)S(1)}, bf16[16,3584]{1,0:T(8,128)(2,1)S(1)}, u32[]{:S(2)}, u32[]{:S(2)}) %collective-permute-start.12) | collective-permute-done | bytes 114720 | tf_op jit(solution)/shard_map/ppermute | solution.py:388
  76.8 1.7 %collective-permute-start.13 = (bf16[16,3712]{1,0:T(8,128)(2,1)S(1)}, bf16[16,3712]{1,0:T(8,128)(2,1)S(1)}, u32[]{:S(2)}, u32[]{:S(2)}) collective-permute-start(bf16[16,3712]{1,0:T(8,128)(2,1)S(1)} %concatenate.49), channel_id=1, source_target_pairs={{0,8},{1,9},{2,10},{3,11},{4,12},{5,13},{6,14},{7,15},{8,0},{9,1},... | collective-permute-start | bytes 356360 | tf_op jit(solution)/shard_map/ppermute | solution.py:388
  78.5 2.7 %collective-permute-done.19 = bf16[16,3584]{1,0:T(8,128)(2,1)S(1)} collective-permute-done((bf16[16,3584]{1,0:T(8,128)(2,1)S(1)}, bf16[16,3584]{1,0:T(8,128)(2,1)S(1)}, u32[]{:S(2)}, u32[]{:S(2)}) %collective-permute-start.19) | collective-permute-done | bytes 114720 | tf_op jit(solution)/shard_map/ppermute | solution.py:388
  81.3 4.2 %collective-permute-start.20 = (bf16[32,3584]{1,0:T(8,128)(2,1)S(1)}, bf16[32,3584]{1,0:T(8,128)(2,1)S(1)}, u32[]{:S(2)}, u32[]{:S(2)}) collective-permute-start(bf16[32,3584]{1,0:T(8,128)(2,1)S(1)} %pad_maximum_fusion.12), channel_id=1, source_target_pairs={{0,4},{1,5},{2,6},{3,7},{4,0},{5,1},{6,2},{7,3},{8,12},{9,13},{10,... | collective-permute-start | bytes 688136 | tf_op jit(solution)/shard_map/ppermute | solution.py:388
  85.5 3.2 %collective-permute-start.14 = (bf16[32,3712]{1,0:T(8,128)(2,1)S(1)}, bf16[32,3712]{1,0:T(8,128)(2,1)S(1)}, u32[]{:S(2)}, u32[]{:S(2)}) collective-permute-start(bf16[32,3712]{1,0:T(8,128)(2,1)S(1)} %pad_maximum_fusion.7), channel_id=1, source_target_pairs={{0,4},{1,5},{2,6},{3,7},{4,0},{5,1},{6,2},{7,3},{8,12},{9,13},{10,... | collective-permute-start | bytes 712712 | tf_op jit(solution)/shard_map/ppermute | solution.py:388
  94.3 2.2 %collective-permute-done.23 = bf16[64,1792]{1,0:T(8,128)(2,1)S(1)} collective-permute-done((bf16[64,1792]{1,0:T(8,128)(2,1)S(1)}, bf16[64,1792]{1,0:T(8,128)(2,1)S(1)}, u32[]{:S(2)}, u32[]{:S(2)}) %collective-permute-start.23) | collective-permute-done | bytes 229408 | tf_op jit(solution)/shard_map/ppermute | solution.py:388
  100.4 6.5 %collective-permute-done.15 = bf16[64,1792]{1,0:T(8,128)(2,1)S(1)} collective-permute-done((bf16[64,1792]{1,0:T(8,128)(2,1)S(1)}, bf16[64,1792]{1,0:T(8,128)(2,1)S(1)}, u32[]{:S(2)}, u32[]{:S(2)}) %collective-permute-start.15) | collective-permute-done | bytes 229408 | tf_op jit(solution)/shard_map/ppermute | solution.py:388
  109.8 9.4 %collective-permute-done.22.refs_1_ = bf16[128,1792]{1,0:T(8,128)(2,1)S(1)} collective-permute-done((bf16[128,1792]{1,0:T(8,128)(2,1)S(1)}, bf16[128,1792]{1,0:T(8,128)(2,1)S(1)}, u32[]{:S(2)}, u32[]{:S(2)}) %collective-permute-start.22) | collective-permute-done | bytes 458784 | tf_op jit(solution)/shard_map/ppermute | solution.py:388
  121.7 9.5 %gate_up.1.refs_4_ = f32[2,256,1024]{2,1,0:T(8,128)S(1)} custom-call(bf16[128,1792]{1,0:T(8,128)(2,1)S(1)} %pad_maximum_fusion.3.refs_0_, bf16[128,1792]{1,0:T(8,128)(2,1)S(1)} %collective-permute-done.22.refs_1_, bf16[128,1792]{1,0:T(8,128)(2,1)S(1)} %pad_maximum_fusion.4.refs_2_, bf16[128,1792]{1,0:T(8,128)(2,1)S(1)} %collective-permute-done.24.refs_3_, ...), custom_call_target="tpu_custom_call" | custom-call | flops 3758096384 | bytes 16777216 | tf_op jit(solution)/shard_map/gate_up/pallas_call | solution.py:321
  131.2 19.7 %finish.1 = bf16[192,7168]{1,0:T(8,128)(2,1)} custom-call(s32[2]{0:T(128)S(1)} %pad_add_fusion.place_ref, bf16[128,1792]{1,0:T(8,128)(2,1)S(1)} %pad_maximum_fusion.1.refs_0_, bf16[128,1792]{1,0:T(8,128)(2,1)S(1)} %collective-permute-done.16.refs_1_, bf16[128,1920]{1,0:T(8,128)(2,1)S(1)} %pad_maximum_fusion.refs_2_, ...), custom_call_target="tpu_custom_call" | custom-call | flops 6576668672 | bytes 32112640 | tf_op jit(solution)/shard_map/finish/pallas_call | solution.py:356
  (91 shorter events, 37.2 us)
Async XLA Ops:
  14.5 13.7 %collective-permute-start.1 = (bf16[128,1792]{1,0:T(8,128)(2,1)S(1)}, bf16[128,1792]{1,0:T(8,128)(2,1)S(1)}, u32[]{:S(2)}, u32[]{:S(2)}) collective-permute-start(bf16[128,1792]{1,0:T(8,128)(2,1)S(1)} %get-tuple-element.13), channel_id=1, source_target_pairs={{0,1},{1,0},{2,3},{3,2},{4,5},{5,4},{6,7},{7,6},{8,9},{9,8},{10,11... | collective-permute-start | bytes 1376264 | tf_op jit(solution)/shard_map/ppermute | solution.py:388
  17.4 113.8 %collective-permute-start.27 = (bf16[1,512,7168]{2,1,0:T(8,128)(2,1)}, bf16[1,512,7168]{2,1,0:T(8,128)(2,1)}, u32[]{:S(2)}, u32[]{:S(2)}) collective-permute-start(bf16[1,512,7168]{2,1,0:T(8,128)(2,1)} %refs_9_.1), channel_id=1, source_target_pairs={{0,16},{16,0},{1,17},{17,1},{2,18},{18,2},{3,19},{19,3},{4,20},{20... | collective-permute-start | bytes 22020104 | tf_op jit(solution)/shard_map/ppermute | solution.py:393
  17.4 104.3 %collective-permute-start.25 = (bf16[1,7168,512]{2,1,0:T(8,128)(2,1)}, bf16[1,7168,512]{2,1,0:T(8,128)(2,1)}, u32[]{:S(2)}, u32[]{:S(2)}) collective-permute-start(bf16[1,7168,512]{2,1,0:T(8,128)(2,1)} %refs_5_.1), channel_id=1, source_target_pairs={{0,16},{16,0},{1,17},{17,1},{2,18},{18,2},{3,19},{19,3},{4,20},{20... | collective-permute-start | bytes 22020104 | tf_op jit(solution)/shard_map/ppermute | solution.py:393
  18.0 103.8 %collective-permute-start.26 = (bf16[1,7168,512]{2,1,0:T(8,128)(2,1)}, bf16[1,7168,512]{2,1,0:T(8,128)(2,1)}, u32[]{:S(2)}, u32[]{:S(2)}) collective-permute-start(bf16[1,7168,512]{2,1,0:T(8,128)(2,1)} %refs_7_.1), channel_id=1, source_target_pairs={{0,16},{16,0},{1,17},{17,1},{2,18},{18,2},{3,19},{19,3},{4,20},{20... | collective-permute-start | bytes 22020104 | tf_op jit(solution)/shard_map/ppermute | solution.py:393
  18.1 12.9 %collective-permute-start.2 = (bf16[128,1792]{1,0:T(8,128)(2,1)S(1)}, bf16[128,1792]{1,0:T(8,128)(2,1)S(1)}, u32[]{:S(2)}, u32[]{:S(2)}) collective-permute-start(bf16[128,1792]{1,0:T(8,128)(2,1)S(1)} %get-tuple-element.15), channel_id=1, source_target_pairs={{0,2},{1,3},{2,0},{3,1},{4,6},{5,7},{6,4},{7,5},{8,10},{9,11},{10,... | collective-permute-start | bytes 1376264 | tf_op jit(solution)/shard_map/ppermute | solution.py:388
  28.3 12.1 %collective-permute-start.7 = (bf16[128,1792]{1,0:T(8,128)(2,1)S(1)}, bf16[128,1792]{1,0:T(8,128)(2,1)S(1)}, u32[]{:S(2)}, u32[]{:S(2)}) collective-permute-start(bf16[128,1792]{1,0:T(8,128)(2,1)S(1)} %get-tuple-element.19), channel_id=1, source_target_pairs={{0,1},{1,0},{2,3},{3,2},{4,5},{5,4},{6,7},{7,6},{8,9},{9,8},{10,11... | collective-permute-start | bytes 1376264 | tf_op jit(solution)/shard_map/ppermute | solution.py:388
  31.1 13.4 %collective-permute-start.8 = (bf16[128,1792]{1,0:T(8,128)(2,1)S(1)}, bf16[128,1792]{1,0:T(8,128)(2,1)S(1)}, u32[]{:S(2)}, u32[]{:S(2)}) collective-permute-start(bf16[128,1792]{1,0:T(8,128)(2,1)S(1)} %get-tuple-element.21), channel_id=1, source_target_pairs={{0,2},{1,3},{2,0},{3,1},{4,6},{5,7},{6,4},{7,5},{8,10},{9,11},{10,... | collective-permute-start | bytes 1376264 | tf_op jit(solution)/shard_map/ppermute | solution.py:388
  40.3 7.8 %collective-permute-start.3 = (bf16[64,1792]{1,0:T(8,128)(2,1)S(1)}, bf16[64,1792]{1,0:T(8,128)(2,1)S(1)}, u32[]{:S(2)}, u32[]{:S(2)}) collective-permute-start(bf16[64,1792]{1,0:T(8,128)(2,1)S(1)} %get-tuple-element.31), channel_id=1, source_target_pairs={{0,2},{1,3},{2,0},{3,1},{4,6},{5,7},{6,4},{7,5},{8,10},{9,11},{10,... | collective-permute-start | bytes 688136 | tf_op jit(solution)/shard_map/ppermute | solution.py:388
  48.1 6.3 %collective-permute-start.9 = (bf16[64,1792]{1,0:T(8,128)(2,1)S(1)}, bf16[64,1792]{1,0:T(8,128)(2,1)S(1)}, u32[]{:S(2)}, u32[]{:S(2)}) collective-permute-start(bf16[64,1792]{1,0:T(8,128)(2,1)S(1)} %get-tuple-element.37), channel_id=1, source_target_pairs={{0,2},{1,3},{2,0},{3,1},{4,6},{5,7},{6,4},{7,5},{8,10},{9,11},{10,... | collective-permute-start | bytes 688136 | tf_op jit(solution)/shard_map/ppermute | solution.py:388
  54.5 9.1 %collective-permute-start.5 = (bf16[32,3584]{1,0:T(8,128)(2,1)S(1)}, bf16[32,3584]{1,0:T(8,128)(2,1)S(1)}, u32[]{:S(2)}, u32[]{:S(2)}) collective-permute-start(bf16[32,3584]{1,0:T(8,128)(2,1)S(1)} %get-tuple-element.29), channel_id=1, source_target_pairs={{0,4},{1,5},{2,6},{3,7},{4,0},{5,1},{6,2},{7,3},{8,12},{9,13},{10,... | collective-permute-start | bytes 688136 | tf_op jit(solution)/shard_map/ppermute | solution.py:388
  56.7 9.4 %collective-permute-start.11 = (bf16[32,3584]{1,0:T(8,128)(2,1)S(1)}, bf16[32,3584]{1,0:T(8,128)(2,1)S(1)}, u32[]{:S(2)}, u32[]{:S(2)}) collective-permute-start(bf16[32,3584]{1,0:T(8,128)(2,1)S(1)} %get-tuple-element.35), channel_id=1, source_target_pairs={{0,4},{1,5},{2,6},{3,7},{4,0},{5,1},{6,2},{7,3},{8,12},{9,13},{10,... | collective-permute-start | bytes 688136 | tf_op jit(solution)/shard_map/ppermute | solution.py:388
  63.6 8.0 %collective-permute-start.6 = (bf16[16,3584]{1,0:T(8,128)(2,1)S(1)}, bf16[16,3584]{1,0:T(8,128)(2,1)S(1)}, u32[]{:S(2)}, u32[]{:S(2)}) collective-permute-start(bf16[16,3584]{1,0:T(8,128)(2,1)S(1)} %add_convert_fusion.16), channel_id=1, source_target_pairs={{0,8},{1,9},{2,10},{3,11},{4,12},{5,13},{6,14},{7,15},{8,0},{9,1},... | collective-permute-start | bytes 344072 | tf_op jit(solution)/shard_map/ppermute | solution.py:388
  66.1 8.7 %collective-permute-start.12 = (bf16[16,3584]{1,0:T(8,128)(2,1)S(1)}, bf16[16,3584]{1,0:T(8,128)(2,1)S(1)}, u32[]{:S(2)}, u32[]{:S(2)}) collective-permute-start(bf16[16,3584]{1,0:T(8,128)(2,1)S(1)} %add_convert_fusion.13), channel_id=1, source_target_pairs={{0,8},{1,9},{2,10},{3,11},{4,12},{5,13},{6,14},{7,15},{8,0},{9,1},... | collective-permute-start | bytes 344072 | tf_op jit(solution)/shard_map/ppermute | solution.py:388
  76.8 8.7 %collective-permute-start.13 = (bf16[16,3712]{1,0:T(8,128)(2,1)S(1)}, bf16[16,3712]{1,0:T(8,128)(2,1)S(1)}, u32[]{:S(2)}, u32[]{:S(2)}) collective-permute-start(bf16[16,3712]{1,0:T(8,128)(2,1)S(1)} %concatenate.49), channel_id=1, source_target_pairs={{0,8},{1,9},{2,10},{3,11},{4,12},{5,13},{6,14},{7,15},{8,0},{9,1},... | collective-permute-start | bytes 356360 | tf_op jit(solution)/shard_map/ppermute | solution.py:388
  81.3 8.2 %collective-permute-start.20 = (bf16[32,3584]{1,0:T(8,128)(2,1)S(1)}, bf16[32,3584]{1,0:T(8,128)(2,1)S(1)}, u32[]{:S(2)}, u32[]{:S(2)}) collective-permute-start(bf16[32,3584]{1,0:T(8,128)(2,1)S(1)} %pad_maximum_fusion.12), channel_id=1, source_target_pairs={{0,4},{1,5},{2,6},{3,7},{4,0},{5,1},{6,2},{7,3},{8,12},{9,13},{10,... | collective-permute-start | bytes 688136 | tf_op jit(solution)/shard_map/ppermute | solution.py:388
  85.5 7.3 %collective-permute-start.14 = (bf16[32,3712]{1,0:T(8,128)(2,1)S(1)}, bf16[32,3712]{1,0:T(8,128)(2,1)S(1)}, u32[]{:S(2)}, u32[]{:S(2)}) collective-permute-start(bf16[32,3712]{1,0:T(8,128)(2,1)S(1)} %pad_maximum_fusion.7), channel_id=1, source_target_pairs={{0,4},{1,5},{2,6},{3,7},{4,0},{5,1},{6,2},{7,3},{8,12},{9,13},{10,... | collective-permute-start | bytes 712712 | tf_op jit(solution)/shard_map/ppermute | solution.py:388
  89.6 7.0 %collective-permute-start.23 = (bf16[64,1792]{1,0:T(8,128)(2,1)S(1)}, bf16[64,1792]{1,0:T(8,128)(2,1)S(1)}, u32[]{:S(2)}, u32[]{:S(2)}) collective-permute-start(bf16[64,1792]{1,0:T(8,128)(2,1)S(1)} %get-tuple-element.40), channel_id=1, source_target_pairs={{0,1},{1,0},{2,3},{3,2},{4,5},{5,4},{6,7},{7,6},{8,9},{9,8},{10,11... | collective-permute-start | bytes 688136 | tf_op jit(solution)/shard_map/ppermute | solution.py:388
  92.8 6.0 %collective-permute-start.21 = (bf16[64,1792]{1,0:T(8,128)(2,1)S(1)}, bf16[64,1792]{1,0:T(8,128)(2,1)S(1)}, u32[]{:S(2)}, u32[]{:S(2)}) collective-permute-start(bf16[64,1792]{1,0:T(8,128)(2,1)S(1)} %get-tuple-element.41), channel_id=1, source_target_pairs={{0,2},{1,3},{2,0},{3,1},{4,6},{5,7},{6,4},{7,5},{8,10},{9,11},{10,... | collective-permute-start | bytes 688136 | tf_op jit(solution)/shard_map/ppermute | solution.py:388
  96.5 11.5 %collective-permute-start.17 = (bf16[64,1920]{1,0:T(8,128)(2,1)S(1)}, bf16[64,1920]{1,0:T(8,128)(2,1)S(1)}, u32[]{:S(2)}, u32[]{:S(2)}) collective-permute-start(bf16[64,1920]{1,0:T(8,128)(2,1)S(1)} %pad_maximum_fusion.5), channel_id=1, source_target_pairs={{0,1},{1,0},{2,3},{3,2},{4,5},{5,4},{6,7},{7,6},{8,9},{9,8},{10,11... | collective-permute-start | bytes 737288 | tf_op jit(solution)/shard_map/ppermute | solution.py:388
  98.8 8.1 %collective-permute-start.15 = (bf16[64,1792]{1,0:T(8,128)(2,1)S(1)}, bf16[64,1792]{1,0:T(8,128)(2,1)S(1)}, u32[]{:S(2)}, u32[]{:S(2)}) collective-permute-start(bf16[64,1792]{1,0:T(8,128)(2,1)S(1)} %pad_maximum_fusion.8), channel_id=1, source_target_pairs={{0,2},{1,3},{2,0},{3,1},{4,6},{5,7},{6,4},{7,5},{8,10},{9,11},{10,... | collective-permute-start | bytes 688136 | tf_op jit(solution)/shard_map/ppermute | solution.py:388
  106.8 12.3 %collective-permute-start.22 = (bf16[128,1792]{1,0:T(8,128)(2,1)S(1)}, bf16[128,1792]{1,0:T(8,128)(2,1)S(1)}, u32[]{:S(2)}, u32[]{:S(2)}) collective-permute-start(bf16[128,1792]{1,0:T(8,128)(2,1)S(1)} %pad_maximum_fusion.3.refs_0_), channel_id=1, source_target_pairs={{0,1},{1,0},{2,3},{3,2},{4,5},{5,4},{6,7},{7,6},{8,9},{9,8},{10,11... | collective-permute-start | bytes 1376264 | tf_op jit(solution)/shard_map/ppermute | solution.py:388
  108.0 11.9 %collective-permute-start.24 = (bf16[128,1792]{1,0:T(8,128)(2,1)S(1)}, bf16[128,1792]{1,0:T(8,128)(2,1)S(1)}, u32[]{:S(2)}, u32[]{:S(2)}) collective-permute-start(bf16[128,1792]{1,0:T(8,128)(2,1)S(1)} %pad_maximum_fusion.4.refs_2_), channel_id=1, source_target_pairs={{0,2},{1,3},{2,0},{3,1},{4,6},{5,7},{6,4},{7,5},{8,10},{9,11},{10,... | collective-permute-start | bytes 1376264 | tf_op jit(solution)/shard_map/ppermute | solution.py:388
  119.1 12.1 %collective-permute-start.16 = (bf16[128,1792]{1,0:T(8,128)(2,1)S(1)}, bf16[128,1792]{1,0:T(8,128)(2,1)S(1)}, u32[]{:S(2)}, u32[]{:S(2)}) collective-permute-start(bf16[128,1792]{1,0:T(8,128)(2,1)S(1)} %pad_maximum_fusion.1.refs_0_), channel_id=1, source_target_pairs={{0,1},{1,0},{2,3},{3,2},{4,5},{5,4},{6,7},{7,6},{8,9},{9,8},{10,11... | collective-permute-start | bytes 1376264 | tf_op jit(solution)/shard_map/ppermute | solution.py:388
  119.9 11.3 %collective-permute-start.18 = (bf16[128,1920]{1,0:T(8,128)(2,1)S(1)}, bf16[128,1920]{1,0:T(8,128)(2,1)S(1)}, u32[]{:S(2)}, u32[]{:S(2)}) collective-permute-start(bf16[128,1920]{1,0:T(8,128)(2,1)S(1)} %pad_maximum_fusion.refs_2_), channel_id=1, source_target_pairs={{0,2},{1,3},{2,0},{3,1},{4,6},{5,7},{6,4},{7,5},{8,10},{9,11},{10,... | collective-permute-start | bytes 1474568 | tf_op jit(solution)/shard_map/ppermute | solution.py:388
  (13 other events, 141.9 us)

commit v2 on v1

--- a/solution.py
+++ b/solution.py
@@ -111,6 +111,10 @@
     project(hvb_ref, wb_ref, kb_ref, sb_ref)
 
 
+def in_hbm(value):
+    return pltpu.with_memory_space_constraint(value, pltpu.HBM)
+
+
 def column_tile(columns, most):
     tiles = columns // LANES
     return LANES * max(t for t in range(1, tiles + 1) if tiles % t == 0 and t * LANES <= most)
@@ -162,14 +166,14 @@
             pltpu.VMEM((len(offsets), deep, span), bf16),
             pltpu.VMEM((rows, inner), bf16),
         ],
-        compiler_params=pltpu.CompilerParams(vmem_limit_bytes=40 << 20),
+        compiler_params=pltpu.CompilerParams(vmem_limit_bytes=24 << 20),
         cost_estimate=pl.CostEstimate(
             flops=flops,
             bytes_accessed=inner * width + rows * width + queries.size * 2,
             transcendentals=rows * span * heads,
         ),
         name="attend_project",
-    )(place, queries, *keys, value_up, out_proj, out_proj)
+    )(place, in_hbm(queries), *keys, in_hbm(value_up), in_hbm(out_proj), in_hbm(out_proj))
 
 
 def project_more(hva, hvb, out_proj, chunk):
@@ -185,14 +189,14 @@
         in_specs=[whole(hva.shape), whole(hvb.shape), *weights],
         out_specs=outs,
         out_shape=shapes,
-        compiler_params=pltpu.CompilerParams(vmem_limit_bytes=32 << 20),
+        compiler_params=pltpu.CompilerParams(vmem_limit_bytes=16 << 20),
         cost_estimate=pl.CostEstimate(
             flops=rows * inner * width,
             bytes_accessed=inner * width + rows * width,
             transcendentals=0,
         ),
         name="project_more",
-    )(hva, hvb, out_proj, out_proj)
+    )(hva, hvb, in_hbm(out_proj), in_hbm(out_proj))
 
 
 def place_rows(quarter_rows, columns, deep, a_refs, b_refs, x_ref):
@@ -332,7 +336,7 @@
             transcendentals=0,
         ),
         name="gate_up",
-    )(*a, *b, *gates, *ups)
+    )(*a, *b, *map(in_hbm, gates + ups))
 
 
 def finish(place, a, b, base, gates, ups, downs, deep, block, order, top, senders, capacity):
@@ -341,7 +345,7 @@
     hidden = sum(w.shape[2] for w in gates)
     width = downs[0].shape[2]
     steps = 2 * columns // deep
-    tile = column_tile(width, 1024)
+    tile = column_tile(width, 1792)
     more = width // tile
     slots = senders * capacity
     last = steps - 1
@@ -370,14 +374,14 @@
             pltpu.VMEM((slots, hidden), bf16),
             pltpu.VMEM((slots, LANES), f32),
         ],
-        compiler_params=pltpu.CompilerParams(vmem_limit_bytes=48 << 20),
+        compiler_params=pltpu.CompilerParams(vmem_limit_bytes=44 << 20),
         cost_estimate=pl.CostEstimate(
             flops=8 * rows * columns * hidden + 2 * slots * hidden * width,
             bytes_accessed=8 * columns * hidden + 2 * hidden * width + 2 * slots * width,
             transcendentals=rows * hidden,
         ),
         name="finish",
-    )(place, *a, *b, base, *gates, *ups, *downs)
+    )(place, *a, *b, base, *map(in_hbm, gates + ups + downs))
 
 
 def add(a, b):
@@ -395,19 +399,31 @@
     ]
 
 
-def scatter_sum(parts, count, bits):
-    keep_a, send_a, keep_b, send_b = parts
-    got_a, got_b = swap(send_a, 0, count), swap(send_b, 1, count)
+def tie(*values):
+    return lax.optimization_barrier(values)
+
+
+def first_swap(parts, count):
+    _, send_a, _, send_b = parts
+    return swap(send_a, 0, count), swap(send_b, 1, count)
+
+
+def second_swap(parts, got, count):
+    keep_a, _, keep_b, _ = parts
+    got_a, got_b = got
     half = keep_a.shape[0] // 2
     next_a = add(keep_a[half:], got_a[half:])
     next_b = add(keep_b[half:], got_b[half:])
     got_a2, got_b2 = swap(next_a, 1, count), swap(next_b, 0, count)
     keep_a = add(keep_a[:half], got_a[:half])
     keep_b = add(keep_b[:half], got_b[:half])
-    keep, got = (
-        jnp.concatenate([keep_a, keep_b], axis=1),
-        jnp.concatenate([got_a2, got_b2], axis=1),
-    )
+    return keep_a, keep_b, got_a2, got_b2
+
+
+def last_swaps(terms, count, bits):
+    keep_a, keep_b, got_a, got_b = terms
+    keep = jnp.concatenate([keep_a, keep_b], axis=1)
+    got = jnp.concatenate([got_a, got_b], axis=1)
     for bit in range(2, bits):
         half = keep.shape[0] // 2
         arrived = swap(add(keep[half:], got[half:]), bit, count)
@@ -440,18 +456,25 @@
 
     keys = shifted(latent.T, slabs)
     gate_parts = shifted(w_gate, slabs)
-    up_parts = shifted(w_up, slabs)
-    down_parts = shifted(w_down, slabs)
 
     hva, hvb, *parts = attend_project(
         place, queries, keys, value_up, out_proj, block, orders
     )
-    chunks = [parts, project_more(hva, hvb, out_proj, 1)]
+    more = project_more(hva, hvb, out_proj, 1)
+    got = first_swap(parts, senders)
+    got, more, gate_parts, w_up = tie(got, more, gate_parts, w_up)
+    up_parts = shifted(w_up, slabs)
+    terms = [second_swap(parts, got, senders)]
+    got = first_swap(more, senders)
+    got, terms[0], up_parts, w_down = tie(got, terms[0], up_parts, w_down)
+    down_parts = shifted(w_down, slabs)
+    terms.append(second_swap(more, got, senders))
+    sums = [last_swaps(t, senders, bits) for t in terms]
+    sums[1], down_parts = tie(sums[1], down_parts)
     half_width = width // 2
     gain = norm_gain.astype(f32)
     hidden, payload, squares = [], [], 0.0
-    for c, terms in enumerate(chunks):
-        keep, got = scatter_sum(terms, senders, bits)
+    for c, (keep, got) in enumerate(sums):
         cols = slice(c * half_width, (c + 1) * half_width)
         rows = (residual[:, cols].astype(f32) + (keep.astype(f32) + got.astype(f32))).astype(bf16)
         wide = rows.astype(f32)
@@ -472,7 +495,7 @@
     )
     payload[1] = jnp.concatenate([payload[1], meta], axis=1)
 
-    deep = column_tile(half_width, 512)
+    deep = column_tile(half_width, 1792)
     a, b = gather_rows(payload[0], half_width // 2, senders, bits)
     base = gate_up(a, b, gate_parts, up_parts, deep)
     a, b = gather_rows(payload[1], half_width // 2, senders, bits)

time: 152 us -> 145 us (0.954)
  waiting for transfers between devices: 61 us -> 72.6 us
  starting transfers between devices: 40.2 us -> 29.9 us
  local copies, waits for them, and re-layouts: 10 us -> 4.56 us
  Pallas kernels: 36.7 us -> 35 us
    ppermute x24, starting transfers between devices: 39.1 us -> 29.3 us  [swap(): return lax.ppermute(value, 'exp', [(i, i ^ 1 << bit) for i in range(count)])]
    ppermute x24, waiting for transfers between devices: 59.7 us -> 66.4 us  [swap(): return lax.ppermute(value, 'exp', [(i, i ^ 1 << bit) for i in range(count)])]
    unnamed x20 -> x17, local copies, waits for them, and re-layouts: 9.49 us -> 4.03 us
    ppermute x4, waiting for transfers between devices: 1.35 us -> 6.14 us  [shifted(): lax.ppermute(value, 'ctx', [(i, (i + k) % count) for i in range(count)])]
    pallas_call x1, Pallas kernels: 19.7 us -> 17.1 us  [finish(): pl.pallas_call(functools.partial(finish_kernel, len(gates), rows // 4, co...]
    pallas_call x1, Pallas kernels: 9.48 us -> 7.65 us  [gate_up(): pl.pallas_call(functools.partial(gate_up_kernel, len(gates), rows // 4, c...]
  transfers between devices with their start and end apart: 28 -> 28, of which waited for: 21 -> 15; matrix products, arithmetic and copies ran while one was open for 2% -> 2% of each run, Pallas kernels for 8% -> 12%
where the time goes in v2:
time: 145 us
  waiting for transfers between devices  72.6 us (50%)
  Pallas kernels  35 us (24%)
  starting transfers between devices  29.9 us (21%)
  local copies, waits for them, and re-layouts  4.56 us (3%)
  other arithmetic  2.19 us (2%)
    ppermute x24, waiting for transfers between devices, swap(): return lax.ppermute(value, 'exp', [(i, i ^ 1 << bit) for i in range(count)])  66.4 us
    ppermute x24, starting transfers between devices, swap(): return lax.ppermute(value, 'exp', [(i, i ^ 1 << bit) for i in range(count)])  29.3 us
    pallas_call x1, Pallas kernels, finish(): pl.pallas_call(functools.partial(finish_kernel, len(gates), rows // 4, co...  17.1 us
    pallas_call x1, Pallas kernels, gate_up(): pl.pallas_call(functools.partial(gate_up_kernel, len(gates), rows // 4, c...  7.65 us
    pallas_call x1, Pallas kernels, attend_project(): pl.pallas_call(functools.partial(attend_kernel, slabs, block, orders), gr...  6.88 us
    ppermute x4, waiting for transfers between devices, shifted(): lax.ppermute(value, 'ctx', [(i, (i + k) % count) for i in range(count)])  6.14 us
    unnamed x17, local copies, waits for them, and re-layouts  4.03 us
    pallas_call x1, Pallas kernels, project_more(): pl.pallas_call(project_kernel, grid=(steps,), in_specs=[whole(hva.shape),...  3.29 us
  transfers between devices with their start and end apart: 28, of which 15 were waited for; matrix products, arithmetic and copies ran while one was open for 2% of the time, Pallas kernels for 12%

profile of v2, /device:TPU:0, one launch (start us, length us, event | category | flops | bytes accessed | tf_op | source)
XLA Modules:
  0.0 145.1 jit_solution(15024026254632697097)
XLA Ops:
  1.3 6.1 %collective-permute-done.refs_1_ = bf16[576,256]{1,0:T(8,128)(2,1)S(1)} collective-permute-done((bf16[576,256]{1,0:T(8,128)(2,1)}, bf16[576,256]{1,0:T(8,128)(2,1)S(1)}, u32[]{:S(2)}, u32[]{:S(2)}) %collective-permute-start) | collective-permute-done | bytes 294944 | tf_op jit(solution)/shard_map/ppermute | solution.py:397
  8.4 6.9 %attend_project.1 = (bf16[256,512]{1,0:T(8,128)(2,1)S(1)}, bf16[256,512]{1,0:T(8,128)(2,1)S(1)}, bf16[128,1792]{1,0:T(8,128)(2,1)S(1)}, bf16[128,1792]{1,0:T(8,1...) custom-call(s32[2]{0:T(128)S(1)} %pad_add_fusion.place_ref, bf16[256,2304]{1,0:T(8,128)(2,1)} %q_ref.1, ...), custom_call_target="tpu_custom_call" | custom-call | flops 2147483648 | bytes 6684672 | tf_op jit(solution)/shard_map/attend_project/pallas_call | solution.py:153
  15.3 3.1 %collective-permute-start.1 = (bf16[128,1792]{1,0:T(8,128)(2,1)S(1)}, bf16[128,1792]{1,0:T(8,128)(2,1)S(1)}, u32[]{:S(2)}, u32[]{:S(2)}) collective-permute-start(bf16[128,1792]{1,0:T(8,128)(2,1)S(1)} %get-tuple-element.34), channel_id=1, source_target_pairs={{0,1},{1,0},{2,3},{3,2},{4,5},{5,4},{6,7},{7,6},{8,9},{9,8},{10,11... | collective-permute-start | bytes 1376264 | tf_op jit(solution)/shard_map/ppermute | solution.py:392
  20.0 3.3 %project_more.1 = (bf16[128,1792]{1,0:T(8,128)(2,1)S(1)}, bf16[128,1792]{1,0:T(8,128)(2,1)S(1)}, bf16[128,1792]{1,0:T(8,128)(2,1)S(1)}, bf16[128,1792]{1,0:T(8,128)(2,1)S(1)}) custom-call(bf16[256,512]{1,0:T(8,128)(2,1)S(1)} %get-tuple-element.36.hva_ref, bf16[256,512]{1,0:T(8,128)(2,1)S(1)} %get-tuple-element.37.hvb_ref, bf16[512,7168]{1,0:T(8,128)(2,1)} %wb_ref.1, ...), custom_call_target="tpu_custom_call" | custom-call | flops 939524096 | bytes 5505024 | tf_op jit(solution)/shard_map/project_more/pallas_call | solution.py:186
  23.3 6.2 %collective-permute-done.1 = bf16[128,1792]{1,0:T(8,128)(2,1)S(1)} collective-permute-done((bf16[128,1792]{1,0:T(8,128)(2,1)S(1)}, bf16[128,1792]{1,0:T(8,128)(2,1)S(1)}, u32[]{:S(2)}, u32[]{:S(2)}) %collective-permute-start.1) | collective-permute-done | bytes 458784 | tf_op jit(solution)/shard_map/ppermute | solution.py:392
  35.4 4.2 %collective-permute-done.7 = bf16[64,1792]{1,0:T(8,128)(2,1)S(1)} collective-permute-done((bf16[64,1792]{1,0:T(8,128)(2,1)S(1)}, bf16[64,1792]{1,0:T(8,128)(2,1)S(1)}, u32[]{:S(2)}, u32[]{:S(2)}) %collective-permute-start.7) | collective-permute-done | bytes 229408 | tf_op jit(solution)/shard_map/ppermute | solution.py:392
  39.5 10.9 %collective-permute-done.6 = bf16[64,1792]{1,0:T(8,128)(2,1)S(1)} collective-permute-done((bf16[64,1792]{1,0:T(8,128)(2,1)S(1)}, bf16[64,1792]{1,0:T(8,128)(2,1)S(1)}, u32[]{:S(2)}, u32[]{:S(2)}) %collective-permute-start.6) | collective-permute-done | bytes 229408 | tf_op jit(solution)/shard_map/ppermute | solution.py:392
  50.5 3.0 %copy-done.2 = bf16[1,7168,512]{2,1,0:T(8,128)(2,1)} copy-done((bf16[1,7168,512]{2,1,0:T(8,128)(2,1)}, bf16[1,7168,512]{2,1,0:T(8,128)(2,1)S(1)}, u32[]{:S(2)}) %copy-start.2) | copy-done | bytes 7340056
  54.3 1.7 %collective-permute-start.11 = (bf16[64,1792]{1,0:T(8,128)(2,1)S(1)}, bf16[64,1792]{1,0:T(8,128)(2,1)S(1)}, u32[]{:S(2)}, u32[]{:S(2)}) collective-permute-start(bf16[64,1792]{1,0:T(8,128)(2,1)S(1)} %get-tuple-element.77), channel_id=1, source_target_pairs={{0,2},{1,3},{2,0},{3,1},{4,6},{5,7},{6,4},{7,5},{8,10},{9,11},{10,... | collective-permute-start | bytes 688136 | tf_op jit(solution)/shard_map/ppermute | solution.py:392
  57.9 4.2 %collective-permute-done.11 = bf16[64,1792]{1,0:T(8,128)(2,1)S(1)} collective-permute-done((bf16[64,1792]{1,0:T(8,128)(2,1)S(1)}, bf16[64,1792]{1,0:T(8,128)(2,1)S(1)}, u32[]{:S(2)}, u32[]{:S(2)}) %collective-permute-start.11) | collective-permute-done | bytes 229408 | tf_op jit(solution)/shard_map/ppermute | solution.py:392
  62.3 1.8 %collective-permute-start.13 = (bf16[32,3584]{1,0:T(8,128)(2,1)S(1)}, bf16[32,3584]{1,0:T(8,128)(2,1)S(1)}, u32[]{:S(2)}, u32[]{:S(2)}) collective-permute-start(bf16[32,3584]{1,0:T(8,128)(2,1)S(1)} %get-tuple-element.75), channel_id=1, source_target_pairs={{0,4},{1,5},{2,6},{3,7},{4,0},{5,1},{6,2},{7,3},{8,12},{9,13},{10,... | collective-permute-start | bytes 688136 | tf_op jit(solution)/shard_map/ppermute | solution.py:392
  64.1 2.7 %collective-permute-start.10 = (bf16[16,3584]{1,0:T(8,128)(2,1)S(1)}, bf16[16,3584]{1,0:T(8,128)(2,1)S(1)}, u32[]{:S(2)}, u32[]{:S(2)}) collective-permute-start(bf16[16,3584]{1,0:T(8,128)(2,1)S(1)} %add_convert_fusion.16), channel_id=1, source_target_pairs={{0,8},{1,9},{2,10},{3,11},{4,12},{5,13},{6,14},{7,15},{8,0},{9,1},... | collective-permute-start | bytes 344072 | tf_op jit(solution)/shard_map/ppermute | solution.py:392
  66.8 5.0 %collective-permute-done.13 = bf16[32,3584]{1,0:T(8,128)(2,1)S(1)} collective-permute-done((bf16[32,3584]{1,0:T(8,128)(2,1)S(1)}, bf16[32,3584]{1,0:T(8,128)(2,1)S(1)}, u32[]{:S(2)}, u32[]{:S(2)}) %collective-permute-start.13) | collective-permute-done | bytes 229408 | tf_op jit(solution)/shard_map/ppermute | solution.py:392
  71.8 1.9 %collective-permute-start.14 = (bf16[16,3584]{1,0:T(8,128)(2,1)S(1)}, bf16[16,3584]{1,0:T(8,128)(2,1)S(1)}, u32[]{:S(2)}, u32[]{:S(2)}) collective-permute-start(bf16[16,3584]{1,0:T(8,128)(2,1)S(1)} %get-tuple-element.86), channel_id=1, source_target_pairs={{0,8},{1,9},{2,10},{3,11},{4,12},{5,13},{6,14},{7,15},{8,0},{9,1},... | collective-permute-start | bytes 344072 | tf_op jit(solution)/shard_map/ppermute | solution.py:392
  73.7 5.1 %collective-permute-done.14 = bf16[16,3584]{1,0:T(8,128)(2,1)S(1)} collective-permute-done((bf16[16,3584]{1,0:T(8,128)(2,1)S(1)}, bf16[16,3584]{1,0:T(8,128)(2,1)S(1)}, u32[]{:S(2)}, u32[]{:S(2)}) %collective-permute-start.14) | collective-permute-done | bytes 114720 | tf_op jit(solution)/shard_map/ppermute | solution.py:392
  80.1 2.4 %collective-permute-start.16 = (bf16[16,3712]{1,0:T(8,128)(2,1)S(1)}, bf16[16,3712]{1,0:T(8,128)(2,1)S(1)}, u32[]{:S(2)}, u32[]{:S(2)}) collective-permute-start(bf16[16,3712]{1,0:T(8,128)(2,1)S(1)} %concatenate.49), channel_id=1, source_target_pairs={{0,8},{1,9},{2,10},{3,11},{4,12},{5,13},{6,14},{7,15},{8,0},{9,1},... | collective-permute-start | bytes 356360 | tf_op jit(solution)/shard_map/ppermute | solution.py:392
  82.5 4.9 %collective-permute-done.22 = bf16[16,3584]{1,0:T(8,128)(2,1)S(1)} collective-permute-done((bf16[16,3584]{1,0:T(8,128)(2,1)S(1)}, bf16[16,3584]{1,0:T(8,128)(2,1)S(1)}, u32[]{:S(2)}, u32[]{:S(2)}) %collective-permute-start.22) | collective-permute-done | bytes 114720 | tf_op jit(solution)/shard_map/ppermute | solution.py:392
  87.6 2.2 %collective-permute-done.16 = bf16[16,3712]{1,0:T(8,128)(2,1)S(1)} collective-permute-done((bf16[16,3712]{1,0:T(8,128)(2,1)S(1)}, bf16[16,3712]{1,0:T(8,128)(2,1)S(1)}, u32[]{:S(2)}, u32[]{:S(2)}) %collective-permute-start.16) | collective-permute-done | bytes 118816 | tf_op jit(solution)/shard_map/ppermute | solution.py:392
  89.9 5.7 %collective-permute-done.23 = bf16[32,3584]{1,0:T(8,128)(2,1)S(1)} collective-permute-done((bf16[32,3584]{1,0:T(8,128)(2,1)S(1)}, bf16[32,3584]{1,0:T(8,128)(2,1)S(1)}, u32[]{:S(2)}, u32[]{:S(2)}) %collective-permute-start.23) | collective-permute-done | bytes 229408 | tf_op jit(solution)/shard_map/ppermute | solution.py:392
  100.7 5.0 %collective-permute-done.24 = bf16[64,1792]{1,0:T(8,128)(2,1)S(1)} collective-permute-done((bf16[64,1792]{1,0:T(8,128)(2,1)S(1)}, bf16[64,1792]{1,0:T(8,128)(2,1)S(1)}, u32[]{:S(2)}, u32[]{:S(2)}) %collective-permute-start.24) | collective-permute-done | bytes 229408 | tf_op jit(solution)/shard_map/ppermute | solution.py:392
  106.9 3.8 %collective-permute-done.18 = bf16[64,1792]{1,0:T(8,128)(2,1)S(1)} collective-permute-done((bf16[64,1792]{1,0:T(8,128)(2,1)S(1)}, bf16[64,1792]{1,0:T(8,128)(2,1)S(1)}, u32[]{:S(2)}, u32[]{:S(2)}) %collective-permute-start.18) | collective-permute-done | bytes 229408 | tf_op jit(solution)/shard_map/ppermute | solution.py:392
  112.5 6.8 %collective-permute-done.25.refs_1_ = bf16[128,1792]{1,0:T(8,128)(2,1)S(1)} collective-permute-done((bf16[128,1792]{1,0:T(8,128)(2,1)S(1)}, bf16[128,1792]{1,0:T(8,128)(2,1)S(1)}, u32[]{:S(2)}, u32[]{:S(2)}) %collective-permute-start.25) | collective-permute-done | bytes 458784 | tf_op jit(solution)/shard_map/ppermute | solution.py:392
  120.3 7.7 %gate_up.1.refs_4_ = f32[2,256,1024]{2,1,0:T(8,128)S(1)} custom-call(bf16[128,1792]{1,0:T(8,128)(2,1)S(1)} %pad_maximum_fusion.3.refs_0_, bf16[128,1792]{1,0:T(8,128)(2,1)S(1)} %collective-permute-done.25.refs_1_, bf16[128,1792]{1,0:T(8,128)(2,1)S(1)} %pad_maximum_fusion.4.refs_2_, bf16[128,1792]{1,0:T(8,128)(2,1)S(1)} %collective-permute-done.27.refs_3_, ...), custom_call_target="tpu_custom_call" | custom-call | flops 3758096384 | bytes 16777216 | tf_op jit(solution)/shard_map/gate_up/pallas_call | solution.py:325
  127.9 17.1 %finish.1 = bf16[192,7168]{1,0:T(8,128)(2,1)} custom-call(s32[2]{0:T(128)S(1)} %pad_add_fusion.place_ref, bf16[128,1792]{1,0:T(8,128)(2,1)S(1)} %pad_maximum_fusion.1.refs_0_, bf16[128,1792]{1,0:T(8,128)(2,1)S(1)} %collective-permute-done.19.refs_1_, bf16[128,1920]{1,0:T(8,128)(2,1)S(1)} %pad_maximum_fusion.refs_2_, ...), custom_call_target="tpu_custom_call" | custom-call | flops 6576668672 | bytes 32112640 | tf_op jit(solution)/shard_map/finish/pallas_call | solution.py:360
  (89 shorter events, 22.5 us)
Async XLA Ops:
  0.6 30.3 %collective-permute-start.3 = (bf16[1,7168,512]{2,1,0:T(8,128)(2,1)}, bf16[1,7168,512]{2,1,0:T(8,128)(2,1)}, u32[]{:S(2)}, u32[]{:S(2)}) collective-permute-start(bf16[1,7168,512]{2,1,0:T(8,128)(2,1)} %refs_5_), channel_id=1, source_target_pairs={{0,16},{16,0},{1,17},{17,1},{2,18},{18,2},{3,19},{19,3},{4,20},{20... | collective-permute-start | bytes 22020104 | tf_op jit(solution)/shard_map/ppermute | solution.py:397
  15.3 14.2 %collective-permute-start.1 = (bf16[128,1792]{1,0:T(8,128)(2,1)S(1)}, bf16[128,1792]{1,0:T(8,128)(2,1)S(1)}, u32[]{:S(2)}, u32[]{:S(2)}) collective-permute-start(bf16[128,1792]{1,0:T(8,128)(2,1)S(1)} %get-tuple-element.34), channel_id=1, source_target_pairs={{0,1},{1,0},{2,3},{3,2},{4,5},{5,4},{6,7},{7,6},{8,9},{9,8},{10,11... | collective-permute-start | bytes 1376264 | tf_op jit(solution)/shard_map/ppermute | solution.py:392
  18.4 12.5 %collective-permute-start.2 = (bf16[128,1792]{1,0:T(8,128)(2,1)S(1)}, bf16[128,1792]{1,0:T(8,128)(2,1)S(1)}, u32[]{:S(2)}, u32[]{:S(2)}) collective-permute-start(bf16[128,1792]{1,0:T(8,128)(2,1)S(1)} %get-tuple-element.35), channel_id=1, source_target_pairs={{0,2},{1,3},{2,0},{3,1},{4,6},{5,7},{6,4},{7,5},{8,10},{9,11},{10,... | collective-permute-start | bytes 1376264 | tf_op jit(solution)/shard_map/ppermute | solution.py:392
  30.9 19.5 %collective-permute-start.8 = (bf16[1,7168,512]{2,1,0:T(8,128)(2,1)S(1)}, bf16[1,7168,512]{2,1,0:T(8,128)(2,1)S(1)}, u32[]{:S(2)}, u32[]{:S(2)}) collective-permute-start(bf16[1,7168,512]{2,1,0:T(8,128)(2,1)S(1)} %copy-done.1), channel_id=1, source_target_pairs={{0,16},{16,0},{1,17},{17,1},{2,18},{18,2},{3,19},{19,3},{4,20},{20... | collective-permute-start | bytes 22020104 | tf_op jit(solution)/shard_map/ppermute | solution.py:397
  31.1 8.5 %collective-permute-start.7 = (bf16[64,1792]{1,0:T(8,128)(2,1)S(1)}, bf16[64,1792]{1,0:T(8,128)(2,1)S(1)}, u32[]{:S(2)}, u32[]{:S(2)}) collective-permute-start(bf16[64,1792]{1,0:T(8,128)(2,1)S(1)} %get-tuple-element.80), channel_id=1, source_target_pairs={{0,1},{1,0},{2,3},{3,2},{4,5},{5,4},{6,7},{7,6},{8,9},{9,8},{10,11... | collective-permute-start | bytes 688136 | tf_op jit(solution)/shard_map/ppermute | solution.py:392
  31.5 18.9 %collective-permute-start.4 = (bf16[128,1792]{1,0:T(8,128)(2,1)S(1)}, bf16[128,1792]{1,0:T(8,128)(2,1)S(1)}, u32[]{:S(2)}, u32[]{:S(2)}) collective-permute-start(bf16[128,1792]{1,0:T(8,128)(2,1)S(1)} %get-tuple-element.42), channel_id=1, source_target_pairs={{0,1},{1,0},{2,3},{3,2},{4,5},{5,4},{6,7},{7,6},{8,9},{9,8},{10,11... | collective-permute-start | bytes 1376264 | tf_op jit(solution)/shard_map/ppermute | solution.py:392
  33.2 17.3 %collective-permute-start.5 = (bf16[128,1792]{1,0:T(8,128)(2,1)S(1)}, bf16[128,1792]{1,0:T(8,128)(2,1)S(1)}, u32[]{:S(2)}, u32[]{:S(2)}) collective-permute-start(bf16[128,1792]{1,0:T(8,128)(2,1)S(1)} %get-tuple-element.43), channel_id=1, source_target_pairs={{0,2},{1,3},{2,0},{3,1},{4,6},{5,7},{6,4},{7,5},{8,10},{9,11},{10,... | collective-permute-start | bytes 1376264 | tf_op jit(solution)/shard_map/ppermute | solution.py:392
  34.8 15.6 %collective-permute-start.6 = (bf16[64,1792]{1,0:T(8,128)(2,1)S(1)}, bf16[64,1792]{1,0:T(8,128)(2,1)S(1)}, u32[]{:S(2)}, u32[]{:S(2)}) collective-permute-start(bf16[64,1792]{1,0:T(8,128)(2,1)S(1)} %get-tuple-element.82), channel_id=1, source_target_pairs={{0,2},{1,3},{2,0},{3,1},{4,6},{5,7},{6,4},{7,5},{8,10},{9,11},{10,... | collective-permute-start | bytes 688136 | tf_op jit(solution)/shard_map/ppermute | solution.py:392
  53.5 25.4 %collective-permute-start.15 = (bf16[1,512,7168]{2,1,0:T(8,128)(2,1)}, bf16[1,512,7168]{2,1,0:T(8,128)(2,1)}, u32[]{:S(2)}, u32[]{:S(2)}) collective-permute-start(bf16[1,512,7168]{2,1,0:T(8,128)(2,1)} %refs_9_), channel_id=1, source_target_pairs={{0,16},{16,0},{1,17},{17,1},{2,18},{18,2},{3,19},{19,3},{4,20},{20... | collective-permute-start | bytes 22020104 | tf_op jit(solution)/shard_map/ppermute | solution.py:397
  53.8 8.4 %collective-permute-start.12 = (bf16[64,1792]{1,0:T(8,128)(2,1)S(1)}, bf16[64,1792]{1,0:T(8,128)(2,1)S(1)}, u32[]{:S(2)}, u32[]{:S(2)}) collective-permute-start(bf16[64,1792]{1,0:T(8,128)(2,1)S(1)} %get-tuple-element.79), channel_id=1, source_target_pairs={{0,1},{1,0},{2,3},{3,2},{4,5},{5,4},{6,7},{7,6},{8,9},{9,8},{10,11... | collective-permute-start | bytes 688136 | tf_op jit(solution)/shard_map/ppermute | solution.py:392
  62.3 9.5 %collective-permute-start.13 = (bf16[32,3584]{1,0:T(8,128)(2,1)S(1)}, bf16[32,3584]{1,0:T(8,128)(2,1)S(1)}, u32[]{:S(2)}, u32[]{:S(2)}) collective-permute-start(bf16[32,3584]{1,0:T(8,128)(2,1)S(1)} %get-tuple-element.75), channel_id=1, source_target_pairs={{0,4},{1,5},{2,6},{3,7},{4,0},{5,1},{6,2},{7,3},{8,12},{9,13},{10,... | collective-permute-start | bytes 688136 | tf_op jit(solution)/shard_map/ppermute | solution.py:392
  64.1 14.7 %collective-permute-start.10 = (bf16[16,3584]{1,0:T(8,128)(2,1)S(1)}, bf16[16,3584]{1,0:T(8,128)(2,1)S(1)}, u32[]{:S(2)}, u32[]{:S(2)}) collective-permute-start(bf16[16,3584]{1,0:T(8,128)(2,1)S(1)} %add_convert_fusion.16), channel_id=1, source_target_pairs={{0,8},{1,9},{2,10},{3,11},{4,12},{5,13},{6,14},{7,15},{8,0},{9,1},... | collective-permute-start | bytes 344072 | tf_op jit(solution)/shard_map/ppermute | solution.py:392
  79.4 8.0 %collective-permute-start.22 = (bf16[16,3584]{1,0:T(8,128)(2,1)S(1)}, bf16[16,3584]{1,0:T(8,128)(2,1)S(1)}, u32[]{:S(2)}, u32[]{:S(2)}) collective-permute-start(bf16[16,3584]{1,0:T(8,128)(2,1)S(1)} %get-tuple-element.66), channel_id=1, source_target_pairs={{0,8},{1,9},{2,10},{3,11},{4,12},{5,13},{6,14},{7,15},{8,0},{9,1},... | collective-permute-start | bytes 344072 | tf_op jit(solution)/shard_map/ppermute | solution.py:392
  80.1 9.6 %collective-permute-start.16 = (bf16[16,3712]{1,0:T(8,128)(2,1)S(1)}, bf16[16,3712]{1,0:T(8,128)(2,1)S(1)}, u32[]{:S(2)}, u32[]{:S(2)}) collective-permute-start(bf16[16,3712]{1,0:T(8,128)(2,1)S(1)} %concatenate.49), channel_id=1, source_target_pairs={{0,8},{1,9},{2,10},{3,11},{4,12},{5,13},{6,14},{7,15},{8,0},{9,1},... | collective-permute-start | bytes 356360 | tf_op jit(solution)/shard_map/ppermute | solution.py:392
  87.5 8.1 %collective-permute-start.23 = (bf16[32,3584]{1,0:T(8,128)(2,1)S(1)}, bf16[32,3584]{1,0:T(8,128)(2,1)S(1)}, u32[]{:S(2)}, u32[]{:S(2)}) collective-permute-start(bf16[32,3584]{1,0:T(8,128)(2,1)S(1)} %pad_maximum_fusion.11), channel_id=1, source_target_pairs={{0,4},{1,5},{2,6},{3,7},{4,0},{5,1},{6,2},{7,3},{8,12},{9,13},{10,... | collective-permute-start | bytes 688136 | tf_op jit(solution)/shard_map/ppermute | solution.py:392
  89.8 8.3 %collective-permute-start.17 = (bf16[32,3712]{1,0:T(8,128)(2,1)S(1)}, bf16[32,3712]{1,0:T(8,128)(2,1)S(1)}, u32[]{:S(2)}, u32[]{:S(2)}) collective-permute-start(bf16[32,3712]{1,0:T(8,128)(2,1)S(1)} %pad_maximum_fusion.7), channel_id=1, source_target_pairs={{0,4},{1,5},{2,6},{3,7},{4,0},{5,1},{6,2},{7,3},{8,12},{9,13},{10,... | collective-permute-start | bytes 712712 | tf_op jit(solution)/shard_map/ppermute | solution.py:392
  95.6 10.7 %collective-permute-start.26 = (bf16[64,1792]{1,0:T(8,128)(2,1)S(1)}, bf16[64,1792]{1,0:T(8,128)(2,1)S(1)}, u32[]{:S(2)}, u32[]{:S(2)}) collective-permute-start(bf16[64,1792]{1,0:T(8,128)(2,1)S(1)} %get-tuple-element.84), channel_id=1, source_target_pairs={{0,1},{1,0},{2,3},{3,2},{4,5},{5,4},{6,7},{7,6},{8,9},{9,8},{10,11... | collective-permute-start | bytes 688136 | tf_op jit(solution)/shard_map/ppermute | solution.py:392
  97.2 8.5 %collective-permute-start.24 = (bf16[64,1792]{1,0:T(8,128)(2,1)S(1)}, bf16[64,1792]{1,0:T(8,128)(2,1)S(1)}, u32[]{:S(2)}, u32[]{:S(2)}) collective-permute-start(bf16[64,1792]{1,0:T(8,128)(2,1)S(1)} %get-tuple-element.85), channel_id=1, source_target_pairs={{0,2},{1,3},{2,0},{3,1},{4,6},{5,7},{6,4},{7,5},{8,10},{9,11},{10,... | collective-permute-start | bytes 688136 | tf_op jit(solution)/shard_map/ppermute | solution.py:392
  98.2 12.5 %collective-permute-start.18 = (bf16[64,1792]{1,0:T(8,128)(2,1)S(1)}, bf16[64,1792]{1,0:T(8,128)(2,1)S(1)}, u32[]{:S(2)}, u32[]{:S(2)}) collective-permute-start(bf16[64,1792]{1,0:T(8,128)(2,1)S(1)} %pad_maximum_fusion.8), channel_id=1, source_target_pairs={{0,2},{1,3},{2,0},{3,1},{4,6},{5,7},{6,4},{7,5},{8,10},{9,11},{10,... | collective-permute-start | bytes 688136 | tf_op jit(solution)/shard_map/ppermute | solution.py:392
  99.3 11.9 %collective-permute-start.20 = (bf16[64,1920]{1,0:T(8,128)(2,1)S(1)}, bf16[64,1920]{1,0:T(8,128)(2,1)S(1)}, u32[]{:S(2)}, u32[]{:S(2)}) collective-permute-start(bf16[64,1920]{1,0:T(8,128)(2,1)S(1)} %pad_maximum_fusion.5), channel_id=1, source_target_pairs={{0,1},{1,0},{2,3},{3,2},{4,5},{5,4},{6,7},{7,6},{8,9},{9,8},{10,11... | collective-permute-start | bytes 737288 | tf_op jit(solution)/shard_map/ppermute | solution.py:392
  105.8 13.5 %collective-permute-start.25 = (bf16[128,1792]{1,0:T(8,128)(2,1)S(1)}, bf16[128,1792]{1,0:T(8,128)(2,1)S(1)}, u32[]{:S(2)}, u32[]{:S(2)}) collective-permute-start(bf16[128,1792]{1,0:T(8,128)(2,1)S(1)} %pad_maximum_fusion.3.refs_0_), channel_id=1, source_target_pairs={{0,1},{1,0},{2,3},{3,2},{4,5},{5,4},{6,7},{7,6},{8,9},{9,8},{10,11... | collective-permute-start | bytes 1376264 | tf_op jit(solution)/shard_map/ppermute | solution.py:392
  106.4 13.9 %collective-permute-start.27 = (bf16[128,1792]{1,0:T(8,128)(2,1)S(1)}, bf16[128,1792]{1,0:T(8,128)(2,1)S(1)}, u32[]{:S(2)}, u32[]{:S(2)}) collective-permute-start(bf16[128,1792]{1,0:T(8,128)(2,1)S(1)} %pad_maximum_fusion.4.refs_2_), channel_id=1, source_target_pairs={{0,2},{1,3},{2,0},{3,1},{4,6},{5,7},{6,4},{7,5},{8,10},{9,11},{10,... | collective-permute-start | bytes 1376264 | tf_op jit(solution)/shard_map/ppermute | solution.py:392
  110.7 17.2 %collective-permute-start.19 = (bf16[128,1792]{1,0:T(8,128)(2,1)S(1)}, bf16[128,1792]{1,0:T(8,128)(2,1)S(1)}, u32[]{:S(2)}, u32[]{:S(2)}) collective-permute-start(bf16[128,1792]{1,0:T(8,128)(2,1)S(1)} %pad_maximum_fusion.1.refs_0_), channel_id=1, source_target_pairs={{0,1},{1,0},{2,3},{3,2},{4,5},{5,4},{6,7},{7,6},{8,9},{9,8},{10,11... | collective-permute-start | bytes 1376264 | tf_op jit(solution)/shard_map/ppermute | solution.py:392
  111.3 16.6 %collective-permute-start.21 = (bf16[128,1920]{1,0:T(8,128)(2,1)S(1)}, bf16[128,1920]{1,0:T(8,128)(2,1)S(1)}, u32[]{:S(2)}, u32[]{:S(2)}) collective-permute-start(bf16[128,1920]{1,0:T(8,128)(2,1)S(1)} %pad_maximum_fusion.refs_2_), channel_id=1, source_target_pairs={{0,2},{1,3},{2,0},{3,1},{4,6},{5,7},{6,4},{7,5},{8,10},{9,11},{10,... | collective-permute-start | bytes 1474568 | tf_op jit(solution)/shard_map/ppermute | solution.py:392
  (11 other events, 217.1 us)

commit v3 on v2

--- a/solution.py
+++ b/solution.py
@@ -173,7 +173,7 @@
             transcendentals=rows * span * heads,
         ),
         name="attend_project",
-    )(place, in_hbm(queries), *keys, in_hbm(value_up), in_hbm(out_proj), in_hbm(out_proj))
+    )(place, in_hbm(queries), in_hbm(keys[0]), *keys[1:], in_hbm(value_up), in_hbm(out_proj), in_hbm(out_proj))
 
 
 def project_more(hva, hvb, out_proj, chunk):
@@ -199,189 +199,238 @@
     )(hva, hvb, in_hbm(out_proj), in_hbm(out_proj))
 
 
-def place_rows(quarter_rows, columns, deep, a_refs, b_refs, x_ref):
+def place_rows(quarter_rows, columns, a_refs, b_refs, x_ref):
     a_low, a_high = a_refs
     b_low, b_high = b_refs
     q = quarter_rows
-    pieces = [
+    for ref, source, count, target, first in (
         (a_low, 0, 2 * q, 0, 0),
         (a_high, 0, 2 * q, 2 * q, 0),
         (b_low, 0, q, 0, columns),
         (b_low, q, q, 2 * q, columns),
         (b_high, 0, q, q, columns),
         (b_high, q, q, 3 * q, columns),
-    ]
-    for ref, source, count, target, first in pieces:
-        done = 0
-        while done < columns:
-            tile, inside = divmod(first + done, deep)
-            size = min(deep - inside, columns - done)
-            x_ref[tile, target : target + count, inside : inside + size] = ref[
-                source : source + count, done : done + size
+    ):
+        x_ref[target : target + count, first : first + columns] = ref[
+            source : source + count, :columns
+        ]
+
+
+def weight_copies(pieces, held_ref, sems, first_row):
+    deep = held_ref.shape[1]
+    copies = []
+    for p, w_ref in enumerate(pieces):
+        cuts = (0, deep // 2, deep) if p == 0 else (0, deep)
+        copies.append(
+            [
+                (
+                    low,
+                    high,
+                    pltpu.make_async_copy(
+                        w_ref.at[0, first_row + low : first_row + high, :],
+                        held_ref.at[p, low:high, :],
+                        sems.at[p + (n if p == 0 else 1)],
+                    ),
+                )
+                for n, (low, high) in enumerate(zip(cuts, cuts[1:]))
             ]
-            done += size
-
-
-def gate_up_step(x, gates, ups, acc_ref, base_ref):
-    for n, group in enumerate((gates, ups)):
-        for p, w_ref in enumerate(group):
-            wide = w_ref.shape[2]
-            cols = slice(p * wide, (p + 1) * wide)
-            acc_ref[n, :, cols] = base_ref[n, :, cols] + jnp.dot(
-                x, w_ref[0], preferred_element_type=f32
-            )
-
-
-def gate_up_kernel(slabs, quarter_rows, columns, deep, *refs):
+        )
+    return copies
+
+
+def start_all(copies):
+    for group in copies:
+        for _, _, copy in group:
+            copy.start()
+
+
+def times_piece(x_ref, held_ref, p, group):
+    total = None
+    for low, high, copy in group:
+        copy.wait()
+        term = jnp.dot(x_ref[:, low:high], held_ref[p, low:high, :], preferred_element_type=f32)
+        total = term if total is None else total + term
+    return total
+
+
+def gate_up_kernel(slabs, quarter_rows, columns, *refs):
     a_refs, b_refs = refs[:2], refs[2:4]
-    gates, ups = refs[4 : 4 + slabs], refs[4 + slabs : 4 + 2 * slabs]
-    acc_ref, x_ref = refs[4 + 2 * slabs :]
-
-    @pl.when(pl.program_id(0) == 0)
-    def _():
-        place_rows(quarter_rows, columns, deep, a_refs, b_refs, x_ref)
-        acc_ref[...] = jnp.zeros_like(acc_ref)
-
-    gate_up_step(x_ref[pl.program_id(0)], gates, ups, acc_ref, acc_ref)
-
-
-def finish_kernel(
-    slabs, quarter_rows, columns, deep, steps, block, order, top, senders, slots, place_ref, *refs
-):
+    pieces = refs[4 : 4 + 2 * slabs]
+    acc_ref, x_ref, held_ref, sems = refs[4 + 2 * slabs :]
+    copies = weight_copies(pieces, held_ref, sems, 0)
+    start_all(copies)
+    place_rows(quarter_rows, columns, a_refs, b_refs, x_ref)
+    wide = held_ref.shape[2]
+    for p, group in enumerate(copies):
+        kind, place = divmod(p, slabs)
+        acc_ref[kind, :, place * wide : (place + 1) * wide] = times_piece(
+            x_ref, held_ref, p, group
+        )
+
+
+def finish_kernel(slabs, quarter_rows, columns, block, order, top, senders, place_ref, *refs):
     a_refs, b_refs = refs[:2], refs[2:4]
     base_ref = refs[4]
-    gates, ups = refs[5 : 5 + slabs], refs[5 + slabs : 5 + 2 * slabs]
+    pieces = refs[5 : 5 + 2 * slabs]
     downs = refs[5 + 2 * slabs : 5 + 3 * slabs]
-    out_ref, x_ref, acc_ref, act_ref, gate_ref = refs[5 + 3 * slabs :]
-    step = pl.program_id(0)
+    (out_hbm, x_ref, held_ref, acc_ref, act_ref, down_ref, out_ref, sems, down_sems, out_sems) = refs[
+        5 + 3 * slabs :
+    ]
     rows = 4 * quarter_rows
     q = quarter_rows
-
-    @pl.when(step == 0)
-    def _():
-        place_rows(quarter_rows, columns, deep, a_refs, b_refs, x_ref)
-        gate_up_step(x_ref[0], gates, ups, acc_ref, base_ref)
-
-    @pl.when((step > 0) & (step < steps))
-    def _():
-        gate_up_step(x_ref[step], gates, ups, acc_ref, acc_ref)
-
-    @pl.when(step == steps - 1)
-    def _():
-        me = place_ref[1]
-        b_low, b_high = b_refs
-        meta = jnp.concatenate(
-            [b_low[:q, columns:], b_high[:q, columns:], b_low[q:, columns:], b_high[q:, columns:]],
-            axis=0,
-        ).astype(f32)
-        lane = lax.broadcasted_iota(jnp.int32, (rows, LANES), 1)
-        named = (lane < top) & (meta == me.astype(f32))
-        hit = jnp.max(jnp.where(named, 1.0, 0.0), axis=1, keepdims=True)
-        aligned = pltpu.roll(meta, LANES - top, 1)
-        gate = jnp.sum(jnp.where(named, aligned, 0.0), axis=1, keepdims=True)
-        inverse = jnp.sum(
-            jnp.where((lane == 2 * top) | (lane == 2 * top + 1), meta, 0.0), axis=1, keepdims=True
-        )
-        r = lax.broadcasted_iota(jnp.int32, (rows, rows), 0)
-        c = lax.broadcasted_iota(jnp.int32, (rows, rows), 1)
-        shift = bits_of(block)
-        before = jnp.where(((r >> shift) == (c >> shift)) & (c < r), 1.0, 0.0).astype(bf16)
-        hits = jnp.broadcast_to(hit, (rows, LANES))
-        slot = jnp.dot(before, hits.astype(bf16), preferred_element_type=f32)
-        pos = lax.broadcasted_iota(jnp.int32, (rows, LANES), 0) >> shift
-        sender = (relative_of(pos, order) ^ me).astype(f32)
-        target = jnp.where(hits > 0.5, slot * senders + sender, -1.0)
-        target_row = jnp.transpose(target)[:1, :]
-        wanted = lax.broadcasted_iota(jnp.int32, (slots, rows), 0).astype(f32)
-        select = jnp.where(wanted == target_row, 1.0, 0.0).astype(bf16)
-        gate_ref[...] = jnp.dot(
-            select,
-            jnp.broadcast_to(gate, (rows, LANES)).astype(bf16),
-            preferred_element_type=f32,
-        )
-        gated = acc_ref[0] * inverse
-        upped = acc_ref[1] * inverse
-        act = (gated / (1.0 + jnp.exp(-gated)) * upped).astype(bf16)
-        act_ref[...] = jnp.dot(select, act, preferred_element_type=f32).astype(bf16)
-
-    @pl.when(step >= steps)
-    def _():
-        total = None
-        for p, w_ref in enumerate(downs):
-            part = w_ref.shape[1]
-            term = jnp.dot(
-                act_ref[:, p * part : (p + 1) * part], w_ref[0], preferred_element_type=f32
+    slots, width = out_ref.shape
+    part = downs[0].shape[1]
+    wide = held_ref.shape[2]
+    tiles = down_sems.shape[0]
+    tile = width // tiles
+    copies = weight_copies(pieces, held_ref, sems, 2 * columns)
+    start_all(copies)
+    down_copies = [
+        [
+            pltpu.make_async_copy(
+                w_ref.at[0, :, j * tile : (j + 1) * tile],
+                down_ref.at[p * part : (p + 1) * part, j * tile : (j + 1) * tile],
+                down_sems.at[j, p],
             )
-            total = term if total is None else total + term
-        out_ref[...] = (total * gate_ref[:, :1]).astype(bf16)
-
-
-def gate_up(a, b, gates, ups, deep):
+            for p, w_ref in enumerate(downs)
+        ]
+        for j in range(tiles)
+    ]
+    for group in down_copies:
+        for copy in group:
+            copy.start()
+    place_rows(quarter_rows, columns, a_refs, b_refs, x_ref)
+
+    me = place_ref[1]
+    b_low, b_high = b_refs
+    meta = jnp.concatenate(
+        [b_low[:q, columns:], b_high[:q, columns:], b_low[q:, columns:], b_high[q:, columns:]],
+        axis=0,
+    ).astype(f32)
+    lane = lax.broadcasted_iota(jnp.int32, (rows, LANES), 1)
+    named = (lane < top) & (meta == me.astype(f32))
+    hit = jnp.max(jnp.where(named, 1.0, 0.0), axis=1, keepdims=True)
+    aligned = pltpu.roll(meta, LANES - top, 1)
+    gate = jnp.sum(jnp.where(named, aligned, 0.0), axis=1, keepdims=True)
+    inverse = jnp.sum(
+        jnp.where((lane == 2 * top) | (lane == 2 * top + 1), meta, 0.0), axis=1, keepdims=True
+    )
+    r = lax.broadcasted_iota(jnp.int32, (rows, rows), 0)
+    c = lax.broadcasted_iota(jnp.int32, (rows, rows), 1)
+    shift = bits_of(block)
+    before = jnp.where(((r >> shift) == (c >> shift)) & (c < r), 1.0, 0.0).astype(bf16)
+    hits = jnp.broadcast_to(hit, (rows, LANES))
+    slot = jnp.dot(before, hits.astype(bf16), preferred_element_type=f32)
+    pos = lax.broadcasted_iota(jnp.int32, (rows, LANES), 0) >> shift
+    sender = (relative_of(pos, order) ^ me).astype(f32)
+    target = jnp.where(hits > 0.5, slot * senders + sender, -1.0)
+    target_row = jnp.transpose(target)[:1, :]
+    wanted = lax.broadcasted_iota(jnp.int32, (slots, rows), 0).astype(f32)
+    select = jnp.where(wanted == target_row, 1.0, 0.0).astype(bf16)
+    slot_gate = jnp.dot(
+        select,
+        jnp.broadcast_to(gate, (rows, LANES)).astype(bf16),
+        preferred_element_type=f32,
+    )[:, :1]
+
+    for place in range(slabs):
+        cols = slice(place * wide, (place + 1) * wide)
+        both = []
+        for kind in range(2):
+            p = kind * slabs + place
+            total = base_ref[kind, :, cols] + times_piece(x_ref, held_ref, p, copies[p])
+            if kind == 0:
+                acc_ref[:, cols] = total
+            both.append(total)
+        gated = acc_ref[:, cols] * inverse
+        act = (gated / (1.0 + jnp.exp(-gated)) * (both[1] * inverse)).astype(bf16)
+        act_ref[:, cols] = jnp.dot(select, act, preferred_element_type=f32).astype(bf16)
+
+    out_copies = []
+    for j, group in enumerate(down_copies):
+        cols = slice(j * tile, (j + 1) * tile)
+        for copy in group:
+            copy.wait()
+        total = jnp.dot(act_ref[...], down_ref[:, cols], preferred_element_type=f32)
+        out_ref[:, cols] = (total * slot_gate).astype(bf16)
+        copy = pltpu.make_async_copy(out_ref.at[:, cols], out_hbm.at[:, cols], out_sems.at[j])
+        copy.start()
+        out_copies.append(copy)
+    for copy in out_copies:
+        copy.wait()
+
+
+def in_vmem():
+    return pl.BlockSpec(memory_space=pltpu.VMEM)
+
+
+def in_any():
+    return pl.BlockSpec(memory_space=pl.ANY)
+
+
+def gate_up(a, b, gates, ups):
     half, columns = a[0].shape
     rows = 2 * half
-    hidden = sum(w.shape[2] for w in gates)
-    steps = 2 * columns // deep
-    spec = [pl.BlockSpec((1, deep, w.shape[2]), lambda i: (0, i, 0)) for w in gates + ups]
+    pieces = gates + ups
+    wide = pieces[0].shape[2]
+    hidden = wide * len(gates)
     return pl.pallas_call(
-        functools.partial(gate_up_kernel, len(gates), rows // 4, columns, deep),
-        grid=(steps,),
-        in_specs=[whole(v.shape) for v in a + b] + spec,
-        out_specs=whole((2, rows, hidden)),
+        functools.partial(gate_up_kernel, len(gates), rows // 4, columns),
+        in_specs=[in_vmem()] * 4 + [in_any()] * len(pieces),
+        out_specs=in_vmem(),
         out_shape=jax.ShapeDtypeStruct((2, rows, hidden), f32),
-        scratch_shapes=[pltpu.VMEM((steps, rows, deep), bf16)],
-        compiler_params=pltpu.CompilerParams(vmem_limit_bytes=40 << 20),
+        scratch_shapes=[
+            pltpu.VMEM((rows, 2 * columns), bf16),
+            pltpu.VMEM((len(pieces), 2 * columns, wide), bf16),
+            pltpu.SemaphoreType.DMA((len(pieces) + 1,)),
+        ],
+        compiler_params=pltpu.CompilerParams(vmem_limit_bytes=20 << 20),
         cost_estimate=pl.CostEstimate(
             flops=8 * rows * columns * hidden,
             bytes_accessed=8 * columns * hidden + 8 * rows * hidden,
             transcendentals=0,
         ),
         name="gate_up",
-    )(*a, *b, *map(in_hbm, gates + ups))
-
-
-def finish(place, a, b, base, gates, ups, downs, deep, block, order, top, senders, capacity):
+    )(*a, *b, *map(in_hbm, pieces))
+
+
+def finish(place, a, b, base, gates, ups, downs, block, order, top, senders, capacity):
     half, columns = a[0].shape
     rows = 2 * half
-    hidden = sum(w.shape[2] for w in gates)
+    pieces = gates + ups
+    wide = pieces[0].shape[2]
+    hidden = wide * len(gates)
     width = downs[0].shape[2]
-    steps = 2 * columns // deep
-    tile = column_tile(width, 1792)
-    more = width // tile
+    tiles = width // column_tile(width, 1024)
     slots = senders * capacity
-    last = steps - 1
-    spec = [
-        pl.BlockSpec((1, deep, w.shape[2]), lambda i: (0, steps + jnp.minimum(i, last), 0))
-        for w in gates + ups
-    ]
-    spec += [
-        pl.BlockSpec((1, w.shape[1], tile), lambda i: (0, 0, jnp.maximum(i - steps, 0)))
-        for w in downs
-    ]
     return pl.pallas_call(
         functools.partial(
-            finish_kernel, len(gates), rows // 4, columns, deep, steps, block, order, top, senders, slots
+            finish_kernel, len(gates), rows // 4, columns, block, order, top, senders
         ),
-        grid=(steps + more,),
         in_specs=[pl.BlockSpec(memory_space=pltpu.SMEM)]
-        + [whole(v.shape) for v in a + b]
-        + [whole(base.shape)]
-        + spec,
-        out_specs=pl.BlockSpec((slots, tile), lambda i: (0, jnp.maximum(i - steps, 0))),
+        + [in_vmem()] * 5
+        + [in_any()] * (len(pieces) + len(downs)),
+        out_specs=in_any(),
         out_shape=jax.ShapeDtypeStruct((slots, width), bf16),
         scratch_shapes=[
-            pltpu.VMEM((steps, rows, deep), bf16),
-            pltpu.VMEM((2, rows, hidden), f32),
+            pltpu.VMEM((rows, 2 * columns), bf16),
+            pltpu.VMEM((len(pieces), 2 * columns, wide), bf16),
+            pltpu.VMEM((rows, hidden), f32),
             pltpu.VMEM((slots, hidden), bf16),
-            pltpu.VMEM((slots, LANES), f32),
+            pltpu.VMEM((hidden, width), bf16),
+            pltpu.VMEM((slots, width), bf16),
+            pltpu.SemaphoreType.DMA((len(pieces) + 1,)),
+            pltpu.SemaphoreType.DMA((tiles, len(downs))),
+            pltpu.SemaphoreType.DMA((tiles,)),
         ],
-        compiler_params=pltpu.CompilerParams(vmem_limit_bytes=44 << 20),
+        compiler_params=pltpu.CompilerParams(vmem_limit_bytes=42 << 20),
         cost_estimate=pl.CostEstimate(
             flops=8 * rows * columns * hidden + 2 * slots * hidden * width,
             bytes_accessed=8 * columns * hidden + 2 * hidden * width + 2 * slots * width,
             transcendentals=rows * hidden,
         ),
         name="finish",
-    )(place, *a, *b, base, *map(in_hbm, gates + ups + downs))
+    )(place, *a, *b, base, *map(in_hbm, pieces + downs))
 
 
 def add(a, b):
@@ -455,22 +504,27 @@
     place = jnp.stack([lax.axis_index("ctx"), lax.axis_index("exp")]).astype(jnp.int32)
 
     keys = shifted(latent.T, slabs)
-    gate_parts = shifted(w_gate, slabs)
+    arrived, gate_source, up_source = tie(keys[1:], w_gate, w_up)
+    keys = [keys[0], *arrived]
+    gate_others = shifted(gate_source, slabs)[1:]
+    up_others = shifted(up_source, slabs)[1:]
 
     hva, hvb, *parts = attend_project(
         place, queries, keys, value_up, out_proj, block, orders
     )
     more = project_more(hva, hvb, out_proj, 1)
     got = first_swap(parts, senders)
-    got, more, gate_parts, w_up = tie(got, more, gate_parts, w_up)
-    up_parts = shifted(w_up, slabs)
+    got, more, gate_others = tie(got, more, gate_others)
     terms = [second_swap(parts, got, senders)]
     got = first_swap(more, senders)
-    got, terms[0], up_parts, w_down = tie(got, terms[0], up_parts, w_down)
-    down_parts = shifted(w_down, slabs)
+    got, terms[0], up_others, down_source = tie(got, terms[0], up_others, w_down)
+    down_others = shifted(down_source, slabs)[1:]
     terms.append(second_swap(more, got, senders))
     sums = [last_swaps(t, senders, bits) for t in terms]
-    sums[1], down_parts = tie(sums[1], down_parts)
+    sums[1], down_others = tie(sums[1], down_others)
+    gate_parts = [w_gate, *gate_others]
+    up_parts = [w_up, *up_others]
+    down_parts = [w_down, *down_others]
     half_width = width // 2
     gain = norm_gain.astype(f32)
     hidden, payload, squares = [], [], 0.0
@@ -495,12 +549,11 @@
     )
     payload[1] = jnp.concatenate([payload[1], meta], axis=1)
 
-    deep = column_tile(half_width, 1792)
     a, b = gather_rows(payload[0], half_width // 2, senders, bits)
-    base = gate_up(a, b, gate_parts, up_parts, deep)
+    base = gate_up(a, b, gate_parts, up_parts)
     a, b = gather_rows(payload[1], half_width // 2, senders, bits)
     slots = finish(
-        place, a, b, base, gate_parts, up_parts, down_parts, deep, block, orders[0], top, senders, capacity
+        place, a, b, base, gate_parts, up_parts, down_parts, block, orders[0], top, senders, capacity
     )
     expert_out = slots.reshape(capacity, senders, width).transpose(1, 0, 2)[None, None]
     return jnp.concatenate(hidden, axis=1), expert_out

time: 145 us -> 135 us (0.931)
  waiting for transfers between devices: 72.6 us -> 65.2 us
  local copies, waits for them, and re-layouts: 4.56 us -> 0.6 us
    ppermute x4, waiting for transfers between devices: 6.14 us -> 1.43 us  [shifted(): lax.ppermute(value, 'ctx', [(i, (i + k) % count) for i in range(count)])]
    unnamed x17 -> x11, local copies, waits for them, and re-layouts: 4.03 us -> 0.07 us
    ppermute x24, waiting for transfers between devices: 66.4 us -> 63.7 us  [swap(): return lax.ppermute(value, 'exp', [(i, i ^ 1 << bit) for i in range(count)])]
  transfers between devices with their start and end apart: 28 -> 28, of which waited for: 15 -> 15; matrix products, arithmetic and copies ran while one was open for 2% -> 2% of each run, Pallas kernels for 12% -> 13%
where the time goes in v3:
time: 135 us; the launch traced here: 134 us
  waiting for transfers between devices  65.2 us (48%)
  Pallas kernels  34.4 us (25%)
  starting transfers between devices  30.9 us (23%)
  other arithmetic  2.2 us (2%)
    ppermute x24, waiting for transfers between devices, swap(): return lax.ppermute(value, 'exp', [(i, i ^ 1 << bit) for i in range(count)])  63.7 us
    ppermute x24, starting transfers between devices, swap(): return lax.ppermute(value, 'exp', [(i, i ^ 1 << bit) for i in range(count)])  29.9 us
    pallas_call x1, Pallas kernels, finish(): pl.pallas_call(functools.partial(finish_kernel, len(gates), rows // 4, co...  17.6 us
    pallas_call x1, Pallas kernels, attend_project(): pl.pallas_call(functools.partial(attend_kernel, slabs, block, orders), gr...  6.97 us
    pallas_call x1, Pallas kernels, gate_up(): pl.pallas_call(functools.partial(gate_up_kernel, len(gates), rows // 4, c...  6.54 us
    pallas_call x1, Pallas kernels, project_more(): pl.pallas_call(project_kernel, grid=(steps,), in_specs=[whole(hva.shape),...  3.33 us
  transfers between devices with their start and end apart: 28, of which 15 were waited for; matrix products, arithmetic and copies ran while one was open for 2% of the time, Pallas kernels for 13%

profile of v3, /device:TPU:0, one launch (start us, length us, event | category | flops | bytes accessed | tf_op | source)
XLA Modules:
  0.0 134.4 jit_solution(11937023910454288687)
XLA Ops:
  3.2 7.0 %attend_project.1 = (bf16[256,512]{1,0:T(8,128)(2,1)S(1)}, bf16[256,512]{1,0:T(8,128)(2,1)S(1)}, bf16[128,1792]{1,0:T(8,128)(2,1)S(1)}, bf16[128,1792]{1,0:T(8,1...) custom-call(s32[2]{0:T(128)S(1)} %pad_add_fusion.place_ref, bf16[256,2304]{1,0:T(8,128)(2,1)} %q_ref.1, ...), custom_call_target="tpu_custom_call" | custom-call | flops 2147483648 | bytes 6684672 | tf_op jit(solution)/shard_map/attend_project/pallas_call | solution.py:153
  10.1 2.9 %collective-permute-start.1 = (bf16[128,1792]{1,0:T(8,128)(2,1)S(1)}, bf16[128,1792]{1,0:T(8,128)(2,1)S(1)}, u32[]{:S(2)}, u32[]{:S(2)}) collective-permute-start(bf16[128,1792]{1,0:T(8,128)(2,1)S(1)} %get-tuple-element.34), channel_id=1, source_target_pairs={{0,1},{1,0},{2,3},{3,2},{4,5},{5,4},{6,7},{7,6},{8,9},{9,8},{10,11... | collective-permute-start | bytes 1376264 | tf_op jit(solution)/shard_map/ppermute | solution.py:441
  13.0 1.5 %collective-permute-start.2 = (bf16[128,1792]{1,0:T(8,128)(2,1)S(1)}, bf16[128,1792]{1,0:T(8,128)(2,1)S(1)}, u32[]{:S(2)}, u32[]{:S(2)}) collective-permute-start(bf16[128,1792]{1,0:T(8,128)(2,1)S(1)} %get-tuple-element.35), channel_id=1, source_target_pairs={{0,2},{1,3},{2,0},{3,1},{4,6},{5,7},{6,4},{7,5},{8,10},{9,11},{10,... | collective-permute-start | bytes 1376264 | tf_op jit(solution)/shard_map/ppermute | solution.py:441
  14.6 3.3 %project_more.1 = (bf16[128,1792]{1,0:T(8,128)(2,1)S(1)}, bf16[128,1792]{1,0:T(8,128)(2,1)S(1)}, bf16[128,1792]{1,0:T(8,128)(2,1)S(1)}, bf16[128,1792]{1,0:T(8,128)(2,1)S(1)}) custom-call(bf16[256,512]{1,0:T(8,128)(2,1)S(1)} %get-tuple-element.36.hva_ref, bf16[256,512]{1,0:T(8,128)(2,1)S(1)} %get-tuple-element.37.hvb_ref, bf16[512,7168]{1,0:T(8,128)(2,1)} %wb_ref.1, ...), custom_call_target="tpu_custom_call" | custom-call | flops 939524096 | bytes 5505024 | tf_op jit(solution)/shard_map/project_more/pallas_call | solution.py:186
  17.9 5.9 %collective-permute-done.1 = bf16[128,1792]{1,0:T(8,128)(2,1)S(1)} collective-permute-done((bf16[128,1792]{1,0:T(8,128)(2,1)S(1)}, bf16[128,1792]{1,0:T(8,128)(2,1)S(1)}, u32[]{:S(2)}, u32[]{:S(2)}) %collective-permute-start.1) | collective-permute-done | bytes 458784 | tf_op jit(solution)/shard_map/ppermute | solution.py:441
  25.9 1.6 %collective-permute-start.4 = (bf16[128,1792]{1,0:T(8,128)(2,1)S(1)}, bf16[128,1792]{1,0:T(8,128)(2,1)S(1)}, u32[]{:S(2)}, u32[]{:S(2)}) collective-permute-start(bf16[128,1792]{1,0:T(8,128)(2,1)S(1)} %get-tuple-element.43), channel_id=1, source_target_pairs={{0,1},{1,0},{2,3},{3,2},{4,5},{5,4},{6,7},{7,6},{8,9},{9,8},{10,11... | collective-permute-start | bytes 1376264 | tf_op jit(solution)/shard_map/ppermute | solution.py:441
  29.8 4.3 %collective-permute-done.7 = bf16[64,1792]{1,0:T(8,128)(2,1)S(1)} collective-permute-done((bf16[64,1792]{1,0:T(8,128)(2,1)S(1)}, bf16[64,1792]{1,0:T(8,128)(2,1)S(1)}, u32[]{:S(2)}, u32[]{:S(2)}) %collective-permute-start.7) | collective-permute-done | bytes 229408 | tf_op jit(solution)/shard_map/ppermute | solution.py:441
  34.1 9.3 %collective-permute-done.6 = bf16[64,1792]{1,0:T(8,128)(2,1)S(1)} collective-permute-done((bf16[64,1792]{1,0:T(8,128)(2,1)S(1)}, bf16[64,1792]{1,0:T(8,128)(2,1)S(1)}, u32[]{:S(2)}, u32[]{:S(2)}) %collective-permute-start.6) | collective-permute-done | bytes 229408 | tf_op jit(solution)/shard_map/ppermute | solution.py:441
  46.2 1.7 %collective-permute-start.9 = (bf16[32,3584]{1,0:T(8,128)(2,1)S(1)}, bf16[32,3584]{1,0:T(8,128)(2,1)S(1)}, u32[]{:S(2)}, u32[]{:S(2)}) collective-permute-start(bf16[32,3584]{1,0:T(8,128)(2,1)S(1)} %get-tuple-element.71), channel_id=1, source_target_pairs={{0,4},{1,5},{2,6},{3,7},{4,0},{5,1},{6,2},{7,3},{8,12},{9,13},{10,... | collective-permute-start | bytes 688136 | tf_op jit(solution)/shard_map/ppermute | solution.py:441
  47.9 4.4 %collective-permute-done.11 = bf16[64,1792]{1,0:T(8,128)(2,1)S(1)} collective-permute-done((bf16[64,1792]{1,0:T(8,128)(2,1)S(1)}, bf16[64,1792]{1,0:T(8,128)(2,1)S(1)}, u32[]{:S(2)}, u32[]{:S(2)}) %collective-permute-start.11) | collective-permute-done | bytes 229408 | tf_op jit(solution)/shard_map/ppermute | solution.py:441
  52.5 1.6 %collective-permute-start.13 = (bf16[32,3584]{1,0:T(8,128)(2,1)S(1)}, bf16[32,3584]{1,0:T(8,128)(2,1)S(1)}, u32[]{:S(2)}, u32[]{:S(2)}) collective-permute-start(bf16[32,3584]{1,0:T(8,128)(2,1)S(1)} %get-tuple-element.73), channel_id=1, source_target_pairs={{0,4},{1,5},{2,6},{3,7},{4,0},{5,1},{6,2},{7,3},{8,12},{9,13},{10,... | collective-permute-start | bytes 688136 | tf_op jit(solution)/shard_map/ppermute | solution.py:441
  54.1 2.7 %collective-permute-start.10 = (bf16[16,3584]{1,0:T(8,128)(2,1)S(1)}, bf16[16,3584]{1,0:T(8,128)(2,1)S(1)}, u32[]{:S(2)}, u32[]{:S(2)}) collective-permute-start(bf16[16,3584]{1,0:T(8,128)(2,1)S(1)} %add_convert_fusion.16), channel_id=1, source_target_pairs={{0,8},{1,9},{2,10},{3,11},{4,12},{5,13},{6,14},{7,15},{8,0},{9,1},... | collective-permute-start | bytes 344072 | tf_op jit(solution)/shard_map/ppermute | solution.py:441
  56.7 5.2 %collective-permute-done.13 = bf16[32,3584]{1,0:T(8,128)(2,1)S(1)} collective-permute-done((bf16[32,3584]{1,0:T(8,128)(2,1)S(1)}, bf16[32,3584]{1,0:T(8,128)(2,1)S(1)}, u32[]{:S(2)}, u32[]{:S(2)}) %collective-permute-start.13) | collective-permute-done | bytes 229408 | tf_op jit(solution)/shard_map/ppermute | solution.py:441
  61.9 1.7 %collective-permute-start.14 = (bf16[16,3584]{1,0:T(8,128)(2,1)S(1)}, bf16[16,3584]{1,0:T(8,128)(2,1)S(1)}, u32[]{:S(2)}, u32[]{:S(2)}) collective-permute-start(bf16[16,3584]{1,0:T(8,128)(2,1)S(1)} %get-tuple-element.84), channel_id=1, source_target_pairs={{0,8},{1,9},{2,10},{3,11},{4,12},{5,13},{6,14},{7,15},{8,0},{9,1},... | collective-permute-start | bytes 344072 | tf_op jit(solution)/shard_map/ppermute | solution.py:441
  63.6 5.3 %collective-permute-done.14 = bf16[16,3584]{1,0:T(8,128)(2,1)S(1)} collective-permute-done((bf16[16,3584]{1,0:T(8,128)(2,1)S(1)}, bf16[16,3584]{1,0:T(8,128)(2,1)S(1)}, u32[]{:S(2)}, u32[]{:S(2)}) %collective-permute-start.14) | collective-permute-done | bytes 114720 | tf_op jit(solution)/shard_map/ppermute | solution.py:441
  70.1 2.5 %collective-permute-start.16 = (bf16[16,3712]{1,0:T(8,128)(2,1)S(1)}, bf16[16,3712]{1,0:T(8,128)(2,1)S(1)}, u32[]{:S(2)}, u32[]{:S(2)}) collective-permute-start(bf16[16,3712]{1,0:T(8,128)(2,1)S(1)} %concatenate.49), channel_id=1, source_target_pairs={{0,8},{1,9},{2,10},{3,11},{4,12},{5,13},{6,14},{7,15},{8,0},{9,1},... | collective-permute-start | bytes 356360 | tf_op jit(solution)/shard_map/ppermute | solution.py:441
  72.6 4.6 %collective-permute-done.22 = bf16[16,3584]{1,0:T(8,128)(2,1)S(1)} collective-permute-done((bf16[16,3584]{1,0:T(8,128)(2,1)S(1)}, bf16[16,3584]{1,0:T(8,128)(2,1)S(1)}, u32[]{:S(2)}, u32[]{:S(2)}) %collective-permute-start.22) | collective-permute-done | bytes 114720 | tf_op jit(solution)/shard_map/ppermute | solution.py:441
  77.4 2.3 %collective-permute-done.16 = bf16[16,3712]{1,0:T(8,128)(2,1)S(1)} collective-permute-done((bf16[16,3712]{1,0:T(8,128)(2,1)S(1)}, bf16[16,3712]{1,0:T(8,128)(2,1)S(1)}, u32[]{:S(2)}, u32[]{:S(2)}) %collective-permute-start.16) | collective-permute-done | bytes 118816 | tf_op jit(solution)/shard_map/ppermute | solution.py:441
  79.8 5.6 %collective-permute-done.23 = bf16[32,3584]{1,0:T(8,128)(2,1)S(1)} collective-permute-done((bf16[32,3584]{1,0:T(8,128)(2,1)S(1)}, bf16[32,3584]{1,0:T(8,128)(2,1)S(1)}, u32[]{:S(2)}, u32[]{:S(2)}) %collective-permute-start.23) | collective-permute-done | bytes 229408 | tf_op jit(solution)/shard_map/ppermute | solution.py:441
  90.7 4.8 %collective-permute-done.24 = bf16[64,1792]{1,0:T(8,128)(2,1)S(1)} collective-permute-done((bf16[64,1792]{1,0:T(8,128)(2,1)S(1)}, bf16[64,1792]{1,0:T(8,128)(2,1)S(1)}, u32[]{:S(2)}, u32[]{:S(2)}) %collective-permute-start.24) | collective-permute-done | bytes 229408 | tf_op jit(solution)/shard_map/ppermute | solution.py:441
  97.1 3.2 %collective-permute-done.18 = bf16[64,1792]{1,0:T(8,128)(2,1)S(1)} collective-permute-done((bf16[64,1792]{1,0:T(8,128)(2,1)S(1)}, bf16[64,1792]{1,0:T(8,128)(2,1)S(1)}, u32[]{:S(2)}, u32[]{:S(2)}) %collective-permute-start.18) | collective-permute-done | bytes 229408 | tf_op jit(solution)/shard_map/ppermute | solution.py:441
  102.7 6.4 %collective-permute-done.25.refs_1_ = bf16[128,1792]{1,0:T(8,128)(2,1)S(1)} collective-permute-done((bf16[128,1792]{1,0:T(8,128)(2,1)S(1)}, bf16[128,1792]{1,0:T(8,128)(2,1)S(1)}, u32[]{:S(2)}, u32[]{:S(2)}) %collective-permute-start.25) | collective-permute-done | bytes 458784 | tf_op jit(solution)/shard_map/ppermute | solution.py:441
  110.1 6.5 %gate_up.1.refs_4_ = f32[2,256,1024]{2,1,0:T(8,128)S(1)} custom-call(bf16[128,1792]{1,0:T(8,128)(2,1)S(1)} %pad_maximum_fusion.3.refs_0_, bf16[128,1792]{1,0:T(8,128)(2,1)S(1)} %collective-permute-done.25.refs_1_, bf16[128,1792]{1,0:T(8,128)(2,1)S(1)} %pad_maximum_fusion.4.refs_2_, bf16[128,1792]{1,0:T(8,128)(2,1)S(1)} %collective-permute-done.27.refs_3_, ...), custom_call_target="tpu_custom_call" | custom-call | flops 3758096384 | bytes 16777216 | tf_op jit(solution)/shard_map/gate_up/pallas_call | solution.py:377
  116.6 17.6 %finish.1 = bf16[192,7168]{1,0:T(8,128)(2,1)} custom-call(s32[2]{0:T(128)S(1)} %pad_add_fusion.place_ref, bf16[128,1792]{1,0:T(8,128)(2,1)S(1)} %pad_maximum_fusion.1.refs_0_, bf16[128,1792]{1,0:T(8,128)(2,1)S(1)} %collective-permute-done.19.refs_1_, bf16[128,1920]{1,0:T(8,128)(2,1)S(1)} %pad_maximum_fusion.refs_2_, ...), custom_call_target="tpu_custom_call" | custom-call | flops 6576668672 | bytes 32112640 | tf_op jit(solution)/shard_map/finish/pallas_call | solution.py:406
  (83 shorter events, 21.4 us)
Async XLA Ops:
  2.6 22.8 %collective-permute-start.3 = (bf16[1,7168,512]{2,1,0:T(8,128)(2,1)}, bf16[1,7168,512]{2,1,0:T(8,128)(2,1)}, u32[]{:S(2)}, u32[]{:S(2)}) collective-permute-start(bf16[1,7168,512]{2,1,0:T(8,128)(2,1)} %refs_5_.1), channel_id=1, source_target_pairs={{0,16},{16,0},{1,17},{17,1},{2,18},{18,2},{3,19},{19,3},{4,20},{20... | collective-permute-start | bytes 22020104 | tf_op jit(solution)/shard_map/ppermute | solution.py:446
  2.9 26.8 %collective-permute-start.8 = (bf16[1,7168,512]{2,1,0:T(8,128)(2,1)}, bf16[1,7168,512]{2,1,0:T(8,128)(2,1)}, u32[]{:S(2)}, u32[]{:S(2)}) collective-permute-start(bf16[1,7168,512]{2,1,0:T(8,128)(2,1)} %refs_7_.1), channel_id=1, source_target_pairs={{0,16},{16,0},{1,17},{17,1},{2,18},{18,2},{3,19},{19,3},{4,20},{20... | collective-permute-start | bytes 22020104 | tf_op jit(solution)/shard_map/ppermute | solution.py:446
  10.1 13.7 %collective-permute-start.1 = (bf16[128,1792]{1,0:T(8,128)(2,1)S(1)}, bf16[128,1792]{1,0:T(8,128)(2,1)S(1)}, u32[]{:S(2)}, u32[]{:S(2)}) collective-permute-start(bf16[128,1792]{1,0:T(8,128)(2,1)S(1)} %get-tuple-element.34), channel_id=1, source_target_pairs={{0,1},{1,0},{2,3},{3,2},{4,5},{5,4},{6,7},{7,6},{8,9},{9,8},{10,11... | collective-permute-start | bytes 1376264 | tf_op jit(solution)/shard_map/ppermute | solution.py:441
  13.0 12.3 %collective-permute-start.2 = (bf16[128,1792]{1,0:T(8,128)(2,1)S(1)}, bf16[128,1792]{1,0:T(8,128)(2,1)S(1)}, u32[]{:S(2)}, u32[]{:S(2)}) collective-permute-start(bf16[128,1792]{1,0:T(8,128)(2,1)S(1)} %get-tuple-element.35), channel_id=1, source_target_pairs={{0,2},{1,3},{2,0},{3,1},{4,6},{5,7},{6,4},{7,5},{8,10},{9,11},{10,... | collective-permute-start | bytes 1376264 | tf_op jit(solution)/shard_map/ppermute | solution.py:441
  25.5 8.6 %collective-permute-start.7 = (bf16[64,1792]{1,0:T(8,128)(2,1)S(1)}, bf16[64,1792]{1,0:T(8,128)(2,1)S(1)}, u32[]{:S(2)}, u32[]{:S(2)}) collective-permute-start(bf16[64,1792]{1,0:T(8,128)(2,1)S(1)} %get-tuple-element.78), channel_id=1, source_target_pairs={{0,1},{1,0},{2,3},{3,2},{4,5},{5,4},{6,7},{7,6},{8,9},{9,8},{10,11... | collective-permute-start | bytes 688136 | tf_op jit(solution)/shard_map/ppermute | solution.py:441
  25.9 17.4 %collective-permute-start.4 = (bf16[128,1792]{1,0:T(8,128)(2,1)S(1)}, bf16[128,1792]{1,0:T(8,128)(2,1)S(1)}, u32[]{:S(2)}, u32[]{:S(2)}) collective-permute-start(bf16[128,1792]{1,0:T(8,128)(2,1)S(1)} %get-tuple-element.43), channel_id=1, source_target_pairs={{0,1},{1,0},{2,3},{3,2},{4,5},{5,4},{6,7},{7,6},{8,9},{9,8},{10,11... | collective-permute-start | bytes 1376264 | tf_op jit(solution)/shard_map/ppermute | solution.py:441
  27.5 15.8 %collective-permute-start.5 = (bf16[128,1792]{1,0:T(8,128)(2,1)S(1)}, bf16[128,1792]{1,0:T(8,128)(2,1)S(1)}, u32[]{:S(2)}, u32[]{:S(2)}) collective-permute-start(bf16[128,1792]{1,0:T(8,128)(2,1)S(1)} %get-tuple-element.44), channel_id=1, source_target_pairs={{0,2},{1,3},{2,0},{3,1},{4,6},{5,7},{6,4},{7,5},{8,10},{9,11},{10,... | collective-permute-start | bytes 1376264 | tf_op jit(solution)/shard_map/ppermute | solution.py:441
  29.2 14.1 %collective-permute-start.6 = (bf16[64,1792]{1,0:T(8,128)(2,1)S(1)}, bf16[64,1792]{1,0:T(8,128)(2,1)S(1)}, u32[]{:S(2)}, u32[]{:S(2)}) collective-permute-start(bf16[64,1792]{1,0:T(8,128)(2,1)S(1)} %get-tuple-element.80), channel_id=1, source_target_pairs={{0,2},{1,3},{2,0},{3,1},{4,6},{5,7},{6,4},{7,5},{8,10},{9,11},{10,... | collective-permute-start | bytes 688136 | tf_op jit(solution)/shard_map/ppermute | solution.py:441
  43.3 25.6 %collective-permute-start.15 = (bf16[1,512,7168]{2,1,0:T(8,128)(2,1)}, bf16[1,512,7168]{2,1,0:T(8,128)(2,1)}, u32[]{:S(2)}, u32[]{:S(2)}) collective-permute-start(bf16[1,512,7168]{2,1,0:T(8,128)(2,1)} %refs_9_.1), channel_id=1, source_target_pairs={{0,16},{16,0},{1,17},{17,1},{2,18},{18,2},{3,19},{19,3},{4,20},{20... | collective-permute-start | bytes 22020104 | tf_op jit(solution)/shard_map/ppermute | solution.py:446
  43.7 8.7 %collective-permute-start.12 = (bf16[64,1792]{1,0:T(8,128)(2,1)S(1)}, bf16[64,1792]{1,0:T(8,128)(2,1)S(1)}, u32[]{:S(2)}, u32[]{:S(2)}) collective-permute-start(bf16[64,1792]{1,0:T(8,128)(2,1)S(1)} %get-tuple-element.77), channel_id=1, source_target_pairs={{0,1},{1,0},{2,3},{3,2},{4,5},{5,4},{6,7},{7,6},{8,9},{9,8},{10,11... | collective-permute-start | bytes 688136 | tf_op jit(solution)/shard_map/ppermute | solution.py:441
  46.2 7.8 %collective-permute-start.9 = (bf16[32,3584]{1,0:T(8,128)(2,1)S(1)}, bf16[32,3584]{1,0:T(8,128)(2,1)S(1)}, u32[]{:S(2)}, u32[]{:S(2)}) collective-permute-start(bf16[32,3584]{1,0:T(8,128)(2,1)S(1)} %get-tuple-element.71), channel_id=1, source_target_pairs={{0,4},{1,5},{2,6},{3,7},{4,0},{5,1},{6,2},{7,3},{8,12},{9,13},{10,... | collective-permute-start | bytes 688136 | tf_op jit(solution)/shard_map/ppermute | solution.py:441
  52.5 9.4 %collective-permute-start.13 = (bf16[32,3584]{1,0:T(8,128)(2,1)S(1)}, bf16[32,3584]{1,0:T(8,128)(2,1)S(1)}, u32[]{:S(2)}, u32[]{:S(2)}) collective-permute-start(bf16[32,3584]{1,0:T(8,128)(2,1)S(1)} %get-tuple-element.73), channel_id=1, source_target_pairs={{0,4},{1,5},{2,6},{3,7},{4,0},{5,1},{6,2},{7,3},{8,12},{9,13},{10,... | collective-permute-start | bytes 688136 | tf_op jit(solution)/shard_map/ppermute | solution.py:441
  54.1 14.9 %collective-permute-start.10 = (bf16[16,3584]{1,0:T(8,128)(2,1)S(1)}, bf16[16,3584]{1,0:T(8,128)(2,1)S(1)}, u32[]{:S(2)}, u32[]{:S(2)}) collective-permute-start(bf16[16,3584]{1,0:T(8,128)(2,1)S(1)} %add_convert_fusion.16), channel_id=1, source_target_pairs={{0,8},{1,9},{2,10},{3,11},{4,12},{5,13},{6,14},{7,15},{8,0},{9,1},... | collective-permute-start | bytes 344072 | tf_op jit(solution)/shard_map/ppermute | solution.py:441
  70.1 9.6 %collective-permute-start.16 = (bf16[16,3712]{1,0:T(8,128)(2,1)S(1)}, bf16[16,3712]{1,0:T(8,128)(2,1)S(1)}, u32[]{:S(2)}, u32[]{:S(2)}) collective-permute-start(bf16[16,3712]{1,0:T(8,128)(2,1)S(1)} %concatenate.49), channel_id=1, source_target_pairs={{0,8},{1,9},{2,10},{3,11},{4,12},{5,13},{6,14},{7,15},{8,0},{9,1},... | collective-permute-start | bytes 356360 | tf_op jit(solution)/shard_map/ppermute | solution.py:441
  77.3 8.1 %collective-permute-start.23 = (bf16[32,3584]{1,0:T(8,128)(2,1)S(1)}, bf16[32,3584]{1,0:T(8,128)(2,1)S(1)}, u32[]{:S(2)}, u32[]{:S(2)}) collective-permute-start(bf16[32,3584]{1,0:T(8,128)(2,1)S(1)} %pad_maximum_fusion.11), channel_id=1, source_target_pairs={{0,4},{1,5},{2,6},{3,7},{4,0},{5,1},{6,2},{7,3},{8,12},{9,13},{10,... | collective-permute-start | bytes 688136 | tf_op jit(solution)/shard_map/ppermute | solution.py:441
  79.7 8.4 %collective-permute-start.17 = (bf16[32,3712]{1,0:T(8,128)(2,1)S(1)}, bf16[32,3712]{1,0:T(8,128)(2,1)S(1)}, u32[]{:S(2)}, u32[]{:S(2)}) collective-permute-start(bf16[32,3712]{1,0:T(8,128)(2,1)S(1)} %pad_maximum_fusion.7), channel_id=1, source_target_pairs={{0,4},{1,5},{2,6},{3,7},{4,0},{5,1},{6,2},{7,3},{8,12},{9,13},{10,... | collective-permute-start | bytes 712712 | tf_op jit(solution)/shard_map/ppermute | solution.py:441
  85.4 10.7 %collective-permute-start.26 = (bf16[64,1792]{1,0:T(8,128)(2,1)S(1)}, bf16[64,1792]{1,0:T(8,128)(2,1)S(1)}, u32[]{:S(2)}, u32[]{:S(2)}) collective-permute-start(bf16[64,1792]{1,0:T(8,128)(2,1)S(1)} %get-tuple-element.82), channel_id=1, source_target_pairs={{0,1},{1,0},{2,3},{3,2},{4,5},{5,4},{6,7},{7,6},{8,9},{9,8},{10,11... | collective-permute-start | bytes 688136 | tf_op jit(solution)/shard_map/ppermute | solution.py:441
  86.9 8.5 %collective-permute-start.24 = (bf16[64,1792]{1,0:T(8,128)(2,1)S(1)}, bf16[64,1792]{1,0:T(8,128)(2,1)S(1)}, u32[]{:S(2)}, u32[]{:S(2)}) collective-permute-start(bf16[64,1792]{1,0:T(8,128)(2,1)S(1)} %get-tuple-element.83), channel_id=1, source_target_pairs={{0,2},{1,3},{2,0},{3,1},{4,6},{5,7},{6,4},{7,5},{8,10},{9,11},{10,... | collective-permute-start | bytes 688136 | tf_op jit(solution)/shard_map/ppermute | solution.py:441
  88.1 12.2 %collective-permute-start.18 = (bf16[64,1792]{1,0:T(8,128)(2,1)S(1)}, bf16[64,1792]{1,0:T(8,128)(2,1)S(1)}, u32[]{:S(2)}, u32[]{:S(2)}) collective-permute-start(bf16[64,1792]{1,0:T(8,128)(2,1)S(1)} %pad_maximum_fusion.8), channel_id=1, source_target_pairs={{0,2},{1,3},{2,0},{3,1},{4,6},{5,7},{6,4},{7,5},{8,10},{9,11},{10,... | collective-permute-start | bytes 688136 | tf_op jit(solution)/shard_map/ppermute | solution.py:441
  89.2 11.9 %collective-permute-start.20 = (bf16[64,1920]{1,0:T(8,128)(2,1)S(1)}, bf16[64,1920]{1,0:T(8,128)(2,1)S(1)}, u32[]{:S(2)}, u32[]{:S(2)}) collective-permute-start(bf16[64,1920]{1,0:T(8,128)(2,1)S(1)} %pad_maximum_fusion.5), channel_id=1, source_target_pairs={{0,1},{1,0},{2,3},{3,2},{4,5},{5,4},{6,7},{7,6},{8,9},{9,8},{10,11... | collective-permute-start | bytes 737288 | tf_op jit(solution)/shard_map/ppermute | solution.py:441
  95.5 13.6 %collective-permute-start.25 = (bf16[128,1792]{1,0:T(8,128)(2,1)S(1)}, bf16[128,1792]{1,0:T(8,128)(2,1)S(1)}, u32[]{:S(2)}, u32[]{:S(2)}) collective-permute-start(bf16[128,1792]{1,0:T(8,128)(2,1)S(1)} %pad_maximum_fusion.3.refs_0_), channel_id=1, source_target_pairs={{0,1},{1,0},{2,3},{3,2},{4,5},{5,4},{6,7},{7,6},{8,9},{9,8},{10,11... | collective-permute-start | bytes 1376264 | tf_op jit(solution)/shard_map/ppermute | solution.py:441
  96.2 13.9 %collective-permute-start.27 = (bf16[128,1792]{1,0:T(8,128)(2,1)S(1)}, bf16[128,1792]{1,0:T(8,128)(2,1)S(1)}, u32[]{:S(2)}, u32[]{:S(2)}) collective-permute-start(bf16[128,1792]{1,0:T(8,128)(2,1)S(1)} %pad_maximum_fusion.4.refs_2_), channel_id=1, source_target_pairs={{0,2},{1,3},{2,0},{3,1},{4,6},{5,7},{6,4},{7,5},{8,10},{9,11},{10,... | collective-permute-start | bytes 1376264 | tf_op jit(solution)/shard_map/ppermute | solution.py:441
  100.4 16.2 %collective-permute-start.19 = (bf16[128,1792]{1,0:T(8,128)(2,1)S(1)}, bf16[128,1792]{1,0:T(8,128)(2,1)S(1)}, u32[]{:S(2)}, u32[]{:S(2)}) collective-permute-start(bf16[128,1792]{1,0:T(8,128)(2,1)S(1)} %pad_maximum_fusion.1.refs_0_), channel_id=1, source_target_pairs={{0,1},{1,0},{2,3},{3,2},{4,5},{5,4},{6,7},{7,6},{8,9},{9,8},{10,11... | collective-permute-start | bytes 1376264 | tf_op jit(solution)/shard_map/ppermute | solution.py:441
  101.1 15.5 %collective-permute-start.21 = (bf16[128,1920]{1,0:T(8,128)(2,1)S(1)}, bf16[128,1920]{1,0:T(8,128)(2,1)S(1)}, u32[]{:S(2)}, u32[]{:S(2)}) collective-permute-start(bf16[128,1920]{1,0:T(8,128)(2,1)S(1)} %pad_maximum_fusion.refs_2_), channel_id=1, source_target_pairs={{0,2},{1,3},{2,0},{3,1},{4,6},{5,7},{6,4},{7,5},{8,10},{9,11},{10,... | collective-permute-start | bytes 1474568 | tf_op jit(solution)/shard_map/ppermute | solution.py:441
  (8 other events, 178.8 us)

commit v4 on v3

--- a/solution.py
+++ b/solution.py
@@ -1,4 +1,5 @@
 import functools
+import math
 
 import jax
 import jax.numpy as jnp
@@ -11,6 +12,7 @@
 norm_epsilon = 1e-06
 masked_value = -1e30
 LANES = 128
+first_share = 12
 f32 = jnp.float32
 bf16 = jnp.bfloat16
 
@@ -120,15 +122,15 @@
     return LANES * max(t for t in range(1, tiles + 1) if tiles % t == 0 and t * LANES <= most)
 
 
-def project_specs(rows, inner, quarter, tile, chunk):
-    steps = quarter // tile
-    first = 2 * chunk * steps
+def project_specs(rows, inner, first, half):
+    tile = column_tile(math.gcd(first, half), 1024)
+    steps = half // tile
     weights = [
-        pl.BlockSpec((inner, tile), lambda i, first=first: (0, first + i)),
-        pl.BlockSpec((inner, tile), lambda i, first=first + steps: (0, first + i)),
+        pl.BlockSpec((inner, tile), lambda i, at=at: (0, at + i))
+        for at in (first // tile, first // tile + steps)
     ]
     outs = [pl.BlockSpec((rows // 2, tile), lambda i: (0, i))] * 4
-    shapes = [jax.ShapeDtypeStruct((rows // 2, quarter), bf16)] * 4
+    shapes = [jax.ShapeDtypeStruct((rows // 2, half), bf16)] * 4
     return steps, weights, outs, shapes
 
 
@@ -136,20 +138,17 @@
     return pl.BlockSpec(shape, lambda i: (0,) * len(shape))
 
 
-def attend_project(place, queries, keys, value_up, out_proj, block, orders):
+def attend_project(place, queries, keys, value_up, out_proj, half, block, orders):
     rows, _ = queries.shape
     heads, _, value_width = value_up.shape
     qk, slab = keys[0].shape
     slabs = len(keys)
     span = slab * slabs
-    inner, width = out_proj.shape
-    quarter = width // 4
-    steps, weights, outs, shapes = project_specs(
-        rows, inner, quarter, column_tile(quarter, 896), 0
-    )
+    inner = out_proj.shape[0]
+    steps, weights, outs, shapes = project_specs(rows, inner, 0, half)
     offsets = {(h * qk) % LANES for h in range(heads)}
     deep = max(-(-(o + qk) // LANES) * LANES for o in offsets)
-    flops = 2 * rows * (heads * span * 2 * qk + inner * (width // 2))
+    flops = 2 * rows * (heads * span * 2 * qk + inner * 2 * half)
     return pl.pallas_call(
         functools.partial(attend_kernel, slabs, block, orders),
         grid=(steps,),
@@ -169,20 +168,16 @@
         compiler_params=pltpu.CompilerParams(vmem_limit_bytes=24 << 20),
         cost_estimate=pl.CostEstimate(
             flops=flops,
-            bytes_accessed=inner * width + rows * width + queries.size * 2,
+            bytes_accessed=4 * (inner + rows) * half + queries.size * 2,
             transcendentals=rows * span * heads,
         ),
         name="attend_project",
     )(place, in_hbm(queries), in_hbm(keys[0]), *keys[1:], in_hbm(value_up), in_hbm(out_proj), in_hbm(out_proj))
 
 
-def project_more(hva, hvb, out_proj, chunk):
+def project_more(hva, hvb, out_proj, first, half):
     rows, inner = hva.shape
-    width = out_proj.shape[1]
-    quarter = width // 4
-    steps, weights, outs, shapes = project_specs(
-        rows, inner, quarter, column_tile(quarter, 896), chunk
-    )
+    steps, weights, outs, shapes = project_specs(rows, inner, first, half)
     return pl.pallas_call(
         project_kernel,
         grid=(steps,),
@@ -191,8 +186,8 @@
         out_shape=shapes,
         compiler_params=pltpu.CompilerParams(vmem_limit_bytes=16 << 20),
         cost_estimate=pl.CostEstimate(
-            flops=rows * inner * width,
-            bytes_accessed=inner * width + rows * width,
+            flops=4 * rows * inner * half,
+            bytes_accessed=4 * (inner + rows) * half,
             transcendentals=0,
         ),
         name="project_more",
@@ -221,35 +216,41 @@
     copies = []
     for p, w_ref in enumerate(pieces):
         cuts = (0, deep // 2, deep) if p == 0 else (0, deep)
-        copies.append(
-            [
-                (
-                    low,
-                    high,
-                    pltpu.make_async_copy(
-                        w_ref.at[0, first_row + low : first_row + high, :],
-                        held_ref.at[p, low:high, :],
-                        sems.at[p + (n if p == 0 else 1)],
-                    ),
-                )
-                for n, (low, high) in enumerate(zip(cuts, cuts[1:]))
-            ]
-        )
+        for n, (low, high) in enumerate(zip(cuts, cuts[1:])):
+            copy = pltpu.make_async_copy(
+                w_ref.at[0, first_row + low : first_row + high, :],
+                held_ref.at[p, low:high, :],
+                sems.at[p + (n if p == 0 else 1)],
+            )
+            copies.append((p, low, high, [copy]))
     return copies
 
 
-def start_all(copies):
-    for group in copies:
-        for _, _, copy in group:
+class Window:
+    def __init__(self, groups, ahead):
+        self.groups, self.ahead, self.used = groups, ahead, 0
+        for group in groups[:ahead]:
+            self.start(group)
+
+    def start(self, group):
+        for copy in group:
             copy.start()
 
-
-def times_piece(x_ref, held_ref, p, group):
+    def take(self):
+        for copy in self.groups[self.used]:
+            copy.wait()
+        if self.used + self.ahead < len(self.groups):
+            self.start(self.groups[self.used + self.ahead])
+        self.used += 1
+
+
+def times_piece(x_ref, held_ref, window, copies, piece):
     total = None
-    for low, high, copy in group:
-        copy.wait()
-        term = jnp.dot(x_ref[:, low:high], held_ref[p, low:high, :], preferred_element_type=f32)
-        total = term if total is None else total + term
+    for p, low, high, _ in copies:
+        if p == piece:
+            window.take()
+            term = jnp.dot(x_ref[:, low:high], held_ref[p, low:high, :], preferred_element_type=f32)
+            total = term if total is None else total + term
     return total
 
 
@@ -258,17 +259,17 @@
     pieces = refs[4 : 4 + 2 * slabs]
     acc_ref, x_ref, held_ref, sems = refs[4 + 2 * slabs :]
     copies = weight_copies(pieces, held_ref, sems, 0)
-    start_all(copies)
+    window = Window([c[3] for c in copies], 3)
     place_rows(quarter_rows, columns, a_refs, b_refs, x_ref)
     wide = held_ref.shape[2]
-    for p, group in enumerate(copies):
-        kind, place = divmod(p, slabs)
+    for p in range(len(pieces)):
+        place, kind = divmod(p, 2)
         acc_ref[kind, :, place * wide : (place + 1) * wide] = times_piece(
-            x_ref, held_ref, p, group
+            x_ref, held_ref, window, copies, p
         )
 
 
-def finish_kernel(slabs, quarter_rows, columns, block, order, top, senders, place_ref, *refs):
+def finish_kernel(slabs, quarter_rows, columns, first_row, block, order, top, senders, place_ref, *refs):
     a_refs, b_refs = refs[:2], refs[2:4]
     base_ref = refs[4]
     pieces = refs[5 : 5 + 2 * slabs]
@@ -283,8 +284,7 @@
     wide = held_ref.shape[2]
     tiles = down_sems.shape[0]
     tile = width // tiles
-    copies = weight_copies(pieces, held_ref, sems, 2 * columns)
-    start_all(copies)
+    copies = weight_copies(pieces, held_ref, sems, first_row)
     down_copies = [
         [
             pltpu.make_async_copy(
@@ -296,9 +296,7 @@
         ]
         for j in range(tiles)
     ]
-    for group in down_copies:
-        for copy in group:
-            copy.start()
+    window = Window([c[3] for c in copies] + down_copies, 3)
     place_rows(quarter_rows, columns, a_refs, b_refs, x_ref)
 
     me = place_ref[1]
@@ -337,8 +335,9 @@
         cols = slice(place * wide, (place + 1) * wide)
         both = []
         for kind in range(2):
-            p = kind * slabs + place
-            total = base_ref[kind, :, cols] + times_piece(x_ref, held_ref, p, copies[p])
+            total = base_ref[kind, :, cols] + times_piece(
+                x_ref, held_ref, window, copies, 2 * place + kind
+            )
             if kind == 0:
                 acc_ref[:, cols] = total
             both.append(total)
@@ -347,10 +346,9 @@
         act_ref[:, cols] = jnp.dot(select, act, preferred_element_type=f32).astype(bf16)
 
     out_copies = []
-    for j, group in enumerate(down_copies):
+    for j in range(tiles):
         cols = slice(j * tile, (j + 1) * tile)
-        for copy in group:
-            copy.wait()
+        window.take()
         total = jnp.dot(act_ref[...], down_ref[:, cols], preferred_element_type=f32)
         out_ref[:, cols] = (total * slot_gate).astype(bf16)
         copy = pltpu.make_async_copy(out_ref.at[:, cols], out_hbm.at[:, cols], out_sems.at[j])
@@ -371,7 +369,7 @@
 def gate_up(a, b, gates, ups):
     half, columns = a[0].shape
     rows = 2 * half
-    pieces = gates + ups
+    pieces = [w for pair in zip(gates, ups) for w in pair]
     wide = pieces[0].shape[2]
     hidden = wide * len(gates)
     return pl.pallas_call(
@@ -394,10 +392,10 @@
     )(*a, *b, *map(in_hbm, pieces))
 
 
-def finish(place, a, b, base, gates, ups, downs, block, order, top, senders, capacity):
+def finish(place, a, b, base, gates, ups, downs, first_row, block, order, top, senders, capacity):
     half, columns = a[0].shape
     rows = 2 * half
-    pieces = gates + ups
+    pieces = [w for pair in zip(gates, ups) for w in pair]
     wide = pieces[0].shape[2]
     hidden = wide * len(gates)
     width = downs[0].shape[2]
@@ -405,7 +403,7 @@
     slots = senders * capacity
     return pl.pallas_call(
         functools.partial(
-            finish_kernel, len(gates), rows // 4, columns, block, order, top, senders
+            finish_kernel, len(gates), rows // 4, columns, first_row, block, order, top, senders
         ),
         in_specs=[pl.BlockSpec(memory_space=pltpu.SMEM)]
         + [in_vmem()] * 5
@@ -501,6 +499,9 @@
     expert_count = senders * w_gate.shape[0]
     capacity = max(2, 3 * block * top // (2 * expert_count))
     orders = (list(range(bits)), [1, 0, *range(2, bits)])
+    tiles = width // (2 * LANES)
+    low = LANES * (tiles * first_share // 28)
+    halves = (low, LANES * tiles - low)
     place = jnp.stack([lax.axis_index("ctx"), lax.axis_index("exp")]).astype(jnp.int32)
 
     keys = shifted(latent.T, slabs)
@@ -510,9 +511,9 @@
     up_others = shifted(up_source, slabs)[1:]
 
     hva, hvb, *parts = attend_project(
-        place, queries, keys, value_up, out_proj, block, orders
+        place, queries, keys, value_up, out_proj, halves[0], block, orders
     )
-    more = project_more(hva, hvb, out_proj, 1)
+    more = project_more(hva, hvb, out_proj, 2 * halves[0], halves[1])
     got = first_swap(parts, senders)
     got, more, gate_others = tie(got, more, gate_others)
     terms = [second_swap(parts, got, senders)]
@@ -525,11 +526,10 @@
     gate_parts = [w_gate, *gate_others]
     up_parts = [w_up, *up_others]
     down_parts = [w_down, *down_others]
-    half_width = width // 2
     gain = norm_gain.astype(f32)
     hidden, payload, squares = [], [], 0.0
     for c, (keep, got) in enumerate(sums):
-        cols = slice(c * half_width, (c + 1) * half_width)
+        cols = slice(2 * halves[0] * c, 2 * (halves[0] + halves[1] * c))
         rows = (residual[:, cols].astype(f32) + (keep.astype(f32) + got.astype(f32))).astype(bf16)
         wide = rows.astype(f32)
         squares = squares + jnp.sum(wide * wide, axis=1, keepdims=True)
@@ -549,11 +549,11 @@
     )
     payload[1] = jnp.concatenate([payload[1], meta], axis=1)
 
-    a, b = gather_rows(payload[0], half_width // 2, senders, bits)
+    a, b = gather_rows(payload[0], halves[0], senders, bits)
     base = gate_up(a, b, gate_parts, up_parts)
-    a, b = gather_rows(payload[1], half_width // 2, senders, bits)
+    a, b = gather_rows(payload[1], halves[1], senders, bits)
     slots = finish(
-        place, a, b, base, gate_parts, up_parts, down_parts, block, orders[0], top, senders, capacity
+        place, a, b, base, gate_parts, up_parts, down_parts, 2 * halves[0], block, orders[0], top, senders, capacity
     )
     expert_out = slots.reshape(capacity, senders, width).transpose(1, 0, 2)[None, None]
     return jnp.concatenate(hidden, axis=1), expert_out

time: 135 us -> 125 us (0.926)
  waiting for transfers between devices: 65.2 us -> 51.6 us
  starting transfers between devices: 30.9 us -> 39.5 us
  Pallas kernels: 34.4 us -> 30.1 us
    ppermute x24, waiting for transfers between devices: 63.7 us -> 50.2 us  [swap(): return lax.ppermute(value, 'exp', [(i, i ^ 1 << bit) for i in range(count)])]
    ppermute x24, starting transfers between devices: 29.9 us -> 38.4 us  [swap(): return lax.ppermute(value, 'exp', [(i, i ^ 1 << bit) for i in range(count)])]
    pallas_call x1, Pallas kernels: 17.6 us -> 14.2 us  [finish(): pl.pallas_call(functools.partial(finish_kernel, len(gates), rows // 4, co...]
  transfers between devices with their start and end apart: 28 -> 28, of which waited for: 15 -> 18; matrix products, arithmetic and copies ran while one was open for 2% -> 2% of each run, Pallas kernels for 13% -> 13%
where the time goes in v4:
time: 125 us
  waiting for transfers between devices  51.6 us (41%)
  starting transfers between devices  39.5 us (32%)
  Pallas kernels  30.1 us (24%)
  other arithmetic  2.24 us (2%)
    ppermute x24, waiting for transfers between devices, swap(): return lax.ppermute(value, 'exp', [(i, i ^ 1 << bit) for i in range(count)])  50.2 us
    ppermute x24, starting transfers between devices, swap(): return lax.ppermute(value, 'exp', [(i, i ^ 1 << bit) for i in range(count)])  38.4 us
    pallas_call x1, Pallas kernels, finish(): pl.pallas_call(functools.partial(finish_kernel, len(gates), rows // 4, co...  14.2 us
    pallas_call x1, Pallas kernels, attend_project(): pl.pallas_call(functools.partial(attend_kernel, slabs, block, orders), gr...  6.54 us
    pallas_call x1, Pallas kernels, gate_up(): pl.pallas_call(functools.partial(gate_up_kernel, len(gates), rows // 4, c...  5.97 us
    pallas_call x1, Pallas kernels, project_more(): pl.pallas_call(project_kernel, grid=(steps,), in_specs=[whole(hva.shape),...  3.42 us
  transfers between devices with their start and end apart: 28, of which 18 were waited for; matrix products, arithmetic and copies ran while one was open for 2% of the time, Pallas kernels for 13%

profile of v4, /device:TPU:0, one launch (start us, length us, event | category | flops | bytes accessed | tf_op | source)
XLA Modules:
  0.0 125.1 jit_solution(2698712089251314094)
XLA Ops:
  3.2 6.5 %attend_project.1 = (bf16[256,512]{1,0:T(8,128)(2,1)S(1)}, bf16[256,512]{1,0:T(8,128)(2,1)S(1)}, bf16[128,1536]{1,0:T(8,128)(2,1)S(1)}, bf16[128,1536]{1,0:T(8,1...) custom-call(s32[2]{0:T(128)S(1)} %pad_add_fusion.place_ref, bf16[256,2304]{1,0:T(8,128)(2,1)} %q_ref.1, ...), custom_call_target="tpu_custom_call" | custom-call | flops 2013265920 | bytes 5898240 | tf_op jit(solution)/shard_map/attend_project/pallas_call | solution.py:152
  9.7 2.9 %collective-permute-start.1 = (bf16[128,1536]{1,0:T(8,128)(2,1)S(1)}, bf16[128,1536]{1,0:T(8,128)(2,1)S(1)}, u32[]{:S(2)}, u32[]{:S(2)}) collective-permute-start(bf16[128,1536]{1,0:T(8,128)(2,1)S(1)} %get-tuple-element.34), channel_id=1, source_target_pairs={{0,1},{1,0},{2,3},{3,2},{4,5},{5,4},{6,7},{7,6},{8,9},{9,8},{10,11... | collective-permute-start | bytes 1179656 | tf_op jit(solution)/shard_map/ppermute | solution.py:439
  14.2 3.4 %project_more.1 = (bf16[128,2048]{1,0:T(8,128)(2,1)S(1)}, bf16[128,2048]{1,0:T(8,128)(2,1)S(1)}, bf16[128,2048]{1,0:T(8,128)(2,1)S(1)}, bf16[128,2048]{1,0:T(8,128)(2,1)S(1)}) custom-call(bf16[256,512]{1,0:T(8,128)(2,1)S(1)} %get-tuple-element.36.hva_ref, bf16[256,512]{1,0:T(8,128)(2,1)S(1)} %get-tuple-element.37.hvb_ref, bf16[512,7168]{1,0:T(8,128)(2,1)} %wb_ref.1, ...), custom_call_target="tpu_custom_call" | custom-call | flops 1073741824 | bytes 6291456 | tf_op jit(solution)/shard_map/project_more/pallas_call | solution.py:181
  17.6 4.4 %collective-permute-done.1 = bf16[128,1536]{1,0:T(8,128)(2,1)S(1)} collective-permute-done((bf16[128,1536]{1,0:T(8,128)(2,1)S(1)}, bf16[128,1536]{1,0:T(8,128)(2,1)S(1)}, u32[]{:S(2)}, u32[]{:S(2)}) %collective-permute-start.1) | collective-permute-done | bytes 393248 | tf_op jit(solution)/shard_map/ppermute | solution.py:439
  24.0 1.7 %collective-permute-start.4 = (bf16[128,2048]{1,0:T(8,128)(2,1)S(1)}, bf16[128,2048]{1,0:T(8,128)(2,1)S(1)}, u32[]{:S(2)}, u32[]{:S(2)}) collective-permute-start(bf16[128,2048]{1,0:T(8,128)(2,1)S(1)} %get-tuple-element.43), channel_id=1, source_target_pairs={{0,1},{1,0},{2,3},{3,2},{4,5},{5,4},{6,7},{7,6},{8,9},{9,8},{10,11... | collective-permute-start | bytes 1572872 | tf_op jit(solution)/shard_map/ppermute | solution.py:439
  27.9 3.6 %collective-permute-done.7 = bf16[64,1536]{1,0:T(8,128)(2,1)S(1)} collective-permute-done((bf16[64,1536]{1,0:T(8,128)(2,1)S(1)}, bf16[64,1536]{1,0:T(8,128)(2,1)S(1)}, u32[]{:S(2)}, u32[]{:S(2)}) %collective-permute-start.7) | collective-permute-done | bytes 196640 | tf_op jit(solution)/shard_map/ppermute | solution.py:439
  31.5 10.7 %collective-permute-done.6 = bf16[64,1536]{1,0:T(8,128)(2,1)S(1)} collective-permute-done((bf16[64,1536]{1,0:T(8,128)(2,1)S(1)}, bf16[64,1536]{1,0:T(8,128)(2,1)S(1)}, u32[]{:S(2)}, u32[]{:S(2)}) %collective-permute-start.6) | collective-permute-done | bytes 196640 | tf_op jit(solution)/shard_map/ppermute | solution.py:439
  43.5 1.5 %collective-permute-start.9 = (bf16[32,3072]{1,0:T(8,128)(2,1)S(1)}, bf16[32,3072]{1,0:T(8,128)(2,1)S(1)}, u32[]{:S(2)}, u32[]{:S(2)}) collective-permute-start(bf16[32,3072]{1,0:T(8,128)(2,1)S(1)} %get-tuple-element.77), channel_id=1, source_target_pairs={{0,4},{1,5},{2,6},{3,7},{4,0},{5,1},{6,2},{7,3},{8,12},{9,13},{10,... | collective-permute-start | bytes 589832 | tf_op jit(solution)/shard_map/ppermute | solution.py:439
  45.2 1.6 %collective-permute-start.11 = (bf16[64,2048]{1,0:T(8,128)(2,1)S(1)}, bf16[64,2048]{1,0:T(8,128)(2,1)S(1)}, u32[]{:S(2)}, u32[]{:S(2)}) collective-permute-start(bf16[64,2048]{1,0:T(8,128)(2,1)S(1)} %get-tuple-element.73), channel_id=1, source_target_pairs={{0,2},{1,3},{2,0},{3,1},{4,6},{5,7},{6,4},{7,5},{8,10},{9,11},{10,... | collective-permute-start | bytes 786440 | tf_op jit(solution)/shard_map/ppermute | solution.py:439
  46.8 3.8 %collective-permute-done.9 = bf16[32,3072]{1,0:T(8,128)(2,1)S(1)} collective-permute-done((bf16[32,3072]{1,0:T(8,128)(2,1)S(1)}, bf16[32,3072]{1,0:T(8,128)(2,1)S(1)}, u32[]{:S(2)}, u32[]{:S(2)}) %collective-permute-start.9) | collective-permute-done | bytes 196640 | tf_op jit(solution)/shard_map/ppermute | solution.py:439
  50.6 2.6 %collective-permute-start.10 = (bf16[16,3072]{1,0:T(8,128)(2,1)S(1)}, bf16[16,3072]{1,0:T(8,128)(2,1)S(1)}, u32[]{:S(2)}, u32[]{:S(2)}) collective-permute-start(bf16[16,3072]{1,0:T(8,128)(2,1)S(1)} %add_convert_fusion.16), channel_id=1, source_target_pairs={{0,8},{1,9},{2,10},{3,11},{4,12},{5,13},{6,14},{7,15},{8,0},{9,1},... | collective-permute-start | bytes 294920 | tf_op jit(solution)/shard_map/ppermute | solution.py:439
  55.0 2.8 %collective-permute-done.10 = bf16[16,3072]{1,0:T(8,128)(2,1)S(1)} collective-permute-done((bf16[16,3072]{1,0:T(8,128)(2,1)S(1)}, bf16[16,3072]{1,0:T(8,128)(2,1)S(1)}, u32[]{:S(2)}, u32[]{:S(2)}) %collective-permute-start.10) | collective-permute-done | bytes 98336 | tf_op jit(solution)/shard_map/ppermute | solution.py:439
  57.9 2.0 %collective-permute-start.22 = (bf16[16,3072]{1,0:T(8,128)(2,1)S(1)}, bf16[16,3072]{1,0:T(8,128)(2,1)S(1)}, u32[]{:S(2)}, u32[]{:S(2)}) collective-permute-start(bf16[16,3072]{1,0:T(8,128)(2,1)S(1)} %get-tuple-element.64), channel_id=1, source_target_pairs={{0,8},{1,9},{2,10},{3,11},{4,12},{5,13},{6,14},{7,15},{8,0},{9,1},... | collective-permute-start | bytes 294920 | tf_op jit(solution)/shard_map/ppermute | solution.py:439
  60.0 4.1 %collective-permute-done.22 = bf16[16,3072]{1,0:T(8,128)(2,1)S(1)} collective-permute-done((bf16[16,3072]{1,0:T(8,128)(2,1)S(1)}, bf16[16,3072]{1,0:T(8,128)(2,1)S(1)}, u32[]{:S(2)}, u32[]{:S(2)}) %collective-permute-start.22) | collective-permute-done | bytes 98336 | tf_op jit(solution)/shard_map/ppermute | solution.py:439
  64.1 1.7 %collective-permute-start.23 = (bf16[32,3072]{1,0:T(8,128)(2,1)S(1)}, bf16[32,3072]{1,0:T(8,128)(2,1)S(1)}, u32[]{:S(2)}, u32[]{:S(2)}) collective-permute-start(bf16[32,3072]{1,0:T(8,128)(2,1)S(1)} %pad_maximum_fusion.11), channel_id=1, source_target_pairs={{0,4},{1,5},{2,6},{3,7},{4,0},{5,1},{6,2},{7,3},{8,12},{9,13},{10,... | collective-permute-start | bytes 589832 | tf_op jit(solution)/shard_map/ppermute | solution.py:439
  65.8 3.2 %collective-permute-start.14 = (bf16[16,4096]{1,0:T(8,128)(2,1)S(1)}, bf16[16,4096]{1,0:T(8,128)(2,1)S(1)}, u32[]{:S(2)}, u32[]{:S(2)}) collective-permute-start(bf16[16,4096]{1,0:T(8,128)(2,1)S(1)} %get-tuple-element.82), channel_id=1, source_target_pairs={{0,8},{1,9},{2,10},{3,11},{4,12},{5,13},{6,14},{7,15},{8,0},{9,1},... | collective-permute-start | bytes 393224 | tf_op jit(solution)/shard_map/ppermute | solution.py:439
  69.1 2.8 %collective-permute-done.23 = bf16[32,3072]{1,0:T(8,128)(2,1)S(1)} collective-permute-done((bf16[32,3072]{1,0:T(8,128)(2,1)S(1)}, bf16[32,3072]{1,0:T(8,128)(2,1)S(1)}, u32[]{:S(2)}, u32[]{:S(2)}) %collective-permute-start.23) | collective-permute-done | bytes 196640 | tf_op jit(solution)/shard_map/ppermute | solution.py:439
  73.2 2.6 %collective-permute-start.16 = (bf16[16,4224]{1,0:T(8,128)(2,1)S(1)}, bf16[16,4224]{1,0:T(8,128)(2,1)S(1)}, u32[]{:S(2)}, u32[]{:S(2)}) collective-permute-start(bf16[16,4224]{1,0:T(8,128)(2,1)S(1)} %concatenate.49), channel_id=1, source_target_pairs={{0,8},{1,9},{2,10},{3,11},{4,12},{5,13},{6,14},{7,15},{8,0},{9,1},... | collective-permute-start | bytes 405512 | tf_op jit(solution)/shard_map/ppermute | solution.py:439
  79.1 2.3 %collective-permute-start.17 = (bf16[32,4224]{1,0:T(8,128)(2,1)S(1)}, bf16[32,4224]{1,0:T(8,128)(2,1)S(1)}, u32[]{:S(2)}, u32[]{:S(2)}) collective-permute-start(bf16[32,4224]{1,0:T(8,128)(2,1)S(1)} %pad_maximum_fusion.7), channel_id=1, source_target_pairs={{0,4},{1,5},{2,6},{3,7},{4,0},{5,1},{6,2},{7,3},{8,12},{9,13},{10,... | collective-permute-start | bytes 811016 | tf_op jit(solution)/shard_map/ppermute | solution.py:439
  81.5 1.9 %collective-permute-done.24 = bf16[64,1536]{1,0:T(8,128)(2,1)S(1)} collective-permute-done((bf16[64,1536]{1,0:T(8,128)(2,1)S(1)}, bf16[64,1536]{1,0:T(8,128)(2,1)S(1)}, u32[]{:S(2)}, u32[]{:S(2)}) %collective-permute-start.24) | collective-permute-done | bytes 196640 | tf_op jit(solution)/shard_map/ppermute | solution.py:439
  88.9 5.0 %collective-permute-done.25.refs_1_ = bf16[128,1536]{1,0:T(8,128)(2,1)S(1)} collective-permute-done((bf16[128,1536]{1,0:T(8,128)(2,1)S(1)}, bf16[128,1536]{1,0:T(8,128)(2,1)S(1)}, u32[]{:S(2)}, u32[]{:S(2)}) %collective-permute-start.25) | collective-permute-done | bytes 393248 | tf_op jit(solution)/shard_map/ppermute | solution.py:439
  94.2 6.0 %gate_up.1.refs_4_ = f32[2,256,1024]{2,1,0:T(8,128)S(1)} custom-call(bf16[128,1536]{1,0:T(8,128)(2,1)S(1)} %pad_maximum_fusion.3.refs_0_, bf16[128,1536]{1,0:T(8,128)(2,1)S(1)} %collective-permute-done.25.refs_1_, bf16[128,1536]{1,0:T(8,128)(2,1)S(1)} %pad_maximum_fusion.4.refs_2_, bf16[128,1536]{1,0:T(8,128)(2,1)S(1)} %collective-permute-done.27.refs_3_, ...), custom_call_target="tpu_custom_call" | custom-call | flops 3221225472 | bytes 14680064 | tf_op jit(solution)/shard_map/gate_up/pallas_call | solution.py:375
  103.3 6.1 %collective-permute-done.19.refs_1_ = bf16[128,2048]{1,0:T(8,128)(2,1)S(1)} collective-permute-done((bf16[128,2048]{1,0:T(8,128)(2,1)S(1)}, bf16[128,2048]{1,0:T(8,128)(2,1)S(1)}, u32[]{:S(2)}, u32[]{:S(2)}) %collective-permute-start.19) | collective-permute-done | bytes 524320 | tf_op jit(solution)/shard_map/ppermute | solution.py:439
  110.7 14.2 %finish.1 = bf16[192,7168]{1,0:T(8,128)(2,1)} custom-call(s32[2]{0:T(128)S(1)} %pad_add_fusion.place_ref, bf16[128,2048]{1,0:T(8,128)(2,1)S(1)} %pad_maximum_fusion.1.refs_0_, bf16[128,2048]{1,0:T(8,128)(2,1)S(1)} %collective-permute-done.19.refs_1_, bf16[128,2176]{1,0:T(8,128)(2,1)S(1)} %pad_maximum_fusion.refs_2_, ...), custom_call_target="tpu_custom_call" | custom-call | flops 7113539584 | bytes 34209792 | tf_op jit(solution)/shard_map/finish/pallas_call | solution.py:404
  (85 shorter events, 26.6 us)
Async XLA Ops:
  2.6 20.9 %collective-permute-start.3 = (bf16[1,7168,512]{2,1,0:T(8,128)(2,1)}, bf16[1,7168,512]{2,1,0:T(8,128)(2,1)}, u32[]{:S(2)}, u32[]{:S(2)}) collective-permute-start(bf16[1,7168,512]{2,1,0:T(8,128)(2,1)} %refs_5_.3), channel_id=1, source_target_pairs={{0,16},{16,0},{1,17},{17,1},{2,18},{18,2},{3,19},{19,3},{4,20},{20... | collective-permute-start | bytes 22020104 | tf_op jit(solution)/shard_map/ppermute | solution.py:444
  2.9 24.9 %collective-permute-start.8 = (bf16[1,7168,512]{2,1,0:T(8,128)(2,1)}, bf16[1,7168,512]{2,1,0:T(8,128)(2,1)}, u32[]{:S(2)}, u32[]{:S(2)}) collective-permute-start(bf16[1,7168,512]{2,1,0:T(8,128)(2,1)} %refs_6_.1), channel_id=1, source_target_pairs={{0,16},{16,0},{1,17},{17,1},{2,18},{18,2},{3,19},{19,3},{4,20},{20... | collective-permute-start | bytes 22020104 | tf_op jit(solution)/shard_map/ppermute | solution.py:444
  9.7 12.3 %collective-permute-start.1 = (bf16[128,1536]{1,0:T(8,128)(2,1)S(1)}, bf16[128,1536]{1,0:T(8,128)(2,1)S(1)}, u32[]{:S(2)}, u32[]{:S(2)}) collective-permute-start(bf16[128,1536]{1,0:T(8,128)(2,1)S(1)} %get-tuple-element.34), channel_id=1, source_target_pairs={{0,1},{1,0},{2,3},{3,2},{4,5},{5,4},{6,7},{7,6},{8,9},{9,8},{10,11... | collective-permute-start | bytes 1179656 | tf_op jit(solution)/shard_map/ppermute | solution.py:439
  12.6 10.9 %collective-permute-start.2 = (bf16[128,1536]{1,0:T(8,128)(2,1)S(1)}, bf16[128,1536]{1,0:T(8,128)(2,1)S(1)}, u32[]{:S(2)}, u32[]{:S(2)}) collective-permute-start(bf16[128,1536]{1,0:T(8,128)(2,1)S(1)} %get-tuple-element.35), channel_id=1, source_target_pairs={{0,2},{1,3},{2,0},{3,1},{4,6},{5,7},{6,4},{7,5},{8,10},{9,11},{10,... | collective-permute-start | bytes 1179656 | tf_op jit(solution)/shard_map/ppermute | solution.py:439
  23.6 7.9 %collective-permute-start.7 = (bf16[64,1536]{1,0:T(8,128)(2,1)S(1)}, bf16[64,1536]{1,0:T(8,128)(2,1)S(1)}, u32[]{:S(2)}, u32[]{:S(2)}) collective-permute-start(bf16[64,1536]{1,0:T(8,128)(2,1)S(1)} %get-tuple-element.78), channel_id=1, source_target_pairs={{0,1},{1,0},{2,3},{3,2},{4,5},{5,4},{6,7},{7,6},{8,9},{9,8},{10,11... | collective-permute-start | bytes 589832 | tf_op jit(solution)/shard_map/ppermute | solution.py:439
  24.0 18.1 %collective-permute-start.4 = (bf16[128,2048]{1,0:T(8,128)(2,1)S(1)}, bf16[128,2048]{1,0:T(8,128)(2,1)S(1)}, u32[]{:S(2)}, u32[]{:S(2)}) collective-permute-start(bf16[128,2048]{1,0:T(8,128)(2,1)S(1)} %get-tuple-element.43), channel_id=1, source_target_pairs={{0,1},{1,0},{2,3},{3,2},{4,5},{5,4},{6,7},{7,6},{8,9},{9,8},{10,11... | collective-permute-start | bytes 1572872 | tf_op jit(solution)/shard_map/ppermute | solution.py:439
  25.7 16.5 %collective-permute-start.5 = (bf16[128,2048]{1,0:T(8,128)(2,1)S(1)}, bf16[128,2048]{1,0:T(8,128)(2,1)S(1)}, u32[]{:S(2)}, u32[]{:S(2)}) collective-permute-start(bf16[128,2048]{1,0:T(8,128)(2,1)S(1)} %get-tuple-element.44), channel_id=1, source_target_pairs={{0,2},{1,3},{2,0},{3,1},{4,6},{5,7},{6,4},{7,5},{8,10},{9,11},{10,... | collective-permute-start | bytes 1572872 | tf_op jit(solution)/shard_map/ppermute | solution.py:439
  27.3 14.9 %collective-permute-start.6 = (bf16[64,1536]{1,0:T(8,128)(2,1)S(1)}, bf16[64,1536]{1,0:T(8,128)(2,1)S(1)}, u32[]{:S(2)}, u32[]{:S(2)}) collective-permute-start(bf16[64,1536]{1,0:T(8,128)(2,1)S(1)} %get-tuple-element.80), channel_id=1, source_target_pairs={{0,2},{1,3},{2,0},{3,1},{4,6},{5,7},{6,4},{7,5},{8,10},{9,11},{10,... | collective-permute-start | bytes 589832 | tf_op jit(solution)/shard_map/ppermute | solution.py:439
  42.2 30.5 %collective-permute-start.15 = (bf16[1,512,7168]{2,1,0:T(8,128)(2,1)}, bf16[1,512,7168]{2,1,0:T(8,128)(2,1)}, u32[]{:S(2)}, u32[]{:S(2)}) collective-permute-start(bf16[1,512,7168]{2,1,0:T(8,128)(2,1)} %refs_9_.1), channel_id=1, source_target_pairs={{0,16},{16,0},{1,17},{17,1},{2,18},{18,2},{3,19},{19,3},{4,20},{20... | collective-permute-start | bytes 22020104 | tf_op jit(solution)/shard_map/ppermute | solution.py:444
  42.6 10.8 %collective-permute-start.12 = (bf16[64,2048]{1,0:T(8,128)(2,1)S(1)}, bf16[64,2048]{1,0:T(8,128)(2,1)S(1)}, u32[]{:S(2)}, u32[]{:S(2)}) collective-permute-start(bf16[64,2048]{1,0:T(8,128)(2,1)S(1)} %get-tuple-element.75), channel_id=1, source_target_pairs={{0,1},{1,0},{2,3},{3,2},{4,5},{5,4},{6,7},{7,6},{8,9},{9,8},{10,11... | collective-permute-start | bytes 786440 | tf_op jit(solution)/shard_map/ppermute | solution.py:439
  43.5 7.1 %collective-permute-start.9 = (bf16[32,3072]{1,0:T(8,128)(2,1)S(1)}, bf16[32,3072]{1,0:T(8,128)(2,1)S(1)}, u32[]{:S(2)}, u32[]{:S(2)}) collective-permute-start(bf16[32,3072]{1,0:T(8,128)(2,1)S(1)} %get-tuple-element.77), channel_id=1, source_target_pairs={{0,4},{1,5},{2,6},{3,7},{4,0},{5,1},{6,2},{7,3},{8,12},{9,13},{10,... | collective-permute-start | bytes 589832 | tf_op jit(solution)/shard_map/ppermute | solution.py:439
  45.2 8.2 %collective-permute-start.11 = (bf16[64,2048]{1,0:T(8,128)(2,1)S(1)}, bf16[64,2048]{1,0:T(8,128)(2,1)S(1)}, u32[]{:S(2)}, u32[]{:S(2)}) collective-permute-start(bf16[64,2048]{1,0:T(8,128)(2,1)S(1)} %get-tuple-element.73), channel_id=1, source_target_pairs={{0,2},{1,3},{2,0},{3,1},{4,6},{5,7},{6,4},{7,5},{8,10},{9,11},{10,... | collective-permute-start | bytes 786440 | tf_op jit(solution)/shard_map/ppermute | solution.py:439
  50.6 7.3 %collective-permute-start.10 = (bf16[16,3072]{1,0:T(8,128)(2,1)S(1)}, bf16[16,3072]{1,0:T(8,128)(2,1)S(1)}, u32[]{:S(2)}, u32[]{:S(2)}) collective-permute-start(bf16[16,3072]{1,0:T(8,128)(2,1)S(1)} %add_convert_fusion.16), channel_id=1, source_target_pairs={{0,8},{1,9},{2,10},{3,11},{4,12},{5,13},{6,14},{7,15},{8,0},{9,1},... | collective-permute-start | bytes 294920 | tf_op jit(solution)/shard_map/ppermute | solution.py:439
  53.5 12.2 %collective-permute-start.13 = (bf16[32,4096]{1,0:T(8,128)(2,1)S(1)}, bf16[32,4096]{1,0:T(8,128)(2,1)S(1)}, u32[]{:S(2)}, u32[]{:S(2)}) collective-permute-start(bf16[32,4096]{1,0:T(8,128)(2,1)S(1)} %get-tuple-element.71), channel_id=1, source_target_pairs={{0,4},{1,5},{2,6},{3,7},{4,0},{5,1},{6,2},{7,3},{8,12},{9,13},{10,... | collective-permute-start | bytes 786440 | tf_op jit(solution)/shard_map/ppermute | solution.py:439
  64.1 7.7 %collective-permute-start.23 = (bf16[32,3072]{1,0:T(8,128)(2,1)S(1)}, bf16[32,3072]{1,0:T(8,128)(2,1)S(1)}, u32[]{:S(2)}, u32[]{:S(2)}) collective-permute-start(bf16[32,3072]{1,0:T(8,128)(2,1)S(1)} %pad_maximum_fusion.11), channel_id=1, source_target_pairs={{0,4},{1,5},{2,6},{3,7},{4,0},{5,1},{6,2},{7,3},{8,12},{9,13},{10,... | collective-permute-start | bytes 589832 | tf_op jit(solution)/shard_map/ppermute | solution.py:439
  65.8 6.8 %collective-permute-start.14 = (bf16[16,4096]{1,0:T(8,128)(2,1)S(1)}, bf16[16,4096]{1,0:T(8,128)(2,1)S(1)}, u32[]{:S(2)}, u32[]{:S(2)}) collective-permute-start(bf16[16,4096]{1,0:T(8,128)(2,1)S(1)} %get-tuple-element.82), channel_id=1, source_target_pairs={{0,8},{1,9},{2,10},{3,11},{4,12},{5,13},{6,14},{7,15},{8,0},{9,1},... | collective-permute-start | bytes 393224 | tf_op jit(solution)/shard_map/ppermute | solution.py:439
  75.8 7.9 %collective-permute-start.26 = (bf16[64,1536]{1,0:T(8,128)(2,1)S(1)}, bf16[64,1536]{1,0:T(8,128)(2,1)S(1)}, u32[]{:S(2)}, u32[]{:S(2)}) collective-permute-start(bf16[64,1536]{1,0:T(8,128)(2,1)S(1)} %get-tuple-element.84), channel_id=1, source_target_pairs={{0,1},{1,0},{2,3},{3,2},{4,5},{5,4},{6,7},{7,6},{8,9},{9,8},{10,11... | collective-permute-start | bytes 589832 | tf_op jit(solution)/shard_map/ppermute | solution.py:439
  79.1 6.8 %collective-permute-start.17 = (bf16[32,4224]{1,0:T(8,128)(2,1)S(1)}, bf16[32,4224]{1,0:T(8,128)(2,1)S(1)}, u32[]{:S(2)}, u32[]{:S(2)}) collective-permute-start(bf16[32,4224]{1,0:T(8,128)(2,1)S(1)} %pad_maximum_fusion.7), channel_id=1, source_target_pairs={{0,4},{1,5},{2,6},{3,7},{4,0},{5,1},{6,2},{7,3},{8,12},{9,13},{10,... | collective-permute-start | bytes 811016 | tf_op jit(solution)/shard_map/ppermute | solution.py:439
  83.4 10.5 %collective-permute-start.25 = (bf16[128,1536]{1,0:T(8,128)(2,1)S(1)}, bf16[128,1536]{1,0:T(8,128)(2,1)S(1)}, u32[]{:S(2)}, u32[]{:S(2)}) collective-permute-start(bf16[128,1536]{1,0:T(8,128)(2,1)S(1)} %pad_maximum_fusion.3.refs_0_), channel_id=1, source_target_pairs={{0,1},{1,0},{2,3},{3,2},{4,5},{5,4},{6,7},{7,6},{8,9},{9,8},{10,11... | collective-permute-start | bytes 1179656 | tf_op jit(solution)/shard_map/ppermute | solution.py:439
  83.7 10.5 %collective-permute-start.27 = (bf16[128,1536]{1,0:T(8,128)(2,1)S(1)}, bf16[128,1536]{1,0:T(8,128)(2,1)S(1)}, u32[]{:S(2)}, u32[]{:S(2)}) collective-permute-start(bf16[128,1536]{1,0:T(8,128)(2,1)S(1)} %pad_maximum_fusion.4.refs_2_), channel_id=1, source_target_pairs={{0,2},{1,3},{2,0},{3,1},{4,6},{5,7},{6,4},{7,5},{8,10},{9,11},{10,... | collective-permute-start | bytes 1179656 | tf_op jit(solution)/shard_map/ppermute | solution.py:439
  85.9 14.2 %collective-permute-start.18 = (bf16[64,2048]{1,0:T(8,128)(2,1)S(1)}, bf16[64,2048]{1,0:T(8,128)(2,1)S(1)}, u32[]{:S(2)}, u32[]{:S(2)}) collective-permute-start(bf16[64,2048]{1,0:T(8,128)(2,1)S(1)} %pad_maximum_fusion.8), channel_id=1, source_target_pairs={{0,2},{1,3},{2,0},{3,1},{4,6},{5,7},{6,4},{7,5},{8,10},{9,11},{10,... | collective-permute-start | bytes 786440 | tf_op jit(solution)/shard_map/ppermute | solution.py:439
  87.4 13.7 %collective-permute-start.20 = (bf16[64,2176]{1,0:T(8,128)(2,1)S(1)}, bf16[64,2176]{1,0:T(8,128)(2,1)S(1)}, u32[]{:S(2)}, u32[]{:S(2)}) collective-permute-start(bf16[64,2176]{1,0:T(8,128)(2,1)S(1)} %pad_maximum_fusion.5), channel_id=1, source_target_pairs={{0,1},{1,0},{2,3},{3,2},{4,5},{5,4},{6,7},{7,6},{8,9},{9,8},{10,11... | collective-permute-start | bytes 835592 | tf_op jit(solution)/shard_map/ppermute | solution.py:439
  100.2 9.2 %collective-permute-start.19 = (bf16[128,2048]{1,0:T(8,128)(2,1)S(1)}, bf16[128,2048]{1,0:T(8,128)(2,1)S(1)}, u32[]{:S(2)}, u32[]{:S(2)}) collective-permute-start(bf16[128,2048]{1,0:T(8,128)(2,1)S(1)} %pad_maximum_fusion.1.refs_0_), channel_id=1, source_target_pairs={{0,1},{1,0},{2,3},{3,2},{4,5},{5,4},{6,7},{7,6},{8,9},{9,8},{10,11... | collective-permute-start | bytes 1572872 | tf_op jit(solution)/shard_map/ppermute | solution.py:439
  101.1 9.6 %collective-permute-start.21 = (bf16[128,2176]{1,0:T(8,128)(2,1)S(1)}, bf16[128,2176]{1,0:T(8,128)(2,1)S(1)}, u32[]{:S(2)}, u32[]{:S(2)}) collective-permute-start(bf16[128,2176]{1,0:T(8,128)(2,1)S(1)} %pad_maximum_fusion.refs_2_), channel_id=1, source_target_pairs={{0,2},{1,3},{2,0},{3,1},{4,6},{5,7},{6,4},{7,5},{8,10},{9,11},{10,... | collective-permute-start | bytes 1671176 | tf_op jit(solution)/shard_map/ppermute | solution.py:439
  (8 other events, 144.7 us)

commit v5 on v4

--- a/solution.py
+++ b/solution.py
@@ -12,7 +12,7 @@
 norm_epsilon = 1e-06
 masked_value = -1e30
 LANES = 128
-first_share = 12
+first_share = 16
 f32 = jnp.float32
 bf16 = jnp.bfloat16
 
@@ -467,25 +467,32 @@
     return keep_a, keep_b, got_a2, got_b2
 
 
-def last_swaps(terms, count, bits):
+def joined(terms):
     keep_a, keep_b, got_a, got_b = terms
-    keep = jnp.concatenate([keep_a, keep_b], axis=1)
-    got = jnp.concatenate([got_a, got_b], axis=1)
-    for bit in range(2, bits):
-        half = keep.shape[0] // 2
-        arrived = swap(add(keep[half:], got[half:]), bit, count)
-        keep, got = add(keep[:half], got[:half]), arrived
-    return keep, got
-
-
-def gather_rows(rows, split, count, bits):
-    for bit in range(bits - 1, 1, -1):
-        rows = jnp.concatenate([rows, swap(rows, bit, count)], axis=0)
-    out = []
-    for part, (first, second) in ((rows[:, :split], (1, 0)), (rows[:, split:], (0, 1))):
-        low = jnp.concatenate([part, swap(part, first, count)], axis=0)
-        out.append([low, swap(low, second, count)])
-    return out
+    return (
+        jnp.concatenate([keep_a, keep_b], axis=1),
+        jnp.concatenate([got_a, got_b], axis=1),
+    )
+
+
+def halve(terms, bit, count):
+    keep, got = terms
+    half = keep.shape[0] // 2
+    arrived = swap(add(keep[half:], got[half:]), bit, count)
+    return add(keep[:half], got[:half]), arrived
+
+
+def double(rows, bit, count):
+    return jnp.concatenate([rows, swap(rows, bit, count)], axis=0)
+
+
+def gather_half(rows, split, count):
+    return double(rows[:, :split], 1, count), double(rows[:, split:], 0, count)
+
+
+def gather_last(low, count):
+    low_a, low_b = low
+    return [low_a, swap(low_a, 0, count)], [low_b, swap(low_b, 1, count)]
 
 
 def body(
@@ -514,28 +521,43 @@
         place, queries, keys, value_up, out_proj, halves[0], block, orders
     )
     more = project_more(hva, hvb, out_proj, 2 * halves[0], halves[1])
-    got = first_swap(parts, senders)
-    got, more, gate_others = tie(got, more, gate_others)
-    terms = [second_swap(parts, got, senders)]
-    got = first_swap(more, senders)
-    got, terms[0], up_others, down_source = tie(got, terms[0], up_others, w_down)
-    down_others = shifted(down_source, slabs)[1:]
-    terms.append(second_swap(more, got, senders))
-    sums = [last_swaps(t, senders, bits) for t in terms]
-    sums[1], down_others = tie(sums[1], down_others)
-    gate_parts = [w_gate, *gate_others]
-    up_parts = [w_up, *up_others]
-    down_parts = [w_down, *down_others]
     gain = norm_gain.astype(f32)
-    hidden, payload, squares = [], [], 0.0
-    for c, (keep, got) in enumerate(sums):
+    inner_bits = list(range(2, bits))
+
+    def finished(terms, c):
+        keep, got = terms
         cols = slice(2 * halves[0] * c, 2 * (halves[0] + halves[1] * c))
         rows = (residual[:, cols].astype(f32) + (keep.astype(f32) + got.astype(f32))).astype(bf16)
         wide = rows.astype(f32)
-        squares = squares + jnp.sum(wide * wide, axis=1, keepdims=True)
-        hidden.append(rows)
-        payload.append((wide * gain[None, cols]).astype(bf16))
-    inverse = lax.rsqrt(squares / width + norm_epsilon)
+        return (
+            rows,
+            (wide * gain[None, cols]).astype(bf16),
+            jnp.sum(wide * wide, axis=1, keepdims=True),
+        )
+
+    got = first_swap(parts, senders)
+    got, more, gate_others = tie(got, more, gate_others)
+    terms = second_swap(parts, got, senders)
+    got = first_swap(more, senders)
+    ahead, rest = joined(terms), inner_bits[:-1]
+    for bit in rest:
+        ahead = halve(ahead, bit, senders)
+    got, _, up_others, down_source = tie(got, ahead, up_others, w_down)
+    down_others = shifted(down_source, slabs)[1:]
+
+    behind = second_swap(more, got, senders)
+    ahead = halve(ahead, inner_bits[-1], senders)
+    hidden_0, payload, squares_0 = finished(ahead, 0)
+    behind = joined(behind)
+    for bit in inner_bits[:-1]:
+        behind = halve(behind, bit, senders)
+    payload = double(payload, inner_bits[-1], senders)
+    behind = halve(behind, inner_bits[-1], senders)
+    for bit in inner_bits[-2::-1]:
+        payload = double(payload, bit, senders)
+    behind, down_others = tie(behind, down_others)
+    hidden_1, rows, squares_1 = finished(behind, 1)
+    inverse = lax.rsqrt((squares_0 + squares_1) / width + norm_epsilon)
     coarse = lax.reduce_precision(inverse, 8, 7)
     meta = jnp.concatenate(
         [
@@ -547,16 +569,24 @@
         ],
         axis=1,
     )
-    payload[1] = jnp.concatenate([payload[1], meta], axis=1)
-
-    a, b = gather_rows(payload[0], halves[0], senders, bits)
+    rows = jnp.concatenate([rows, meta], axis=1)
+
+    gate_parts = [w_gate, *gate_others]
+    up_parts = [w_up, *up_others]
+    down_parts = [w_down, *down_others]
+    low = gather_half(payload, halves[0], senders)
+    for bit in inner_bits[::-1]:
+        rows = double(rows, bit, senders)
+    a, b = gather_last(low, senders)
+    low = gather_half(rows, halves[1], senders)
+    a, b, low = tie(a, b, low)
     base = gate_up(a, b, gate_parts, up_parts)
-    a, b = gather_rows(payload[1], halves[1], senders, bits)
+    a, b = gather_last(low, senders)
     slots = finish(
         place, a, b, base, gate_parts, up_parts, down_parts, 2 * halves[0], block, orders[0], top, senders, capacity
     )
     expert_out = slots.reshape(capacity, senders, width).transpose(1, 0, 2)[None, None]
-    return jnp.concatenate(hidden, axis=1), expert_out
+    return jnp.concatenate([hidden_0, hidden_1], axis=1), expert_out
 
 
 def solution(mesh):

time: 125 us -> 122 us (0.976)
  starting transfers between devices: 39.5 us -> 30.7 us
  waiting for transfers between devices: 51.6 us -> 56.8 us
    ppermute x24, starting transfers between devices: 38.4 us -> 29.6 us  [swap(): return lax.ppermute(value, 'exp', [(i, i ^ 1 << bit) for i in range(count)])]
    ppermute x24, waiting for transfers between devices: 50.2 us -> 55.3 us  [swap(): return lax.ppermute(value, 'exp', [(i, i ^ 1 << bit) for i in range(count)])]
    pallas_call x1, Pallas kernels: 14.2 us -> 12.7 us  [finish(): pl.pallas_call(functools.partial(finish_kernel, len(gates), rows // 4, co...]
    pallas_call x1, Pallas kernels: 5.97 us -> 7.41 us  [gate_up(): pl.pallas_call(functools.partial(gate_up_kernel, len(gates), rows // 4, c...]
  transfers between devices with their start and end apart: 28 -> 28, of which waited for: 18 -> 15; matrix products, arithmetic and copies ran while one was open for 2% -> 2% of each run, Pallas kernels for 13% -> 15%
where the time goes in v5:
time: 122 us
  waiting for transfers between devices  56.8 us (47%)
  Pallas kernels  30.8 us (25%)
  starting transfers between devices  30.7 us (25%)
  other arithmetic  2.19 us (2%)
    ppermute x24, waiting for transfers between devices, swap(): return lax.ppermute(value, 'exp', [(i, i ^ 1 << bit) for i in range(count)])  55.3 us
    ppermute x24, starting transfers between devices, swap(): return lax.ppermute(value, 'exp', [(i, i ^ 1 << bit) for i in range(count)])  29.6 us
    pallas_call x1, Pallas kernels, finish(): pl.pallas_call(functools.partial(finish_kernel, len(gates), rows // 4, co...  12.7 us
    pallas_call x1, Pallas kernels, gate_up(): pl.pallas_call(functools.partial(gate_up_kernel, len(gates), rows // 4, c...  7.41 us
    pallas_call x1, Pallas kernels, attend_project(): pl.pallas_call(functools.partial(attend_kernel, slabs, block, orders), gr...  7.03 us
    pallas_call x1, Pallas kernels, project_more(): pl.pallas_call(project_kernel, grid=(steps,), in_specs=[whole(hva.shape),...  3.63 us
  transfers between devices with their start and end apart: 28, of which 15 were waited for; matrix products, arithmetic and copies ran while one was open for 2% of the time, Pallas kernels for 15%

profile of v5, /device:TPU:0, one launch (start us, length us, event | category | flops | bytes accessed | tf_op | source)
XLA Modules:
  0.0 122.0 jit_solution(16939072973312467519)
XLA Ops:
  3.2 7.0 %attend_project.1 = (bf16[256,512]{1,0:T(8,128)(2,1)S(1)}, bf16[256,512]{1,0:T(8,128)(2,1)S(1)}, bf16[128,2048]{1,0:T(8,128)(2,1)S(1)}, bf16[128,2048]{1,0:T(8,1...) custom-call(s32[2]{0:T(128)S(1)} %pad_add_fusion.place_ref, bf16[256,2304]{1,0:T(8,128)(2,1)} %q_ref.1, ...), custom_call_target="tpu_custom_call" | custom-call | flops 2281701376 | bytes 7471104 | tf_op jit(solution)/shard_map/attend_project/pallas_call | solution.py:152
  10.2 2.9 %collective-permute-start.1 = (bf16[128,2048]{1,0:T(8,128)(2,1)S(1)}, bf16[128,2048]{1,0:T(8,128)(2,1)S(1)}, u32[]{:S(2)}, u32[]{:S(2)}) collective-permute-start(bf16[128,2048]{1,0:T(8,128)(2,1)S(1)} %get-tuple-element.37), channel_id=1, source_target_pairs={{0,1},{1,0},{2,3},{3,2},{4,5},{5,4},{6,7},{7,6},{8,9},{9,8},{10,11... | collective-permute-start | bytes 1572872 | tf_op jit(solution)/shard_map/ppermute | solution.py:439
  14.6 3.6 %project_more.1 = (bf16[128,1536]{1,0:T(8,128)(2,1)S(1)}, bf16[128,1536]{1,0:T(8,128)(2,1)S(1)}, bf16[128,1536]{1,0:T(8,128)(2,1)S(1)}, bf16[128,1536]{1,0:T(8,128)(2,1)S(1)}) custom-call(bf16[256,512]{1,0:T(8,128)(2,1)S(1)} %get-tuple-element.39.hva_ref, bf16[256,512]{1,0:T(8,128)(2,1)S(1)} %get-tuple-element.40.hvb_ref, bf16[512,7168]{1,0:T(8,128)(2,1)} %wb_ref.1, ...), custom_call_target="tpu_custom_call" | custom-call | flops 805306368 | bytes 4718592 | tf_op jit(solution)/shard_map/project_more/pallas_call | solution.py:181
  18.3 7.0 %collective-permute-done.1 = bf16[128,2048]{1,0:T(8,128)(2,1)S(1)} collective-permute-done((bf16[128,2048]{1,0:T(8,128)(2,1)S(1)}, bf16[128,2048]{1,0:T(8,128)(2,1)S(1)}, u32[]{:S(2)}, u32[]{:S(2)}) %collective-permute-start.1) | collective-permute-done | bytes 524320 | tf_op jit(solution)/shard_map/ppermute | solution.py:439
  26.9 1.6 %collective-permute-start.4 = (bf16[64,2048]{1,0:T(8,128)(2,1)S(1)}, bf16[64,2048]{1,0:T(8,128)(2,1)S(1)}, u32[]{:S(2)}, u32[]{:S(2)}) collective-permute-start(bf16[64,2048]{1,0:T(8,128)(2,1)S(1)} %get-tuple-element.78), channel_id=1, source_target_pairs={{0,2},{1,3},{2,0},{3,1},{4,6},{5,7},{6,4},{7,5},{8,10},{9,11},{10,... | collective-permute-start | bytes 786440 | tf_op jit(solution)/shard_map/ppermute | solution.py:439
  31.3 5.0 %collective-permute-done.4 = bf16[64,2048]{1,0:T(8,128)(2,1)S(1)} collective-permute-done((bf16[64,2048]{1,0:T(8,128)(2,1)S(1)}, bf16[64,2048]{1,0:T(8,128)(2,1)S(1)}, u32[]{:S(2)}, u32[]{:S(2)}) %collective-permute-start.4) | collective-permute-done | bytes 262176 | tf_op jit(solution)/shard_map/ppermute | solution.py:439
  36.3 1.7 %collective-permute-done.5 = bf16[64,2048]{1,0:T(8,128)(2,1)S(1)} collective-permute-done((bf16[64,2048]{1,0:T(8,128)(2,1)S(1)}, bf16[64,2048]{1,0:T(8,128)(2,1)S(1)}, u32[]{:S(2)}, u32[]{:S(2)}) %collective-permute-start.5) | collective-permute-done | bytes 262176 | tf_op jit(solution)/shard_map/ppermute | solution.py:439
  38.1 1.6 %collective-permute-start.6 = (bf16[32,4096]{1,0:T(8,128)(2,1)S(1)}, bf16[32,4096]{1,0:T(8,128)(2,1)S(1)}, u32[]{:S(2)}, u32[]{:S(2)}) collective-permute-start(bf16[32,4096]{1,0:T(8,128)(2,1)S(1)} %get-tuple-element.74), channel_id=1, source_target_pairs={{0,4},{1,5},{2,6},{3,7},{4,0},{5,1},{6,2},{7,3},{8,12},{9,13},{10,... | collective-permute-start | bytes 786440 | tf_op jit(solution)/shard_map/ppermute | solution.py:439
  39.8 4.3 %collective-permute-done.8 = bf16[128,1536]{1,0:T(8,128)(2,1)S(1)} collective-permute-done((bf16[128,1536]{1,0:T(8,128)(2,1)S(1)}, bf16[128,1536]{1,0:T(8,128)(2,1)S(1)}, u32[]{:S(2)}, u32[]{:S(2)}) %collective-permute-start.8) | collective-permute-done | bytes 393248 | tf_op jit(solution)/shard_map/ppermute | solution.py:439
  44.8 2.7 %collective-permute-start.7 = (bf16[16,4096]{1,0:T(8,128)(2,1)S(1)}, bf16[16,4096]{1,0:T(8,128)(2,1)S(1)}, u32[]{:S(2)}, u32[]{:S(2)}) collective-permute-start(bf16[16,4096]{1,0:T(8,128)(2,1)S(1)} %add_convert_fusion.13), channel_id=1, source_target_pairs={{0,8},{1,9},{2,10},{3,11},{4,12},{5,13},{6,14},{7,15},{8,0},{9,1},... | collective-permute-start | bytes 393224 | tf_op jit(solution)/shard_map/ppermute | solution.py:439
  48.8 5.7 %collective-permute-done.7 = bf16[16,4096]{1,0:T(8,128)(2,1)S(1)} collective-permute-done((bf16[16,4096]{1,0:T(8,128)(2,1)S(1)}, bf16[16,4096]{1,0:T(8,128)(2,1)S(1)}, u32[]{:S(2)}, u32[]{:S(2)}) %collective-permute-start.7) | collective-permute-done | bytes 131104 | tf_op jit(solution)/shard_map/ppermute | solution.py:439
  55.2 3.8 %collective-permute-start.13 = (bf16[32,3072]{1,0:T(8,128)(2,1)S(1)}, bf16[32,3072]{1,0:T(8,128)(2,1)S(1)}, u32[]{:S(2)}, u32[]{:S(2)}) collective-permute-start(bf16[32,3072]{1,0:T(8,128)(2,1)S(1)} %get-tuple-element.81), channel_id=1, source_target_pairs={{0,4},{1,5},{2,6},{3,7},{4,0},{5,1},{6,2},{7,3},{8,12},{9,13},{10,... | collective-permute-start | bytes 589832 | tf_op jit(solution)/shard_map/ppermute | solution.py:439
  59.1 4.7 %collective-permute-done.16 = bf16[16,4096]{1,0:T(8,128)(2,1)S(1)} collective-permute-done((bf16[16,4096]{1,0:T(8,128)(2,1)S(1)}, bf16[16,4096]{1,0:T(8,128)(2,1)S(1)}, u32[]{:S(2)}, u32[]{:S(2)}) %collective-permute-start.16) | collective-permute-done | bytes 131104 | tf_op jit(solution)/shard_map/ppermute | solution.py:439
  63.8 2.1 %collective-permute-done.13 = bf16[32,3072]{1,0:T(8,128)(2,1)S(1)} collective-permute-done((bf16[32,3072]{1,0:T(8,128)(2,1)S(1)}, bf16[32,3072]{1,0:T(8,128)(2,1)S(1)}, u32[]{:S(2)}, u32[]{:S(2)}) %collective-permute-start.13) | collective-permute-done | bytes 196640 | tf_op jit(solution)/shard_map/ppermute | solution.py:439
  66.0 1.5 %collective-permute-start.14 = (bf16[16,3072]{1,0:T(8,128)(2,1)S(1)}, bf16[16,3072]{1,0:T(8,128)(2,1)S(1)}, u32[]{:S(2)}, u32[]{:S(2)}) collective-permute-start(bf16[16,3072]{1,0:T(8,128)(2,1)S(1)} %get-tuple-element.88), channel_id=1, source_target_pairs={{0,8},{1,9},{2,10},{3,11},{4,12},{5,13},{6,14},{7,15},{8,0},{9,1},... | collective-permute-start | bytes 294920 | tf_op jit(solution)/shard_map/ppermute | solution.py:439
  67.5 5.6 %collective-permute-done.17 = bf16[32,4096]{1,0:T(8,128)(2,1)S(1)} collective-permute-done((bf16[32,4096]{1,0:T(8,128)(2,1)S(1)}, bf16[32,4096]{1,0:T(8,128)(2,1)S(1)}, u32[]{:S(2)}, u32[]{:S(2)}) %collective-permute-start.17) | collective-permute-done | bytes 262176 | tf_op jit(solution)/shard_map/ppermute | solution.py:439
  75.3 4.9 %collective-permute-done.18 = bf16[64,2048]{1,0:T(8,128)(2,1)S(1)} collective-permute-done((bf16[64,2048]{1,0:T(8,128)(2,1)S(1)}, bf16[64,2048]{1,0:T(8,128)(2,1)S(1)}, u32[]{:S(2)}, u32[]{:S(2)}) %collective-permute-start.18) | collective-permute-done | bytes 262176 | tf_op jit(solution)/shard_map/ppermute | solution.py:439
  80.3 1.6 %collective-permute-start.19 = (bf16[128,2048]{1,0:T(8,128)(2,1)S(1)}, bf16[128,2048]{1,0:T(8,128)(2,1)S(1)}, u32[]{:S(2)}, u32[]{:S(2)}) collective-permute-start(bf16[128,2048]{1,0:T(8,128)(2,1)S(1)} %pad_maximum_fusion.1.refs_0_), channel_id=1, source_target_pairs={{0,1},{1,0},{2,3},{3,2},{4,5},{5,4},{6,7},{7,6},{8,9},{9,8},{10,11... | collective-permute-start | bytes 1572872 | tf_op jit(solution)/shard_map/ppermute | solution.py:439
  83.2 4.4 %collective-permute-done.23 = bf16[32,3200]{1,0:T(8,128)(2,1)S(1)} collective-permute-done((bf16[32,3200]{1,0:T(8,128)(2,1)S(1)}, bf16[32,3200]{1,0:T(8,128)(2,1)S(1)}, u32[]{:S(2)}, u32[]{:S(2)}) %collective-permute-start.23) | collective-permute-done | bytes 204832 | tf_op jit(solution)/shard_map/ppermute | solution.py:439
  89.0 1.5 %collective-permute-start.25 = (bf16[64,1664]{1,0:T(8,128)(2,1)S(1)}, bf16[64,1664]{1,0:T(8,128)(2,1)S(1)}, u32[]{:S(2)}, u32[]{:S(2)}) collective-permute-start(bf16[64,1664]{1,0:T(8,128)(2,1)S(1)} %pad_maximum_fusion.8), channel_id=1, source_target_pairs={{0,1},{1,0},{2,3},{3,2},{4,5},{5,4},{6,7},{7,6},{8,9},{9,8},{10,11... | collective-permute-start | bytes 638984 | tf_op jit(solution)/shard_map/ppermute | solution.py:439
  90.5 7.7 %collective-permute-done.24 = bf16[64,1536]{1,0:T(8,128)(2,1)S(1)} collective-permute-done((bf16[64,1536]{1,0:T(8,128)(2,1)S(1)}, bf16[64,1536]{1,0:T(8,128)(2,1)S(1)}, u32[]{:S(2)}, u32[]{:S(2)}) %collective-permute-start.24) | collective-permute-done | bytes 196640 | tf_op jit(solution)/shard_map/ppermute | solution.py:439
  100.1 1.6 %collective-permute-start.26 = (bf16[128,1536]{1,0:T(8,128)(2,1)S(1)}, bf16[128,1536]{1,0:T(8,128)(2,1)S(1)}, u32[]{:S(2)}, u32[]{:S(2)}) collective-permute-start(bf16[128,1536]{1,0:T(8,128)(2,1)S(1)} %pad_maximum_fusion.4.refs_0_), channel_id=1, source_target_pairs={{0,1},{1,0},{2,3},{3,2},{4,5},{5,4},{6,7},{7,6},{8,9},{9,8},{10,11... | collective-permute-start | bytes 1179656 | tf_op jit(solution)/shard_map/ppermute | solution.py:439
  101.7 7.4 %gate_up.1.refs_4_ = f32[2,256,1024]{2,1,0:T(8,128)S(1)} custom-call(bf16[128,2048]{1,0:T(8,128)(2,1)S(1)} %pad_maximum_fusion.1.refs_0_, bf16[128,2048]{1,0:T(8,128)(2,1)S(1)} %collective-permute-done.19.refs_1_, bf16[128,2048]{1,0:T(8,128)(2,1)S(1)} %pad_maximum_fusion.2.refs_2_, bf16[128,2048]{1,0:T(8,128)(2,1)S(1)} %collective-permute-done.21.refs_3_, ...), custom_call_target="tpu_custom_call" | custom-call | flops 4294967296 | bytes 18874368 | tf_op jit(solution)/shard_map/gate_up/pallas_call | solution.py:375
  109.2 12.7 %finish.1 = bf16[192,7168]{1,0:T(8,128)(2,1)} custom-call(s32[2]{0:T(128)S(1)} %pad_add_fusion.place_ref, bf16[128,1536]{1,0:T(8,128)(2,1)S(1)} %pad_maximum_fusion.4.refs_0_, bf16[128,1536]{1,0:T(8,128)(2,1)S(1)} %collective-permute-done.26.refs_1_, bf16[128,1664]{1,0:T(8,128)(2,1)S(1)} %pad_maximum_fusion.3.refs_2_, ...), custom_call_target="tpu_custom_call" | custom-call | flops 6039797760 | bytes 30015488 | tf_op jit(solution)/shard_map/finish/pallas_call | solution.py:404
  (84 shorter events, 18.3 us)
Async XLA Ops:
  2.6 24.2 %collective-permute-start.3 = (bf16[1,7168,512]{2,1,0:T(8,128)(2,1)}, bf16[1,7168,512]{2,1,0:T(8,128)(2,1)}, u32[]{:S(2)}, u32[]{:S(2)}) collective-permute-start(bf16[1,7168,512]{2,1,0:T(8,128)(2,1)} %refs_5_.3), channel_id=1, source_target_pairs={{0,16},{16,0},{1,17},{17,1},{2,18},{18,2},{3,19},{19,3},{4,20},{20... | collective-permute-start | bytes 22020104 | tf_op jit(solution)/shard_map/ppermute | solution.py:444
  2.9 36.8 %collective-permute-start.10 = (bf16[1,7168,512]{2,1,0:T(8,128)(2,1)}, bf16[1,7168,512]{2,1,0:T(8,128)(2,1)}, u32[]{:S(2)}, u32[]{:S(2)}) collective-permute-start(bf16[1,7168,512]{2,1,0:T(8,128)(2,1)} %refs_6_.1), channel_id=1, source_target_pairs={{0,16},{16,0},{1,17},{17,1},{2,18},{18,2},{3,19},{19,3},{4,20},{20... | collective-permute-start | bytes 22020104 | tf_op jit(solution)/shard_map/ppermute | solution.py:444
  10.2 15.1 %collective-permute-start.1 = (bf16[128,2048]{1,0:T(8,128)(2,1)S(1)}, bf16[128,2048]{1,0:T(8,128)(2,1)S(1)}, u32[]{:S(2)}, u32[]{:S(2)}) collective-permute-start(bf16[128,2048]{1,0:T(8,128)(2,1)S(1)} %get-tuple-element.37), channel_id=1, source_target_pairs={{0,1},{1,0},{2,3},{3,2},{4,5},{5,4},{6,7},{7,6},{8,9},{9,8},{10,11... | collective-permute-start | bytes 1572872 | tf_op jit(solution)/shard_map/ppermute | solution.py:439
  13.1 13.7 %collective-permute-start.2 = (bf16[128,2048]{1,0:T(8,128)(2,1)S(1)}, bf16[128,2048]{1,0:T(8,128)(2,1)S(1)}, u32[]{:S(2)}, u32[]{:S(2)}) collective-permute-start(bf16[128,2048]{1,0:T(8,128)(2,1)S(1)} %get-tuple-element.38), channel_id=1, source_target_pairs={{0,2},{1,3},{2,0},{3,1},{4,6},{5,7},{6,4},{7,5},{8,10},{9,11},{10,... | collective-permute-start | bytes 1572872 | tf_op jit(solution)/shard_map/ppermute | solution.py:439
  26.9 9.3 %collective-permute-start.4 = (bf16[64,2048]{1,0:T(8,128)(2,1)S(1)}, bf16[64,2048]{1,0:T(8,128)(2,1)S(1)}, u32[]{:S(2)}, u32[]{:S(2)}) collective-permute-start(bf16[64,2048]{1,0:T(8,128)(2,1)S(1)} %get-tuple-element.78), channel_id=1, source_target_pairs={{0,2},{1,3},{2,0},{3,1},{4,6},{5,7},{6,4},{7,5},{8,10},{9,11},{10,... | collective-permute-start | bytes 786440 | tf_op jit(solution)/shard_map/ppermute | solution.py:439
  28.7 9.3 %collective-permute-start.5 = (bf16[64,2048]{1,0:T(8,128)(2,1)S(1)}, bf16[64,2048]{1,0:T(8,128)(2,1)S(1)}, u32[]{:S(2)}, u32[]{:S(2)}) collective-permute-start(bf16[64,2048]{1,0:T(8,128)(2,1)S(1)} %get-tuple-element.76), channel_id=1, source_target_pairs={{0,1},{1,0},{2,3},{3,2},{4,5},{5,4},{6,7},{7,6},{8,9},{9,8},{10,11... | collective-permute-start | bytes 786440 | tf_op jit(solution)/shard_map/ppermute | solution.py:439
  29.3 14.8 %collective-permute-start.8 = (bf16[128,1536]{1,0:T(8,128)(2,1)S(1)}, bf16[128,1536]{1,0:T(8,128)(2,1)S(1)}, u32[]{:S(2)}, u32[]{:S(2)}) collective-permute-start(bf16[128,1536]{1,0:T(8,128)(2,1)S(1)} %get-tuple-element.50), channel_id=1, source_target_pairs={{0,1},{1,0},{2,3},{3,2},{4,5},{5,4},{6,7},{7,6},{8,9},{9,8},{10,11... | collective-permute-start | bytes 1179656 | tf_op jit(solution)/shard_map/ppermute | solution.py:439
  30.7 13.3 %collective-permute-start.9 = (bf16[128,1536]{1,0:T(8,128)(2,1)S(1)}, bf16[128,1536]{1,0:T(8,128)(2,1)S(1)}, u32[]{:S(2)}, u32[]{:S(2)}) collective-permute-start(bf16[128,1536]{1,0:T(8,128)(2,1)S(1)} %get-tuple-element.51), channel_id=1, source_target_pairs={{0,2},{1,3},{2,0},{3,1},{4,6},{5,7},{6,4},{7,5},{8,10},{9,11},{10,... | collective-permute-start | bytes 1179656 | tf_op jit(solution)/shard_map/ppermute | solution.py:439
  44.6 29.9 %collective-permute-start.15 = (bf16[1,512,7168]{2,1,0:T(8,128)(2,1)}, bf16[1,512,7168]{2,1,0:T(8,128)(2,1)}, u32[]{:S(2)}, u32[]{:S(2)}) collective-permute-start(bf16[1,512,7168]{2,1,0:T(8,128)(2,1)} %refs_9_.1), channel_id=1, source_target_pairs={{0,16},{16,0},{1,17},{17,1},{2,18},{18,2},{3,19},{19,3},{4,20},{20... | collective-permute-start | bytes 22020104 | tf_op jit(solution)/shard_map/ppermute | solution.py:444
  44.8 9.7 %collective-permute-start.7 = (bf16[16,4096]{1,0:T(8,128)(2,1)S(1)}, bf16[16,4096]{1,0:T(8,128)(2,1)S(1)}, u32[]{:S(2)}, u32[]{:S(2)}) collective-permute-start(bf16[16,4096]{1,0:T(8,128)(2,1)S(1)} %add_convert_fusion.13), channel_id=1, source_target_pairs={{0,8},{1,9},{2,10},{3,11},{4,12},{5,13},{6,14},{7,15},{8,0},{9,1},... | collective-permute-start | bytes 393224 | tf_op jit(solution)/shard_map/ppermute | solution.py:439
  47.6 7.5 %collective-permute-start.12 = (bf16[64,1536]{1,0:T(8,128)(2,1)S(1)}, bf16[64,1536]{1,0:T(8,128)(2,1)S(1)}, u32[]{:S(2)}, u32[]{:S(2)}) collective-permute-start(bf16[64,1536]{1,0:T(8,128)(2,1)S(1)} %get-tuple-element.85), channel_id=1, source_target_pairs={{0,1},{1,0},{2,3},{3,2},{4,5},{5,4},{6,7},{7,6},{8,9},{9,8},{10,11... | collective-permute-start | bytes 589832 | tf_op jit(solution)/shard_map/ppermute | solution.py:439
  48.3 6.8 %collective-permute-start.11 = (bf16[64,1536]{1,0:T(8,128)(2,1)S(1)}, bf16[64,1536]{1,0:T(8,128)(2,1)S(1)}, u32[]{:S(2)}, u32[]{:S(2)}) collective-permute-start(bf16[64,1536]{1,0:T(8,128)(2,1)S(1)} %get-tuple-element.83), channel_id=1, source_target_pairs={{0,2},{1,3},{2,0},{3,1},{4,6},{5,7},{6,4},{7,5},{8,10},{9,11},{10,... | collective-permute-start | bytes 589832 | tf_op jit(solution)/shard_map/ppermute | solution.py:439
  54.7 9.0 %collective-permute-start.16 = (bf16[16,4096]{1,0:T(8,128)(2,1)S(1)}, bf16[16,4096]{1,0:T(8,128)(2,1)S(1)}, u32[]{:S(2)}, u32[]{:S(2)}) collective-permute-start(bf16[16,4096]{1,0:T(8,128)(2,1)S(1)} %fusion), channel_id=1, source_target_pairs={{0,8},{1,9},{2,10},{3,11},{4,12},{5,13},{6,14},{7,15},{8,0},{9,1},... | collective-permute-start | bytes 393224 | tf_op jit(solution)/shard_map/ppermute | solution.py:439
  55.2 10.7 %collective-permute-start.13 = (bf16[32,3072]{1,0:T(8,128)(2,1)S(1)}, bf16[32,3072]{1,0:T(8,128)(2,1)S(1)}, u32[]{:S(2)}, u32[]{:S(2)}) collective-permute-start(bf16[32,3072]{1,0:T(8,128)(2,1)S(1)} %get-tuple-element.81), channel_id=1, source_target_pairs={{0,4},{1,5},{2,6},{3,7},{4,0},{5,1},{6,2},{7,3},{8,12},{9,13},{10,... | collective-permute-start | bytes 589832 | tf_op jit(solution)/shard_map/ppermute | solution.py:439
  63.7 9.4 %collective-permute-start.17 = (bf16[32,4096]{1,0:T(8,128)(2,1)S(1)}, bf16[32,4096]{1,0:T(8,128)(2,1)S(1)}, u32[]{:S(2)}, u32[]{:S(2)}) collective-permute-start(bf16[32,4096]{1,0:T(8,128)(2,1)S(1)} %pad_maximum_fusion.6), channel_id=1, source_target_pairs={{0,4},{1,5},{2,6},{3,7},{4,0},{5,1},{6,2},{7,3},{8,12},{9,13},{10,... | collective-permute-start | bytes 786440 | tf_op jit(solution)/shard_map/ppermute | solution.py:439
  66.0 8.5 %collective-permute-start.14 = (bf16[16,3072]{1,0:T(8,128)(2,1)S(1)}, bf16[16,3072]{1,0:T(8,128)(2,1)S(1)}, u32[]{:S(2)}, u32[]{:S(2)}) collective-permute-start(bf16[16,3072]{1,0:T(8,128)(2,1)S(1)} %get-tuple-element.88), channel_id=1, source_target_pairs={{0,8},{1,9},{2,10},{3,11},{4,12},{5,13},{6,14},{7,15},{8,0},{9,1},... | collective-permute-start | bytes 294920 | tf_op jit(solution)/shard_map/ppermute | solution.py:439
  73.2 8.7 %collective-permute-start.20 = (bf16[64,2048]{1,0:T(8,128)(2,1)S(1)}, bf16[64,2048]{1,0:T(8,128)(2,1)S(1)}, u32[]{:S(2)}, u32[]{:S(2)}) collective-permute-start(bf16[64,2048]{1,0:T(8,128)(2,1)S(1)} %get-tuple-element.86), channel_id=1, source_target_pairs={{0,1},{1,0},{2,3},{3,2},{4,5},{5,4},{6,7},{7,6},{8,9},{9,8},{10,11... | collective-permute-start | bytes 786440 | tf_op jit(solution)/shard_map/ppermute | solution.py:439
  74.9 6.9 %collective-permute-start.22 = (bf16[16,3200]{1,0:T(8,128)(2,1)S(1)}, bf16[16,3200]{1,0:T(8,128)(2,1)S(1)}, u32[]{:S(2)}, u32[]{:S(2)}) collective-permute-start(bf16[16,3200]{1,0:T(8,128)(2,1)S(1)} %concatenate.53), channel_id=1, source_target_pairs={{0,8},{1,9},{2,10},{3,11},{4,12},{5,13},{6,14},{7,15},{8,0},{9,1},... | collective-permute-start | bytes 307208 | tf_op jit(solution)/shard_map/ppermute | solution.py:439
  80.3 18.0 %collective-permute-start.19 = (bf16[128,2048]{1,0:T(8,128)(2,1)S(1)}, bf16[128,2048]{1,0:T(8,128)(2,1)S(1)}, u32[]{:S(2)}, u32[]{:S(2)}) collective-permute-start(bf16[128,2048]{1,0:T(8,128)(2,1)S(1)} %pad_maximum_fusion.1.refs_0_), channel_id=1, source_target_pairs={{0,1},{1,0},{2,3},{3,2},{4,5},{5,4},{6,7},{7,6},{8,9},{9,8},{10,11... | collective-permute-start | bytes 1572872 | tf_op jit(solution)/shard_map/ppermute | solution.py:439
  82.0 16.3 %collective-permute-start.21 = (bf16[128,2048]{1,0:T(8,128)(2,1)S(1)}, bf16[128,2048]{1,0:T(8,128)(2,1)S(1)}, u32[]{:S(2)}, u32[]{:S(2)}) collective-permute-start(bf16[128,2048]{1,0:T(8,128)(2,1)S(1)} %pad_maximum_fusion.2.refs_2_), channel_id=1, source_target_pairs={{0,2},{1,3},{2,0},{3,1},{4,6},{5,7},{6,4},{7,5},{8,10},{9,11},{10,... | collective-permute-start | bytes 1572872 | tf_op jit(solution)/shard_map/ppermute | solution.py:439
  87.7 10.5 %collective-permute-start.24 = (bf16[64,1536]{1,0:T(8,128)(2,1)S(1)}, bf16[64,1536]{1,0:T(8,128)(2,1)S(1)}, u32[]{:S(2)}, u32[]{:S(2)}) collective-permute-start(bf16[64,1536]{1,0:T(8,128)(2,1)S(1)} %pad_maximum_fusion.11), channel_id=1, source_target_pairs={{0,2},{1,3},{2,0},{3,1},{4,6},{5,7},{6,4},{7,5},{8,10},{9,11},{10,... | collective-permute-start | bytes 589832 | tf_op jit(solution)/shard_map/ppermute | solution.py:439
  89.0 9.2 %collective-permute-start.25 = (bf16[64,1664]{1,0:T(8,128)(2,1)S(1)}, bf16[64,1664]{1,0:T(8,128)(2,1)S(1)}, u32[]{:S(2)}, u32[]{:S(2)}) collective-permute-start(bf16[64,1664]{1,0:T(8,128)(2,1)S(1)} %pad_maximum_fusion.8), channel_id=1, source_target_pairs={{0,1},{1,0},{2,3},{3,2},{4,5},{5,4},{6,7},{7,6},{8,9},{9,8},{10,11... | collective-permute-start | bytes 638984 | tf_op jit(solution)/shard_map/ppermute | solution.py:439
  98.3 10.9 %collective-permute-start.27 = (bf16[128,1664]{1,0:T(8,128)(2,1)S(1)}, bf16[128,1664]{1,0:T(8,128)(2,1)S(1)}, u32[]{:S(2)}, u32[]{:S(2)}) collective-permute-start(bf16[128,1664]{1,0:T(8,128)(2,1)S(1)} %pad_maximum_fusion.3.refs_2_), channel_id=1, source_target_pairs={{0,2},{1,3},{2,0},{3,1},{4,6},{5,7},{6,4},{7,5},{8,10},{9,11},{10,... | collective-permute-start | bytes 1277960 | tf_op jit(solution)/shard_map/ppermute | solution.py:439
  100.1 9.0 %collective-permute-start.26 = (bf16[128,1536]{1,0:T(8,128)(2,1)S(1)}, bf16[128,1536]{1,0:T(8,128)(2,1)S(1)}, u32[]{:S(2)}, u32[]{:S(2)}) collective-permute-start(bf16[128,1536]{1,0:T(8,128)(2,1)S(1)} %pad_maximum_fusion.4.refs_0_), channel_id=1, source_target_pairs={{0,1},{1,0},{2,3},{3,2},{4,5},{5,4},{6,7},{7,6},{8,9},{9,8},{10,11... | collective-permute-start | bytes 1179656 | tf_op jit(solution)/shard_map/ppermute | solution.py:439
  (8 other events, 146.7 us)

commit v6 on v5

--- a/solution.py
+++ b/solution.py
@@ -382,7 +382,7 @@
             pltpu.VMEM((len(pieces), 2 * columns, wide), bf16),
             pltpu.SemaphoreType.DMA((len(pieces) + 1,)),
         ],
-        compiler_params=pltpu.CompilerParams(vmem_limit_bytes=20 << 20),
+        compiler_params=pltpu.CompilerParams(vmem_limit_bytes=24 << 20),
         cost_estimate=pl.CostEstimate(
             flops=8 * rows * columns * hidden,
             bytes_accessed=8 * columns * hidden + 8 * rows * hidden,
@@ -536,13 +536,13 @@
         )
 
     got = first_swap(parts, senders)
-    got, more, gate_others = tie(got, more, gate_others)
+    got, more, gate_others, up_others, down_source = tie(got, more, gate_others, up_others, w_down)
     terms = second_swap(parts, got, senders)
     got = first_swap(more, senders)
     ahead, rest = joined(terms), inner_bits[:-1]
     for bit in rest:
         ahead = halve(ahead, bit, senders)
-    got, _, up_others, down_source = tie(got, ahead, up_others, w_down)
+    got, _ = tie(got, ahead)
     down_others = shifted(down_source, slabs)[1:]
 
     behind = second_swap(more, got, senders)

time: 122 us -> 119 us (0.975)
  waiting for transfers between devices: 56.8 us -> 46.8 us
  starting transfers between devices: 30.7 us -> 37.4 us
    ppermute x24, waiting for transfers between devices: 55.3 us -> 45.4 us  [swap(): return lax.ppermute(value, 'exp', [(i, i ^ 1 << bit) for i in range(count)])]
    ppermute x24, starting transfers between devices: 29.6 us -> 36.4 us  [swap(): return lax.ppermute(value, 'exp', [(i, i ^ 1 << bit) for i in range(count)])]
  transfers between devices with their start and end apart: 28 -> 28, of which waited for: 15 -> 19; matrix products, arithmetic and copies ran while one was open for 2% -> 2% of each run, Pallas kernels for 15% -> 15%
where the time goes in v6:
time: 119 us
  waiting for transfers between devices  46.8 us (39%)
  starting transfers between devices  37.4 us (31%)
  Pallas kernels  30.8 us (26%)
  other arithmetic  2.18 us (2%)
    ppermute x24, waiting for transfers between devices, swap(): return lax.ppermute(value, 'exp', [(i, i ^ 1 << bit) for i in range(count)])  45.4 us
    ppermute x24, starting transfers between devices, swap(): return lax.ppermute(value, 'exp', [(i, i ^ 1 << bit) for i in range(count)])  36.4 us
    pallas_call x1, Pallas kernels, finish(): pl.pallas_call(functools.partial(finish_kernel, len(gates), rows // 4, co...  12.7 us
    pallas_call x1, Pallas kernels, gate_up(): pl.pallas_call(functools.partial(gate_up_kernel, len(gates), rows // 4, c...  7.41 us
    pallas_call x1, Pallas kernels, attend_project(): pl.pallas_call(functools.partial(attend_kernel, slabs, block, orders), gr...  7.03 us
    pallas_call x1, Pallas kernels, project_more(): pl.pallas_call(project_kernel, grid=(steps,), in_specs=[whole(hva.shape),...  3.63 us
  transfers between devices with their start and end apart: 28, of which 19 were waited for; matrix products, arithmetic and copies ran while one was open for 2% of the time, Pallas kernels for 15%

profile of v6, /device:TPU:0, one launch (start us, length us, event | category | flops | bytes accessed | tf_op | source)
XLA Modules:
  0.0 118.8 jit_solution(13212143434726709980)
XLA Ops:
  3.2 7.0 %attend_project.1 = (bf16[256,512]{1,0:T(8,128)(2,1)S(1)}, bf16[256,512]{1,0:T(8,128)(2,1)S(1)}, bf16[128,2048]{1,0:T(8,128)(2,1)S(1)}, bf16[128,2048]{1,0:T(8,1...) custom-call(s32[2]{0:T(128)S(1)} %pad_add_fusion.place_ref, bf16[256,2304]{1,0:T(8,128)(2,1)} %q_ref.1, ...), custom_call_target="tpu_custom_call" | custom-call | flops 2281701376 | bytes 7471104 | tf_op jit(solution)/shard_map/attend_project/pallas_call | solution.py:152
  10.2 2.9 %collective-permute-start.1 = (bf16[128,2048]{1,0:T(8,128)(2,1)S(1)}, bf16[128,2048]{1,0:T(8,128)(2,1)S(1)}, u32[]{:S(2)}, u32[]{:S(2)}) collective-permute-start(bf16[128,2048]{1,0:T(8,128)(2,1)S(1)} %get-tuple-element.37), channel_id=1, source_target_pairs={{0,1},{1,0},{2,3},{3,2},{4,5},{5,4},{6,7},{7,6},{8,9},{9,8},{10,11... | collective-permute-start | bytes 1572872 | tf_op jit(solution)/shard_map/ppermute | solution.py:439
  14.6 3.6 %project_more.1 = (bf16[128,1536]{1,0:T(8,128)(2,1)S(1)}, bf16[128,1536]{1,0:T(8,128)(2,1)S(1)}, bf16[128,1536]{1,0:T(8,128)(2,1)S(1)}, bf16[128,1536]{1,0:T(8,128)(2,1)S(1)}) custom-call(bf16[256,512]{1,0:T(8,128)(2,1)S(1)} %get-tuple-element.39.hva_ref, bf16[256,512]{1,0:T(8,128)(2,1)S(1)} %get-tuple-element.40.hvb_ref, bf16[512,7168]{1,0:T(8,128)(2,1)} %wb_ref.1, ...), custom_call_target="tpu_custom_call" | custom-call | flops 805306368 | bytes 4718592 | tf_op jit(solution)/shard_map/project_more/pallas_call | solution.py:181
  18.3 7.0 %collective-permute-done.1 = bf16[128,2048]{1,0:T(8,128)(2,1)S(1)} collective-permute-done((bf16[128,2048]{1,0:T(8,128)(2,1)S(1)}, bf16[128,2048]{1,0:T(8,128)(2,1)S(1)}, u32[]{:S(2)}, u32[]{:S(2)}) %collective-permute-start.1) | collective-permute-done | bytes 524320 | tf_op jit(solution)/shard_map/ppermute | solution.py:439
  29.8 4.9 %collective-permute-done.5 = bf16[64,2048]{1,0:T(8,128)(2,1)S(1)} collective-permute-done((bf16[64,2048]{1,0:T(8,128)(2,1)S(1)}, bf16[64,2048]{1,0:T(8,128)(2,1)S(1)}, u32[]{:S(2)}, u32[]{:S(2)}) %collective-permute-start.5) | collective-permute-done | bytes 262176 | tf_op jit(solution)/shard_map/ppermute | solution.py:439
  36.6 1.6 %collective-permute-start.7 = (bf16[32,4096]{1,0:T(8,128)(2,1)S(1)}, bf16[32,4096]{1,0:T(8,128)(2,1)S(1)}, u32[]{:S(2)}, u32[]{:S(2)}) collective-permute-start(bf16[32,4096]{1,0:T(8,128)(2,1)S(1)} %get-tuple-element.74), channel_id=1, source_target_pairs={{0,4},{1,5},{2,6},{3,7},{4,0},{5,1},{6,2},{7,3},{8,12},{9,13},{10,... | collective-permute-start | bytes 786440 | tf_op jit(solution)/shard_map/ppermute | solution.py:439
  40.4 3.0 %collective-permute-done.7 = bf16[32,4096]{1,0:T(8,128)(2,1)S(1)} collective-permute-done((bf16[32,4096]{1,0:T(8,128)(2,1)S(1)}, bf16[32,4096]{1,0:T(8,128)(2,1)S(1)}, u32[]{:S(2)}, u32[]{:S(2)}) %collective-permute-start.7) | collective-permute-done | bytes 262176 | tf_op jit(solution)/shard_map/ppermute | solution.py:439
  43.4 2.7 %collective-permute-start.8 = (bf16[16,4096]{1,0:T(8,128)(2,1)S(1)}, bf16[16,4096]{1,0:T(8,128)(2,1)S(1)}, u32[]{:S(2)}, u32[]{:S(2)}) collective-permute-start(bf16[16,4096]{1,0:T(8,128)(2,1)S(1)} %add_convert_fusion.13), channel_id=1, source_target_pairs={{0,8},{1,9},{2,10},{3,11},{4,12},{5,13},{6,14},{7,15},{8,0},{9,1},... | collective-permute-start | bytes 393224 | tf_op jit(solution)/shard_map/ppermute | solution.py:439
  46.1 1.8 %collective-permute-done.9 = bf16[128,1536]{1,0:T(8,128)(2,1)S(1)} collective-permute-done((bf16[128,1536]{1,0:T(8,128)(2,1)S(1)}, bf16[128,1536]{1,0:T(8,128)(2,1)S(1)}, u32[]{:S(2)}, u32[]{:S(2)}) %collective-permute-start.9) | collective-permute-done | bytes 393248 | tf_op jit(solution)/shard_map/ppermute | solution.py:439
  51.0 2.4 %collective-permute-start.16 = (bf16[16,4096]{1,0:T(8,128)(2,1)S(1)}, bf16[16,4096]{1,0:T(8,128)(2,1)S(1)}, u32[]{:S(2)}, u32[]{:S(2)}) collective-permute-start(bf16[16,4096]{1,0:T(8,128)(2,1)S(1)} %fusion), channel_id=1, source_target_pairs={{0,8},{1,9},{2,10},{3,11},{4,12},{5,13},{6,14},{7,15},{8,0},{9,1},... | collective-permute-start | bytes 393224 | tf_op jit(solution)/shard_map/ppermute | solution.py:439
  53.4 2.3 %collective-permute-done.11 = bf16[64,1536]{1,0:T(8,128)(2,1)S(1)} collective-permute-done((bf16[64,1536]{1,0:T(8,128)(2,1)S(1)}, bf16[64,1536]{1,0:T(8,128)(2,1)S(1)}, u32[]{:S(2)}, u32[]{:S(2)}) %collective-permute-start.11) | collective-permute-done | bytes 196640 | tf_op jit(solution)/shard_map/ppermute | solution.py:439
  56.4 2.1 %collective-permute-done.16 = bf16[16,4096]{1,0:T(8,128)(2,1)S(1)} collective-permute-done((bf16[16,4096]{1,0:T(8,128)(2,1)S(1)}, bf16[16,4096]{1,0:T(8,128)(2,1)S(1)}, u32[]{:S(2)}, u32[]{:S(2)}) %collective-permute-start.16) | collective-permute-done | bytes 131104 | tf_op jit(solution)/shard_map/ppermute | solution.py:439
  59.0 5.3 %collective-permute-done.13 = bf16[32,3072]{1,0:T(8,128)(2,1)S(1)} collective-permute-done((bf16[32,3072]{1,0:T(8,128)(2,1)S(1)}, bf16[32,3072]{1,0:T(8,128)(2,1)S(1)}, u32[]{:S(2)}, u32[]{:S(2)}) %collective-permute-start.13) | collective-permute-done | bytes 196640 | tf_op jit(solution)/shard_map/ppermute | solution.py:439
  64.4 1.9 %collective-permute-start.14 = (bf16[16,3072]{1,0:T(8,128)(2,1)S(1)}, bf16[16,3072]{1,0:T(8,128)(2,1)S(1)}, u32[]{:S(2)}, u32[]{:S(2)}) collective-permute-start(bf16[16,3072]{1,0:T(8,128)(2,1)S(1)} %get-tuple-element.88), channel_id=1, source_target_pairs={{0,8},{1,9},{2,10},{3,11},{4,12},{5,13},{6,14},{7,15},{8,0},{9,1},... | collective-permute-start | bytes 294920 | tf_op jit(solution)/shard_map/ppermute | solution.py:439
  67.2 1.8 %collective-permute-start.20 = (bf16[64,2048]{1,0:T(8,128)(2,1)S(1)}, bf16[64,2048]{1,0:T(8,128)(2,1)S(1)}, u32[]{:S(2)}, u32[]{:S(2)}) collective-permute-start(bf16[64,2048]{1,0:T(8,128)(2,1)S(1)} %get-tuple-element.86), channel_id=1, source_target_pairs={{0,1},{1,0},{2,3},{3,2},{4,5},{5,4},{6,7},{7,6},{8,9},{9,8},{10,11... | collective-permute-start | bytes 786440 | tf_op jit(solution)/shard_map/ppermute | solution.py:439
  72.7 2.7 %collective-permute-done.18 = bf16[64,2048]{1,0:T(8,128)(2,1)S(1)} collective-permute-done((bf16[64,2048]{1,0:T(8,128)(2,1)S(1)}, bf16[64,2048]{1,0:T(8,128)(2,1)S(1)}, u32[]{:S(2)}, u32[]{:S(2)}) %collective-permute-start.18) | collective-permute-done | bytes 262176 | tf_op jit(solution)/shard_map/ppermute | solution.py:439
  77.1 3.1 %collective-permute-start.23 = (bf16[32,3200]{1,0:T(8,128)(2,1)S(1)}, bf16[32,3200]{1,0:T(8,128)(2,1)S(1)}, u32[]{:S(2)}, u32[]{:S(2)}) collective-permute-start(bf16[32,3200]{1,0:T(8,128)(2,1)S(1)} %pad_maximum_fusion.10), channel_id=1, source_target_pairs={{0,4},{1,5},{2,6},{3,7},{4,0},{5,1},{6,2},{7,3},{8,12},{9,13},{10,... | collective-permute-start | bytes 614408 | tf_op jit(solution)/shard_map/ppermute | solution.py:439
  81.2 2.7 %collective-permute-done.23 = bf16[32,3200]{1,0:T(8,128)(2,1)S(1)} collective-permute-done((bf16[32,3200]{1,0:T(8,128)(2,1)S(1)}, bf16[32,3200]{1,0:T(8,128)(2,1)S(1)}, u32[]{:S(2)}, u32[]{:S(2)}) %collective-permute-start.23) | collective-permute-done | bytes 204832 | tf_op jit(solution)/shard_map/ppermute | solution.py:439
  84.0 1.7 %collective-permute-start.24 = (bf16[64,1536]{1,0:T(8,128)(2,1)S(1)}, bf16[64,1536]{1,0:T(8,128)(2,1)S(1)}, u32[]{:S(2)}, u32[]{:S(2)}) collective-permute-start(bf16[64,1536]{1,0:T(8,128)(2,1)S(1)} %pad_maximum_fusion.11), channel_id=1, source_target_pairs={{0,2},{1,3},{2,0},{3,1},{4,6},{5,7},{6,4},{7,5},{8,10},{9,11},{10,... | collective-permute-start | bytes 589832 | tf_op jit(solution)/shard_map/ppermute | solution.py:439
  85.7 2.7 %collective-permute-start.25 = (bf16[64,1664]{1,0:T(8,128)(2,1)S(1)}, bf16[64,1664]{1,0:T(8,128)(2,1)S(1)}, u32[]{:S(2)}, u32[]{:S(2)}) collective-permute-start(bf16[64,1664]{1,0:T(8,128)(2,1)S(1)} %pad_maximum_fusion.8), channel_id=1, source_target_pairs={{0,1},{1,0},{2,3},{3,2},{4,5},{5,4},{6,7},{7,6},{8,9},{9,8},{10,11... | collective-permute-start | bytes 638984 | tf_op jit(solution)/shard_map/ppermute | solution.py:439
  88.3 5.3 %collective-permute-done.24 = bf16[64,1536]{1,0:T(8,128)(2,1)S(1)} collective-permute-done((bf16[64,1536]{1,0:T(8,128)(2,1)S(1)}, bf16[64,1536]{1,0:T(8,128)(2,1)S(1)}, u32[]{:S(2)}, u32[]{:S(2)}) %collective-permute-start.24) | collective-permute-done | bytes 196640 | tf_op jit(solution)/shard_map/ppermute | solution.py:439
  96.0 2.5 %collective-permute-start.26 = (bf16[128,1536]{1,0:T(8,128)(2,1)S(1)}, bf16[128,1536]{1,0:T(8,128)(2,1)S(1)}, u32[]{:S(2)}, u32[]{:S(2)}) collective-permute-start(bf16[128,1536]{1,0:T(8,128)(2,1)S(1)} %pad_maximum_fusion.4.refs_0_), channel_id=1, source_target_pairs={{0,1},{1,0},{2,3},{3,2},{4,5},{5,4},{6,7},{7,6},{8,9},{9,8},{10,11... | collective-permute-start | bytes 1179656 | tf_op jit(solution)/shard_map/ppermute | solution.py:439
  98.5 7.4 %gate_up.1.refs_4_ = f32[2,256,1024]{2,1,0:T(8,128)S(1)} custom-call(bf16[128,2048]{1,0:T(8,128)(2,1)S(1)} %pad_maximum_fusion.1.refs_0_, bf16[128,2048]{1,0:T(8,128)(2,1)S(1)} %collective-permute-done.19.refs_1_, bf16[128,2048]{1,0:T(8,128)(2,1)S(1)} %pad_maximum_fusion.2.refs_2_, bf16[128,2048]{1,0:T(8,128)(2,1)S(1)} %collective-permute-done.21.refs_3_, ...), custom_call_target="tpu_custom_call" | custom-call | flops 4294967296 | bytes 18874368 | tf_op jit(solution)/shard_map/gate_up/pallas_call | solution.py:375
  106.0 12.7 %finish.1 = bf16[192,7168]{1,0:T(8,128)(2,1)} custom-call(s32[2]{0:T(128)S(1)} %pad_add_fusion.place_ref, bf16[128,1536]{1,0:T(8,128)(2,1)S(1)} %pad_maximum_fusion.4.refs_0_, bf16[128,1536]{1,0:T(8,128)(2,1)S(1)} %collective-permute-done.26.refs_1_, bf16[128,1664]{1,0:T(8,128)(2,1)S(1)} %pad_maximum_fusion.3.refs_2_, ...), custom_call_target="tpu_custom_call" | custom-call | flops 6039797760 | bytes 30015488 | tf_op jit(solution)/shard_map/finish/pallas_call | solution.py:404
  (84 shorter events, 26.5 us)
Async XLA Ops:
  2.6 24.2 %collective-permute-start.3 = (bf16[1,7168,512]{2,1,0:T(8,128)(2,1)}, bf16[1,7168,512]{2,1,0:T(8,128)(2,1)}, u32[]{:S(2)}, u32[]{:S(2)}) collective-permute-start(bf16[1,7168,512]{2,1,0:T(8,128)(2,1)} %refs_5_.3), channel_id=1, source_target_pairs={{0,16},{16,0},{1,17},{17,1},{2,18},{18,2},{3,19},{19,3},{4,20},{20... | collective-permute-start | bytes 22020104 | tf_op jit(solution)/shard_map/ppermute | solution.py:444
  2.9 23.9 %collective-permute-start.4 = (bf16[1,7168,512]{2,1,0:T(8,128)(2,1)}, bf16[1,7168,512]{2,1,0:T(8,128)(2,1)}, u32[]{:S(2)}, u32[]{:S(2)}) collective-permute-start(bf16[1,7168,512]{2,1,0:T(8,128)(2,1)} %refs_6_.1), channel_id=1, source_target_pairs={{0,16},{16,0},{1,17},{17,1},{2,18},{18,2},{3,19},{19,3},{4,20},{20... | collective-permute-start | bytes 22020104 | tf_op jit(solution)/shard_map/ppermute | solution.py:444
  10.2 15.1 %collective-permute-start.1 = (bf16[128,2048]{1,0:T(8,128)(2,1)S(1)}, bf16[128,2048]{1,0:T(8,128)(2,1)S(1)}, u32[]{:S(2)}, u32[]{:S(2)}) collective-permute-start(bf16[128,2048]{1,0:T(8,128)(2,1)S(1)} %get-tuple-element.37), channel_id=1, source_target_pairs={{0,1},{1,0},{2,3},{3,2},{4,5},{5,4},{6,7},{7,6},{8,9},{9,8},{10,11... | collective-permute-start | bytes 1572872 | tf_op jit(solution)/shard_map/ppermute | solution.py:439
  13.1 13.7 %collective-permute-start.2 = (bf16[128,2048]{1,0:T(8,128)(2,1)S(1)}, bf16[128,2048]{1,0:T(8,128)(2,1)S(1)}, u32[]{:S(2)}, u32[]{:S(2)}) collective-permute-start(bf16[128,2048]{1,0:T(8,128)(2,1)S(1)} %get-tuple-element.38), channel_id=1, source_target_pairs={{0,2},{1,3},{2,0},{3,1},{4,6},{5,7},{6,4},{7,5},{8,10},{9,11},{10,... | collective-permute-start | bytes 1572872 | tf_op jit(solution)/shard_map/ppermute | solution.py:439
  26.9 7.8 %collective-permute-start.5 = (bf16[64,2048]{1,0:T(8,128)(2,1)S(1)}, bf16[64,2048]{1,0:T(8,128)(2,1)S(1)}, u32[]{:S(2)}, u32[]{:S(2)}) collective-permute-start(bf16[64,2048]{1,0:T(8,128)(2,1)S(1)} %get-tuple-element.78), channel_id=1, source_target_pairs={{0,2},{1,3},{2,0},{3,1},{4,6},{5,7},{6,4},{7,5},{8,10},{9,11},{10,... | collective-permute-start | bytes 786440 | tf_op jit(solution)/shard_map/ppermute | solution.py:439
  28.7 7.8 %collective-permute-start.6 = (bf16[64,2048]{1,0:T(8,128)(2,1)S(1)}, bf16[64,2048]{1,0:T(8,128)(2,1)S(1)}, u32[]{:S(2)}, u32[]{:S(2)}) collective-permute-start(bf16[64,2048]{1,0:T(8,128)(2,1)S(1)} %get-tuple-element.76), channel_id=1, source_target_pairs={{0,1},{1,0},{2,3},{3,2},{4,5},{5,4},{6,7},{7,6},{8,9},{9,8},{10,11... | collective-permute-start | bytes 786440 | tf_op jit(solution)/shard_map/ppermute | solution.py:439
  29.8 41.1 %collective-permute-start.15 = (bf16[1,512,7168]{2,1,0:T(8,128)(2,1)}, bf16[1,512,7168]{2,1,0:T(8,128)(2,1)}, u32[]{:S(2)}, u32[]{:S(2)}) collective-permute-start(bf16[1,512,7168]{2,1,0:T(8,128)(2,1)} %refs_9_.1), channel_id=1, source_target_pairs={{0,16},{16,0},{1,17},{17,1},{2,18},{18,2},{3,19},{19,3},{4,20},{20... | collective-permute-start | bytes 22020104 | tf_op jit(solution)/shard_map/ppermute | solution.py:444
  36.6 6.8 %collective-permute-start.7 = (bf16[32,4096]{1,0:T(8,128)(2,1)S(1)}, bf16[32,4096]{1,0:T(8,128)(2,1)S(1)}, u32[]{:S(2)}, u32[]{:S(2)}) collective-permute-start(bf16[32,4096]{1,0:T(8,128)(2,1)S(1)} %get-tuple-element.74), channel_id=1, source_target_pairs={{0,4},{1,5},{2,6},{3,7},{4,0},{5,1},{6,2},{7,3},{8,12},{9,13},{10,... | collective-permute-start | bytes 786440 | tf_op jit(solution)/shard_map/ppermute | solution.py:439
  38.4 9.5 %collective-permute-start.9 = (bf16[128,1536]{1,0:T(8,128)(2,1)S(1)}, bf16[128,1536]{1,0:T(8,128)(2,1)S(1)}, u32[]{:S(2)}, u32[]{:S(2)}) collective-permute-start(bf16[128,1536]{1,0:T(8,128)(2,1)S(1)} %get-tuple-element.51), channel_id=1, source_target_pairs={{0,1},{1,0},{2,3},{3,2},{4,5},{5,4},{6,7},{7,6},{8,9},{9,8},{10,11... | collective-permute-start | bytes 1179656 | tf_op jit(solution)/shard_map/ppermute | solution.py:439
  39.9 9.5 %collective-permute-start.10 = (bf16[128,1536]{1,0:T(8,128)(2,1)S(1)}, bf16[128,1536]{1,0:T(8,128)(2,1)S(1)}, u32[]{:S(2)}, u32[]{:S(2)}) collective-permute-start(bf16[128,1536]{1,0:T(8,128)(2,1)S(1)} %get-tuple-element.52), channel_id=1, source_target_pairs={{0,2},{1,3},{2,0},{3,1},{4,6},{5,7},{6,4},{7,5},{8,10},{9,11},{10,... | collective-permute-start | bytes 1179656 | tf_op jit(solution)/shard_map/ppermute | solution.py:439
  43.4 7.3 %collective-permute-start.8 = (bf16[16,4096]{1,0:T(8,128)(2,1)S(1)}, bf16[16,4096]{1,0:T(8,128)(2,1)S(1)}, u32[]{:S(2)}, u32[]{:S(2)}) collective-permute-start(bf16[16,4096]{1,0:T(8,128)(2,1)S(1)} %add_convert_fusion.13), channel_id=1, source_target_pairs={{0,8},{1,9},{2,10},{3,11},{4,12},{5,13},{6,14},{7,15},{8,0},{9,1},... | collective-permute-start | bytes 393224 | tf_op jit(solution)/shard_map/ppermute | solution.py:439
  51.0 7.4 %collective-permute-start.16 = (bf16[16,4096]{1,0:T(8,128)(2,1)S(1)}, bf16[16,4096]{1,0:T(8,128)(2,1)S(1)}, u32[]{:S(2)}, u32[]{:S(2)}) collective-permute-start(bf16[16,4096]{1,0:T(8,128)(2,1)S(1)} %fusion), channel_id=1, source_target_pairs={{0,8},{1,9},{2,10},{3,11},{4,12},{5,13},{6,14},{7,15},{8,0},{9,1},... | collective-permute-start | bytes 393224 | tf_op jit(solution)/shard_map/ppermute | solution.py:439
  55.9 8.4 %collective-permute-start.13 = (bf16[32,3072]{1,0:T(8,128)(2,1)S(1)}, bf16[32,3072]{1,0:T(8,128)(2,1)S(1)}, u32[]{:S(2)}, u32[]{:S(2)}) collective-permute-start(bf16[32,3072]{1,0:T(8,128)(2,1)S(1)} %get-tuple-element.81), channel_id=1, source_target_pairs={{0,4},{1,5},{2,6},{3,7},{4,0},{5,1},{6,2},{7,3},{8,12},{9,13},{10,... | collective-permute-start | bytes 589832 | tf_op jit(solution)/shard_map/ppermute | solution.py:439
  58.5 8.6 %collective-permute-start.17 = (bf16[32,4096]{1,0:T(8,128)(2,1)S(1)}, bf16[32,4096]{1,0:T(8,128)(2,1)S(1)}, u32[]{:S(2)}, u32[]{:S(2)}) collective-permute-start(bf16[32,4096]{1,0:T(8,128)(2,1)S(1)} %pad_maximum_fusion.6), channel_id=1, source_target_pairs={{0,4},{1,5},{2,6},{3,7},{4,0},{5,1},{6,2},{7,3},{8,12},{9,13},{10,... | collective-permute-start | bytes 786440 | tf_op jit(solution)/shard_map/ppermute | solution.py:439
  64.4 6.5 %collective-permute-start.14 = (bf16[16,3072]{1,0:T(8,128)(2,1)S(1)}, bf16[16,3072]{1,0:T(8,128)(2,1)S(1)}, u32[]{:S(2)}, u32[]{:S(2)}) collective-permute-start(bf16[16,3072]{1,0:T(8,128)(2,1)S(1)} %get-tuple-element.88), channel_id=1, source_target_pairs={{0,8},{1,9},{2,10},{3,11},{4,12},{5,13},{6,14},{7,15},{8,0},{9,1},... | collective-permute-start | bytes 294920 | tf_op jit(solution)/shard_map/ppermute | solution.py:439
  67.2 13.0 %collective-permute-start.20 = (bf16[64,2048]{1,0:T(8,128)(2,1)S(1)}, bf16[64,2048]{1,0:T(8,128)(2,1)S(1)}, u32[]{:S(2)}, u32[]{:S(2)}) collective-permute-start(bf16[64,2048]{1,0:T(8,128)(2,1)S(1)} %get-tuple-element.86), channel_id=1, source_target_pairs={{0,1},{1,0},{2,3},{3,2},{4,5},{5,4},{6,7},{7,6},{8,9},{9,8},{10,11... | collective-permute-start | bytes 786440 | tf_op jit(solution)/shard_map/ppermute | solution.py:439
  69.0 6.4 %collective-permute-start.18 = (bf16[64,2048]{1,0:T(8,128)(2,1)S(1)}, bf16[64,2048]{1,0:T(8,128)(2,1)S(1)}, u32[]{:S(2)}, u32[]{:S(2)}) collective-permute-start(bf16[64,2048]{1,0:T(8,128)(2,1)S(1)} %get-tuple-element.87), channel_id=1, source_target_pairs={{0,2},{1,3},{2,0},{3,1},{4,6},{5,7},{6,4},{7,5},{8,10},{9,11},{10,... | collective-permute-start | bytes 786440 | tf_op jit(solution)/shard_map/ppermute | solution.py:439
  75.4 18.3 %collective-permute-start.19 = (bf16[128,2048]{1,0:T(8,128)(2,1)S(1)}, bf16[128,2048]{1,0:T(8,128)(2,1)S(1)}, u32[]{:S(2)}, u32[]{:S(2)}) collective-permute-start(bf16[128,2048]{1,0:T(8,128)(2,1)S(1)} %pad_maximum_fusion.1.refs_0_), channel_id=1, source_target_pairs={{0,1},{1,0},{2,3},{3,2},{4,5},{5,4},{6,7},{7,6},{8,9},{9,8},{10,11... | collective-permute-start | bytes 1572872 | tf_op jit(solution)/shard_map/ppermute | solution.py:439
  77.1 6.9 %collective-permute-start.23 = (bf16[32,3200]{1,0:T(8,128)(2,1)S(1)}, bf16[32,3200]{1,0:T(8,128)(2,1)S(1)}, u32[]{:S(2)}, u32[]{:S(2)}) collective-permute-start(bf16[32,3200]{1,0:T(8,128)(2,1)S(1)} %pad_maximum_fusion.10), channel_id=1, source_target_pairs={{0,4},{1,5},{2,6},{3,7},{4,0},{5,1},{6,2},{7,3},{8,12},{9,13},{10,... | collective-permute-start | bytes 614408 | tf_op jit(solution)/shard_map/ppermute | solution.py:439
  80.3 13.5 %collective-permute-start.21 = (bf16[128,2048]{1,0:T(8,128)(2,1)S(1)}, bf16[128,2048]{1,0:T(8,128)(2,1)S(1)}, u32[]{:S(2)}, u32[]{:S(2)}) collective-permute-start(bf16[128,2048]{1,0:T(8,128)(2,1)S(1)} %pad_maximum_fusion.2.refs_2_), channel_id=1, source_target_pairs={{0,2},{1,3},{2,0},{3,1},{4,6},{5,7},{6,4},{7,5},{8,10},{9,11},{10,... | collective-permute-start | bytes 1572872 | tf_op jit(solution)/shard_map/ppermute | solution.py:439
  84.0 9.7 %collective-permute-start.24 = (bf16[64,1536]{1,0:T(8,128)(2,1)S(1)}, bf16[64,1536]{1,0:T(8,128)(2,1)S(1)}, u32[]{:S(2)}, u32[]{:S(2)}) collective-permute-start(bf16[64,1536]{1,0:T(8,128)(2,1)S(1)} %pad_maximum_fusion.11), channel_id=1, source_target_pairs={{0,2},{1,3},{2,0},{3,1},{4,6},{5,7},{6,4},{7,5},{8,10},{9,11},{10,... | collective-permute-start | bytes 589832 | tf_op jit(solution)/shard_map/ppermute | solution.py:439
  85.7 8.1 %collective-permute-start.25 = (bf16[64,1664]{1,0:T(8,128)(2,1)S(1)}, bf16[64,1664]{1,0:T(8,128)(2,1)S(1)}, u32[]{:S(2)}, u32[]{:S(2)}) collective-permute-start(bf16[64,1664]{1,0:T(8,128)(2,1)S(1)} %pad_maximum_fusion.8), channel_id=1, source_target_pairs={{0,1},{1,0},{2,3},{3,2},{4,5},{5,4},{6,7},{7,6},{8,9},{9,8},{10,11... | collective-permute-start | bytes 638984 | tf_op jit(solution)/shard_map/ppermute | solution.py:439
  93.8 12.2 %collective-permute-start.27 = (bf16[128,1664]{1,0:T(8,128)(2,1)S(1)}, bf16[128,1664]{1,0:T(8,128)(2,1)S(1)}, u32[]{:S(2)}, u32[]{:S(2)}) collective-permute-start(bf16[128,1664]{1,0:T(8,128)(2,1)S(1)} %pad_maximum_fusion.3.refs_2_), channel_id=1, source_target_pairs={{0,2},{1,3},{2,0},{3,1},{4,6},{5,7},{6,4},{7,5},{8,10},{9,11},{10,... | collective-permute-start | bytes 1277960 | tf_op jit(solution)/shard_map/ppermute | solution.py:439
  96.0 9.9 %collective-permute-start.26 = (bf16[128,1536]{1,0:T(8,128)(2,1)S(1)}, bf16[128,1536]{1,0:T(8,128)(2,1)S(1)}, u32[]{:S(2)}, u32[]{:S(2)}) collective-permute-start(bf16[128,1536]{1,0:T(8,128)(2,1)S(1)} %pad_maximum_fusion.4.refs_0_), channel_id=1, source_target_pairs={{0,1},{1,0},{2,3},{3,2},{4,5},{5,4},{6,7},{7,6},{8,9},{9,8},{10,11... | collective-permute-start | bytes 1179656 | tf_op jit(solution)/shard_map/ppermute | solution.py:439
  (8 other events, 123.0 us)

commit v7 on v6

--- a/solution.py
+++ b/solution.py
@@ -259,7 +259,7 @@
     pieces = refs[4 : 4 + 2 * slabs]
     acc_ref, x_ref, held_ref, sems = refs[4 + 2 * slabs :]
     copies = weight_copies(pieces, held_ref, sems, 0)
-    window = Window([c[3] for c in copies], 3)
+    window = Window([c[3] for c in copies], 4)
     place_rows(quarter_rows, columns, a_refs, b_refs, x_ref)
     wide = held_ref.shape[2]
     for p in range(len(pieces)):
@@ -296,7 +296,7 @@
         ]
         for j in range(tiles)
     ]
-    window = Window([c[3] for c in copies] + down_copies, 3)
+    window = Window([c[3] for c in copies] + down_copies, 4)
     place_rows(quarter_rows, columns, a_refs, b_refs, x_ref)
 
     me = place_ref[1]

time: 119 us -> 118 us (level)
  no operation moved by 1% of the time
where the time goes in v7:
time: 118 us
  waiting for transfers between devices  46.8 us (40%)
  starting transfers between devices  37.4 us (32%)
  Pallas kernels  30.1 us (26%)
  other arithmetic  2.18 us (2%)
    ppermute x24, waiting for transfers between devices, swap(): return lax.ppermute(value, 'exp', [(i, i ^ 1 << bit) for i in range(count)])  45.4 us
    ppermute x24, starting transfers between devices, swap(): return lax.ppermute(value, 'exp', [(i, i ^ 1 << bit) for i in range(count)])  36.4 us
    pallas_call x1, Pallas kernels, finish(): pl.pallas_call(functools.partial(finish_kernel, len(gates), rows // 4, co...  12.1 us
    pallas_call x1, Pallas kernels, gate_up(): pl.pallas_call(functools.partial(gate_up_kernel, len(gates), rows // 4, c...  7.36 us
    pallas_call x1, Pallas kernels, attend_project(): pl.pallas_call(functools.partial(attend_kernel, slabs, block, orders), gr...  7.03 us
    pallas_call x1, Pallas kernels, project_more(): pl.pallas_call(project_kernel, grid=(steps,), in_specs=[whole(hva.shape),...  3.63 us
  transfers between devices with their start and end apart: 28, of which 19 were waited for; matrix products, arithmetic and copies ran while one was open for 2% of the time, Pallas kernels for 15%

profile of v7, /device:TPU:0, one launch (start us, length us, event | category | flops | bytes accessed | tf_op | source)
XLA Modules:
  0.0 118.1 jit_solution(11562176266623995122)
XLA Ops:
  3.2 7.0 %attend_project.1 = (bf16[256,512]{1,0:T(8,128)(2,1)S(1)}, bf16[256,512]{1,0:T(8,128)(2,1)S(1)}, bf16[128,2048]{1,0:T(8,128)(2,1)S(1)}, bf16[128,2048]{1,0:T(8,1...) custom-call(s32[2]{0:T(128)S(1)} %pad_add_fusion.place_ref, bf16[256,2304]{1,0:T(8,128)(2,1)} %q_ref.1, ...), custom_call_target="tpu_custom_call" | custom-call | flops 2281701376 | bytes 7471104 | tf_op jit(solution)/shard_map/attend_project/pallas_call | solution.py:152
  10.2 2.9 %collective-permute-start.1 = (bf16[128,2048]{1,0:T(8,128)(2,1)S(1)}, bf16[128,2048]{1,0:T(8,128)(2,1)S(1)}, u32[]{:S(2)}, u32[]{:S(2)}) collective-permute-start(bf16[128,2048]{1,0:T(8,128)(2,1)S(1)} %get-tuple-element.37), channel_id=1, source_target_pairs={{0,1},{1,0},{2,3},{3,2},{4,5},{5,4},{6,7},{7,6},{8,9},{9,8},{10,11... | collective-permute-start | bytes 1572872 | tf_op jit(solution)/shard_map/ppermute | solution.py:439
  14.6 3.6 %project_more.1 = (bf16[128,1536]{1,0:T(8,128)(2,1)S(1)}, bf16[128,1536]{1,0:T(8,128)(2,1)S(1)}, bf16[128,1536]{1,0:T(8,128)(2,1)S(1)}, bf16[128,1536]{1,0:T(8,128)(2,1)S(1)}) custom-call(bf16[256,512]{1,0:T(8,128)(2,1)S(1)} %get-tuple-element.39.hva_ref, bf16[256,512]{1,0:T(8,128)(2,1)S(1)} %get-tuple-element.40.hvb_ref, bf16[512,7168]{1,0:T(8,128)(2,1)} %wb_ref.1, ...), custom_call_target="tpu_custom_call" | custom-call | flops 805306368 | bytes 4718592 | tf_op jit(solution)/shard_map/project_more/pallas_call | solution.py:181
  18.3 7.0 %collective-permute-done.1 = bf16[128,2048]{1,0:T(8,128)(2,1)S(1)} collective-permute-done((bf16[128,2048]{1,0:T(8,128)(2,1)S(1)}, bf16[128,2048]{1,0:T(8,128)(2,1)S(1)}, u32[]{:S(2)}, u32[]{:S(2)}) %collective-permute-start.1) | collective-permute-done | bytes 524320 | tf_op jit(solution)/shard_map/ppermute | solution.py:439
  29.8 4.9 %collective-permute-done.5 = bf16[64,2048]{1,0:T(8,128)(2,1)S(1)} collective-permute-done((bf16[64,2048]{1,0:T(8,128)(2,1)S(1)}, bf16[64,2048]{1,0:T(8,128)(2,1)S(1)}, u32[]{:S(2)}, u32[]{:S(2)}) %collective-permute-start.5) | collective-permute-done | bytes 262176 | tf_op jit(solution)/shard_map/ppermute | solution.py:439
  36.6 1.6 %collective-permute-start.7 = (bf16[32,4096]{1,0:T(8,128)(2,1)S(1)}, bf16[32,4096]{1,0:T(8,128)(2,1)S(1)}, u32[]{:S(2)}, u32[]{:S(2)}) collective-permute-start(bf16[32,4096]{1,0:T(8,128)(2,1)S(1)} %get-tuple-element.74), channel_id=1, source_target_pairs={{0,4},{1,5},{2,6},{3,7},{4,0},{5,1},{6,2},{7,3},{8,12},{9,13},{10,... | collective-permute-start | bytes 786440 | tf_op jit(solution)/shard_map/ppermute | solution.py:439
  40.4 3.0 %collective-permute-done.7 = bf16[32,4096]{1,0:T(8,128)(2,1)S(1)} collective-permute-done((bf16[32,4096]{1,0:T(8,128)(2,1)S(1)}, bf16[32,4096]{1,0:T(8,128)(2,1)S(1)}, u32[]{:S(2)}, u32[]{:S(2)}) %collective-permute-start.7) | collective-permute-done | bytes 262176 | tf_op jit(solution)/shard_map/ppermute | solution.py:439
  43.4 2.7 %collective-permute-start.8 = (bf16[16,4096]{1,0:T(8,128)(2,1)S(1)}, bf16[16,4096]{1,0:T(8,128)(2,1)S(1)}, u32[]{:S(2)}, u32[]{:S(2)}) collective-permute-start(bf16[16,4096]{1,0:T(8,128)(2,1)S(1)} %add_convert_fusion.13), channel_id=1, source_target_pairs={{0,8},{1,9},{2,10},{3,11},{4,12},{5,13},{6,14},{7,15},{8,0},{9,1},... | collective-permute-start | bytes 393224 | tf_op jit(solution)/shard_map/ppermute | solution.py:439
  46.1 1.8 %collective-permute-done.9 = bf16[128,1536]{1,0:T(8,128)(2,1)S(1)} collective-permute-done((bf16[128,1536]{1,0:T(8,128)(2,1)S(1)}, bf16[128,1536]{1,0:T(8,128)(2,1)S(1)}, u32[]{:S(2)}, u32[]{:S(2)}) %collective-permute-start.9) | collective-permute-done | bytes 393248 | tf_op jit(solution)/shard_map/ppermute | solution.py:439
  51.0 2.4 %collective-permute-start.16 = (bf16[16,4096]{1,0:T(8,128)(2,1)S(1)}, bf16[16,4096]{1,0:T(8,128)(2,1)S(1)}, u32[]{:S(2)}, u32[]{:S(2)}) collective-permute-start(bf16[16,4096]{1,0:T(8,128)(2,1)S(1)} %fusion), channel_id=1, source_target_pairs={{0,8},{1,9},{2,10},{3,11},{4,12},{5,13},{6,14},{7,15},{8,0},{9,1},... | collective-permute-start | bytes 393224 | tf_op jit(solution)/shard_map/ppermute | solution.py:439
  53.4 2.3 %collective-permute-done.11 = bf16[64,1536]{1,0:T(8,128)(2,1)S(1)} collective-permute-done((bf16[64,1536]{1,0:T(8,128)(2,1)S(1)}, bf16[64,1536]{1,0:T(8,128)(2,1)S(1)}, u32[]{:S(2)}, u32[]{:S(2)}) %collective-permute-start.11) | collective-permute-done | bytes 196640 | tf_op jit(solution)/shard_map/ppermute | solution.py:439
  56.4 2.1 %collective-permute-done.16 = bf16[16,4096]{1,0:T(8,128)(2,1)S(1)} collective-permute-done((bf16[16,4096]{1,0:T(8,128)(2,1)S(1)}, bf16[16,4096]{1,0:T(8,128)(2,1)S(1)}, u32[]{:S(2)}, u32[]{:S(2)}) %collective-permute-start.16) | collective-permute-done | bytes 131104 | tf_op jit(solution)/shard_map/ppermute | solution.py:439
  59.0 5.3 %collective-permute-done.13 = bf16[32,3072]{1,0:T(8,128)(2,1)S(1)} collective-permute-done((bf16[32,3072]{1,0:T(8,128)(2,1)S(1)}, bf16[32,3072]{1,0:T(8,128)(2,1)S(1)}, u32[]{:S(2)}, u32[]{:S(2)}) %collective-permute-start.13) | collective-permute-done | bytes 196640 | tf_op jit(solution)/shard_map/ppermute | solution.py:439
  64.4 1.9 %collective-permute-start.14 = (bf16[16,3072]{1,0:T(8,128)(2,1)S(1)}, bf16[16,3072]{1,0:T(8,128)(2,1)S(1)}, u32[]{:S(2)}, u32[]{:S(2)}) collective-permute-start(bf16[16,3072]{1,0:T(8,128)(2,1)S(1)} %get-tuple-element.88), channel_id=1, source_target_pairs={{0,8},{1,9},{2,10},{3,11},{4,12},{5,13},{6,14},{7,15},{8,0},{9,1},... | collective-permute-start | bytes 294920 | tf_op jit(solution)/shard_map/ppermute | solution.py:439
  67.2 1.8 %collective-permute-start.20 = (bf16[64,2048]{1,0:T(8,128)(2,1)S(1)}, bf16[64,2048]{1,0:T(8,128)(2,1)S(1)}, u32[]{:S(2)}, u32[]{:S(2)}) collective-permute-start(bf16[64,2048]{1,0:T(8,128)(2,1)S(1)} %get-tuple-element.86), channel_id=1, source_target_pairs={{0,1},{1,0},{2,3},{3,2},{4,5},{5,4},{6,7},{7,6},{8,9},{9,8},{10,11... | collective-permute-start | bytes 786440 | tf_op jit(solution)/shard_map/ppermute | solution.py:439
  72.7 2.7 %collective-permute-done.18 = bf16[64,2048]{1,0:T(8,128)(2,1)S(1)} collective-permute-done((bf16[64,2048]{1,0:T(8,128)(2,1)S(1)}, bf16[64,2048]{1,0:T(8,128)(2,1)S(1)}, u32[]{:S(2)}, u32[]{:S(2)}) %collective-permute-start.18) | collective-permute-done | bytes 262176 | tf_op jit(solution)/shard_map/ppermute | solution.py:439
  77.1 3.1 %collective-permute-start.23 = (bf16[32,3200]{1,0:T(8,128)(2,1)S(1)}, bf16[32,3200]{1,0:T(8,128)(2,1)S(1)}, u32[]{:S(2)}, u32[]{:S(2)}) collective-permute-start(bf16[32,3200]{1,0:T(8,128)(2,1)S(1)} %pad_maximum_fusion.10), channel_id=1, source_target_pairs={{0,4},{1,5},{2,6},{3,7},{4,0},{5,1},{6,2},{7,3},{8,12},{9,13},{10,... | collective-permute-start | bytes 614408 | tf_op jit(solution)/shard_map/ppermute | solution.py:439
  81.2 2.7 %collective-permute-done.23 = bf16[32,3200]{1,0:T(8,128)(2,1)S(1)} collective-permute-done((bf16[32,3200]{1,0:T(8,128)(2,1)S(1)}, bf16[32,3200]{1,0:T(8,128)(2,1)S(1)}, u32[]{:S(2)}, u32[]{:S(2)}) %collective-permute-start.23) | collective-permute-done | bytes 204832 | tf_op jit(solution)/shard_map/ppermute | solution.py:439
  84.0 1.7 %collective-permute-start.24 = (bf16[64,1536]{1,0:T(8,128)(2,1)S(1)}, bf16[64,1536]{1,0:T(8,128)(2,1)S(1)}, u32[]{:S(2)}, u32[]{:S(2)}) collective-permute-start(bf16[64,1536]{1,0:T(8,128)(2,1)S(1)} %pad_maximum_fusion.11), channel_id=1, source_target_pairs={{0,2},{1,3},{2,0},{3,1},{4,6},{5,7},{6,4},{7,5},{8,10},{9,11},{10,... | collective-permute-start | bytes 589832 | tf_op jit(solution)/shard_map/ppermute | solution.py:439
  85.7 2.7 %collective-permute-start.25 = (bf16[64,1664]{1,0:T(8,128)(2,1)S(1)}, bf16[64,1664]{1,0:T(8,128)(2,1)S(1)}, u32[]{:S(2)}, u32[]{:S(2)}) collective-permute-start(bf16[64,1664]{1,0:T(8,128)(2,1)S(1)} %pad_maximum_fusion.8), channel_id=1, source_target_pairs={{0,1},{1,0},{2,3},{3,2},{4,5},{5,4},{6,7},{7,6},{8,9},{9,8},{10,11... | collective-permute-start | bytes 638984 | tf_op jit(solution)/shard_map/ppermute | solution.py:439
  88.3 5.3 %collective-permute-done.24 = bf16[64,1536]{1,0:T(8,128)(2,1)S(1)} collective-permute-done((bf16[64,1536]{1,0:T(8,128)(2,1)S(1)}, bf16[64,1536]{1,0:T(8,128)(2,1)S(1)}, u32[]{:S(2)}, u32[]{:S(2)}) %collective-permute-start.24) | collective-permute-done | bytes 196640 | tf_op jit(solution)/shard_map/ppermute | solution.py:439
  96.0 2.5 %collective-permute-start.26 = (bf16[128,1536]{1,0:T(8,128)(2,1)S(1)}, bf16[128,1536]{1,0:T(8,128)(2,1)S(1)}, u32[]{:S(2)}, u32[]{:S(2)}) collective-permute-start(bf16[128,1536]{1,0:T(8,128)(2,1)S(1)} %pad_maximum_fusion.4.refs_0_), channel_id=1, source_target_pairs={{0,1},{1,0},{2,3},{3,2},{4,5},{5,4},{6,7},{7,6},{8,9},{9,8},{10,11... | collective-permute-start | bytes 1179656 | tf_op jit(solution)/shard_map/ppermute | solution.py:439
  98.5 7.4 %gate_up.1.refs_4_ = f32[2,256,1024]{2,1,0:T(8,128)S(1)} custom-call(bf16[128,2048]{1,0:T(8,128)(2,1)S(1)} %pad_maximum_fusion.1.refs_0_, bf16[128,2048]{1,0:T(8,128)(2,1)S(1)} %collective-permute-done.19.refs_1_, bf16[128,2048]{1,0:T(8,128)(2,1)S(1)} %pad_maximum_fusion.2.refs_2_, bf16[128,2048]{1,0:T(8,128)(2,1)S(1)} %collective-permute-done.21.refs_3_, ...), custom_call_target="tpu_custom_call" | custom-call | flops 4294967296 | bytes 18874368 | tf_op jit(solution)/shard_map/gate_up/pallas_call | solution.py:375
  105.9 12.1 %finish.1 = bf16[192,7168]{1,0:T(8,128)(2,1)} custom-call(s32[2]{0:T(128)S(1)} %pad_add_fusion.place_ref, bf16[128,1536]{1,0:T(8,128)(2,1)S(1)} %pad_maximum_fusion.4.refs_0_, bf16[128,1536]{1,0:T(8,128)(2,1)S(1)} %collective-permute-done.26.refs_1_, bf16[128,1664]{1,0:T(8,128)(2,1)S(1)} %pad_maximum_fusion.3.refs_2_, ...), custom_call_target="tpu_custom_call" | custom-call | flops 6039797760 | bytes 30015488 | tf_op jit(solution)/shard_map/finish/pallas_call | solution.py:404
  (84 shorter events, 26.5 us)
Async XLA Ops:
  2.6 24.2 %collective-permute-start.3 = (bf16[1,7168,512]{2,1,0:T(8,128)(2,1)}, bf16[1,7168,512]{2,1,0:T(8,128)(2,1)}, u32[]{:S(2)}, u32[]{:S(2)}) collective-permute-start(bf16[1,7168,512]{2,1,0:T(8,128)(2,1)} %refs_5_.3), channel_id=1, source_target_pairs={{0,16},{16,0},{1,17},{17,1},{2,18},{18,2},{3,19},{19,3},{4,20},{20... | collective-permute-start | bytes 22020104 | tf_op jit(solution)/shard_map/ppermute | solution.py:444
  2.9 23.9 %collective-permute-start.4 = (bf16[1,7168,512]{2,1,0:T(8,128)(2,1)}, bf16[1,7168,512]{2,1,0:T(8,128)(2,1)}, u32[]{:S(2)}, u32[]{:S(2)}) collective-permute-start(bf16[1,7168,512]{2,1,0:T(8,128)(2,1)} %refs_6_.1), channel_id=1, source_target_pairs={{0,16},{16,0},{1,17},{17,1},{2,18},{18,2},{3,19},{19,3},{4,20},{20... | collective-permute-start | bytes 22020104 | tf_op jit(solution)/shard_map/ppermute | solution.py:444
  10.2 15.1 %collective-permute-start.1 = (bf16[128,2048]{1,0:T(8,128)(2,1)S(1)}, bf16[128,2048]{1,0:T(8,128)(2,1)S(1)}, u32[]{:S(2)}, u32[]{:S(2)}) collective-permute-start(bf16[128,2048]{1,0:T(8,128)(2,1)S(1)} %get-tuple-element.37), channel_id=1, source_target_pairs={{0,1},{1,0},{2,3},{3,2},{4,5},{5,4},{6,7},{7,6},{8,9},{9,8},{10,11... | collective-permute-start | bytes 1572872 | tf_op jit(solution)/shard_map/ppermute | solution.py:439
  13.1 13.7 %collective-permute-start.2 = (bf16[128,2048]{1,0:T(8,128)(2,1)S(1)}, bf16[128,2048]{1,0:T(8,128)(2,1)S(1)}, u32[]{:S(2)}, u32[]{:S(2)}) collective-permute-start(bf16[128,2048]{1,0:T(8,128)(2,1)S(1)} %get-tuple-element.38), channel_id=1, source_target_pairs={{0,2},{1,3},{2,0},{3,1},{4,6},{5,7},{6,4},{7,5},{8,10},{9,11},{10,... | collective-permute-start | bytes 1572872 | tf_op jit(solution)/shard_map/ppermute | solution.py:439
  26.9 7.8 %collective-permute-start.5 = (bf16[64,2048]{1,0:T(8,128)(2,1)S(1)}, bf16[64,2048]{1,0:T(8,128)(2,1)S(1)}, u32[]{:S(2)}, u32[]{:S(2)}) collective-permute-start(bf16[64,2048]{1,0:T(8,128)(2,1)S(1)} %get-tuple-element.78), channel_id=1, source_target_pairs={{0,2},{1,3},{2,0},{3,1},{4,6},{5,7},{6,4},{7,5},{8,10},{9,11},{10,... | collective-permute-start | bytes 786440 | tf_op jit(solution)/shard_map/ppermute | solution.py:439
  28.7 7.8 %collective-permute-start.6 = (bf16[64,2048]{1,0:T(8,128)(2,1)S(1)}, bf16[64,2048]{1,0:T(8,128)(2,1)S(1)}, u32[]{:S(2)}, u32[]{:S(2)}) collective-permute-start(bf16[64,2048]{1,0:T(8,128)(2,1)S(1)} %get-tuple-element.76), channel_id=1, source_target_pairs={{0,1},{1,0},{2,3},{3,2},{4,5},{5,4},{6,7},{7,6},{8,9},{9,8},{10,11... | collective-permute-start | bytes 786440 | tf_op jit(solution)/shard_map/ppermute | solution.py:439
  29.8 41.1 %collective-permute-start.15 = (bf16[1,512,7168]{2,1,0:T(8,128)(2,1)}, bf16[1,512,7168]{2,1,0:T(8,128)(2,1)}, u32[]{:S(2)}, u32[]{:S(2)}) collective-permute-start(bf16[1,512,7168]{2,1,0:T(8,128)(2,1)} %refs_9_.1), channel_id=1, source_target_pairs={{0,16},{16,0},{1,17},{17,1},{2,18},{18,2},{3,19},{19,3},{4,20},{20... | collective-permute-start | bytes 22020104 | tf_op jit(solution)/shard_map/ppermute | solution.py:444
  36.6 6.8 %collective-permute-start.7 = (bf16[32,4096]{1,0:T(8,128)(2,1)S(1)}, bf16[32,4096]{1,0:T(8,128)(2,1)S(1)}, u32[]{:S(2)}, u32[]{:S(2)}) collective-permute-start(bf16[32,4096]{1,0:T(8,128)(2,1)S(1)} %get-tuple-element.74), channel_id=1, source_target_pairs={{0,4},{1,5},{2,6},{3,7},{4,0},{5,1},{6,2},{7,3},{8,12},{9,13},{10,... | collective-permute-start | bytes 786440 | tf_op jit(solution)/shard_map/ppermute | solution.py:439
  38.4 9.5 %collective-permute-start.9 = (bf16[128,1536]{1,0:T(8,128)(2,1)S(1)}, bf16[128,1536]{1,0:T(8,128)(2,1)S(1)}, u32[]{:S(2)}, u32[]{:S(2)}) collective-permute-start(bf16[128,1536]{1,0:T(8,128)(2,1)S(1)} %get-tuple-element.51), channel_id=1, source_target_pairs={{0,1},{1,0},{2,3},{3,2},{4,5},{5,4},{6,7},{7,6},{8,9},{9,8},{10,11... | collective-permute-start | bytes 1179656 | tf_op jit(solution)/shard_map/ppermute | solution.py:439
  39.9 9.5 %collective-permute-start.10 = (bf16[128,1536]{1,0:T(8,128)(2,1)S(1)}, bf16[128,1536]{1,0:T(8,128)(2,1)S(1)}, u32[]{:S(2)}, u32[]{:S(2)}) collective-permute-start(bf16[128,1536]{1,0:T(8,128)(2,1)S(1)} %get-tuple-element.52), channel_id=1, source_target_pairs={{0,2},{1,3},{2,0},{3,1},{4,6},{5,7},{6,4},{7,5},{8,10},{9,11},{10,... | collective-permute-start | bytes 1179656 | tf_op jit(solution)/shard_map/ppermute | solution.py:439
  43.4 7.3 %collective-permute-start.8 = (bf16[16,4096]{1,0:T(8,128)(2,1)S(1)}, bf16[16,4096]{1,0:T(8,128)(2,1)S(1)}, u32[]{:S(2)}, u32[]{:S(2)}) collective-permute-start(bf16[16,4096]{1,0:T(8,128)(2,1)S(1)} %add_convert_fusion.13), channel_id=1, source_target_pairs={{0,8},{1,9},{2,10},{3,11},{4,12},{5,13},{6,14},{7,15},{8,0},{9,1},... | collective-permute-start | bytes 393224 | tf_op jit(solution)/shard_map/ppermute | solution.py:439
  51.0 7.4 %collective-permute-start.16 = (bf16[16,4096]{1,0:T(8,128)(2,1)S(1)}, bf16[16,4096]{1,0:T(8,128)(2,1)S(1)}, u32[]{:S(2)}, u32[]{:S(2)}) collective-permute-start(bf16[16,4096]{1,0:T(8,128)(2,1)S(1)} %fusion), channel_id=1, source_target_pairs={{0,8},{1,9},{2,10},{3,11},{4,12},{5,13},{6,14},{7,15},{8,0},{9,1},... | collective-permute-start | bytes 393224 | tf_op jit(solution)/shard_map/ppermute | solution.py:439
  55.9 8.4 %collective-permute-start.13 = (bf16[32,3072]{1,0:T(8,128)(2,1)S(1)}, bf16[32,3072]{1,0:T(8,128)(2,1)S(1)}, u32[]{:S(2)}, u32[]{:S(2)}) collective-permute-start(bf16[32,3072]{1,0:T(8,128)(2,1)S(1)} %get-tuple-element.81), channel_id=1, source_target_pairs={{0,4},{1,5},{2,6},{3,7},{4,0},{5,1},{6,2},{7,3},{8,12},{9,13},{10,... | collective-permute-start | bytes 589832 | tf_op jit(solution)/shard_map/ppermute | solution.py:439
  58.5 8.6 %collective-permute-start.17 = (bf16[32,4096]{1,0:T(8,128)(2,1)S(1)}, bf16[32,4096]{1,0:T(8,128)(2,1)S(1)}, u32[]{:S(2)}, u32[]{:S(2)}) collective-permute-start(bf16[32,4096]{1,0:T(8,128)(2,1)S(1)} %pad_maximum_fusion.6), channel_id=1, source_target_pairs={{0,4},{1,5},{2,6},{3,7},{4,0},{5,1},{6,2},{7,3},{8,12},{9,13},{10,... | collective-permute-start | bytes 786440 | tf_op jit(solution)/shard_map/ppermute | solution.py:439
  64.4 6.5 %collective-permute-start.14 = (bf16[16,3072]{1,0:T(8,128)(2,1)S(1)}, bf16[16,3072]{1,0:T(8,128)(2,1)S(1)}, u32[]{:S(2)}, u32[]{:S(2)}) collective-permute-start(bf16[16,3072]{1,0:T(8,128)(2,1)S(1)} %get-tuple-element.88), channel_id=1, source_target_pairs={{0,8},{1,9},{2,10},{3,11},{4,12},{5,13},{6,14},{7,15},{8,0},{9,1},... | collective-permute-start | bytes 294920 | tf_op jit(solution)/shard_map/ppermute | solution.py:439
  67.2 13.0 %collective-permute-start.20 = (bf16[64,2048]{1,0:T(8,128)(2,1)S(1)}, bf16[64,2048]{1,0:T(8,128)(2,1)S(1)}, u32[]{:S(2)}, u32[]{:S(2)}) collective-permute-start(bf16[64,2048]{1,0:T(8,128)(2,1)S(1)} %get-tuple-element.86), channel_id=1, source_target_pairs={{0,1},{1,0},{2,3},{3,2},{4,5},{5,4},{6,7},{7,6},{8,9},{9,8},{10,11... | collective-permute-start | bytes 786440 | tf_op jit(solution)/shard_map/ppermute | solution.py:439
  69.0 6.4 %collective-permute-start.18 = (bf16[64,2048]{1,0:T(8,128)(2,1)S(1)}, bf16[64,2048]{1,0:T(8,128)(2,1)S(1)}, u32[]{:S(2)}, u32[]{:S(2)}) collective-permute-start(bf16[64,2048]{1,0:T(8,128)(2,1)S(1)} %get-tuple-element.87), channel_id=1, source_target_pairs={{0,2},{1,3},{2,0},{3,1},{4,6},{5,7},{6,4},{7,5},{8,10},{9,11},{10,... | collective-permute-start | bytes 786440 | tf_op jit(solution)/shard_map/ppermute | solution.py:439
  75.4 18.3 %collective-permute-start.19 = (bf16[128,2048]{1,0:T(8,128)(2,1)S(1)}, bf16[128,2048]{1,0:T(8,128)(2,1)S(1)}, u32[]{:S(2)}, u32[]{:S(2)}) collective-permute-start(bf16[128,2048]{1,0:T(8,128)(2,1)S(1)} %pad_maximum_fusion.1.refs_0_), channel_id=1, source_target_pairs={{0,1},{1,0},{2,3},{3,2},{4,5},{5,4},{6,7},{7,6},{8,9},{9,8},{10,11... | collective-permute-start | bytes 1572872 | tf_op jit(solution)/shard_map/ppermute | solution.py:439
  77.1 6.9 %collective-permute-start.23 = (bf16[32,3200]{1,0:T(8,128)(2,1)S(1)}, bf16[32,3200]{1,0:T(8,128)(2,1)S(1)}, u32[]{:S(2)}, u32[]{:S(2)}) collective-permute-start(bf16[32,3200]{1,0:T(8,128)(2,1)S(1)} %pad_maximum_fusion.10), channel_id=1, source_target_pairs={{0,4},{1,5},{2,6},{3,7},{4,0},{5,1},{6,2},{7,3},{8,12},{9,13},{10,... | collective-permute-start | bytes 614408 | tf_op jit(solution)/shard_map/ppermute | solution.py:439
  80.3 13.5 %collective-permute-start.21 = (bf16[128,2048]{1,0:T(8,128)(2,1)S(1)}, bf16[128,2048]{1,0:T(8,128)(2,1)S(1)}, u32[]{:S(2)}, u32[]{:S(2)}) collective-permute-start(bf16[128,2048]{1,0:T(8,128)(2,1)S(1)} %pad_maximum_fusion.2.refs_2_), channel_id=1, source_target_pairs={{0,2},{1,3},{2,0},{3,1},{4,6},{5,7},{6,4},{7,5},{8,10},{9,11},{10,... | collective-permute-start | bytes 1572872 | tf_op jit(solution)/shard_map/ppermute | solution.py:439
  84.0 9.7 %collective-permute-start.24 = (bf16[64,1536]{1,0:T(8,128)(2,1)S(1)}, bf16[64,1536]{1,0:T(8,128)(2,1)S(1)}, u32[]{:S(2)}, u32[]{:S(2)}) collective-permute-start(bf16[64,1536]{1,0:T(8,128)(2,1)S(1)} %pad_maximum_fusion.11), channel_id=1, source_target_pairs={{0,2},{1,3},{2,0},{3,1},{4,6},{5,7},{6,4},{7,5},{8,10},{9,11},{10,... | collective-permute-start | bytes 589832 | tf_op jit(solution)/shard_map/ppermute | solution.py:439
  85.7 8.1 %collective-permute-start.25 = (bf16[64,1664]{1,0:T(8,128)(2,1)S(1)}, bf16[64,1664]{1,0:T(8,128)(2,1)S(1)}, u32[]{:S(2)}, u32[]{:S(2)}) collective-permute-start(bf16[64,1664]{1,0:T(8,128)(2,1)S(1)} %pad_maximum_fusion.8), channel_id=1, source_target_pairs={{0,1},{1,0},{2,3},{3,2},{4,5},{5,4},{6,7},{7,6},{8,9},{9,8},{10,11... | collective-permute-start | bytes 638984 | tf_op jit(solution)/shard_map/ppermute | solution.py:439
  93.8 12.1 %collective-permute-start.27 = (bf16[128,1664]{1,0:T(8,128)(2,1)S(1)}, bf16[128,1664]{1,0:T(8,128)(2,1)S(1)}, u32[]{:S(2)}, u32[]{:S(2)}) collective-permute-start(bf16[128,1664]{1,0:T(8,128)(2,1)S(1)} %pad_maximum_fusion.3.refs_2_), channel_id=1, source_target_pairs={{0,2},{1,3},{2,0},{3,1},{4,6},{5,7},{6,4},{7,5},{8,10},{9,11},{10,... | collective-permute-start | bytes 1277960 | tf_op jit(solution)/shard_map/ppermute | solution.py:439
  96.0 9.9 %collective-permute-start.26 = (bf16[128,1536]{1,0:T(8,128)(2,1)S(1)}, bf16[128,1536]{1,0:T(8,128)(2,1)S(1)}, u32[]{:S(2)}, u32[]{:S(2)}) collective-permute-start(bf16[128,1536]{1,0:T(8,128)(2,1)S(1)} %pad_maximum_fusion.4.refs_0_), channel_id=1, source_target_pairs={{0,1},{1,0},{2,3},{3,2},{4,5},{5,4},{6,7},{7,6},{8,9},{9,8},{10,11... | collective-permute-start | bytes 1179656 | tf_op jit(solution)/shard_map/ppermute | solution.py:439
  (8 other events, 123.0 us)
